TPU v7x, 512 devices: a whole 4x8x8 slice. The times are simulated.
512 devices in a mesh: sub: 8 (over y_lo, core), blk: 64 (over y_hi, x, z).
Axes of the slice: x: 4, y: 8 (y_hi: 2, y_lo: 4; y = y_hi * 4 + y_lo), z: 8, core: 2. Of those that a mesh axis runs over, the one named last changes fastest.
Arguments:
- feats: bfloat16 [8, 2, 4096, 512], P('sub', None, 'blk'), may hold values from -8 to 8
- pos: int32 [8, 4096], P('sub'), may hold values from 0 to 4095, as said below
- w_one: bfloat16 [512, 512], replicated, may hold values from -0.25 to 0.25
- b_one: float32 [512], replicated, may hold values from -3 to 3
- w_two: bfloat16 [512, 512], replicated, may hold values from -0.25 to 0.25
Outputs:
- grad_feats: bfloat16 [8, 2, 4096, 512], P('sub', None, 'blk')
- grad_w_one: float32 [512, 512], P('blk')
- grad_b_one: float32 [512], P('blk')
- grad_w_two: float32 [512, 512], P('blk')
Inputs may be any that keep to these rules, and one draw needn't show every extreme that they name: Each row pos[g] names every row of 0 to 4095 exactly once.
All inputs are finite; a program needn't handle non-finite values.
Results may differ from a plain program's by a relative error of at most 0.0059.
Values may be sent and summed in bfloat16 or wider, within the bound.
No kernel may reach another device: no remote copies, remote signals or barrier semaphores. Data moves between devices by JAX's collectives and lax.ppermute only.
A program may use at most 64 MiB of HBM per device.

v0:
```python
import math

import jax
import jax.numpy as jnp
from jax import lax
from jax.sharding import Mesh
from jax.sharding import PartitionSpec as P

BLK = ("blk_0", "blk_1", "blk_2")


temper = 0.2
epsilon = 1e-06


def passed_along(shard, axis, by):
    count = lax.axis_size(axis)
    return lax.ppermute(shard, axis, [(i, (i + by) % count) for i in range(count)])


def split_up(shard, dim, count):
    before, after = (shard.shape[:dim], shard.shape[dim + 1 :])
    return jnp.moveaxis(shard.reshape(*before, count, -1, *after), dim, 0)


def sent_and_summed(shard, axis, dim):
    count = lax.axis_size(axis)
    pieces = lax.all_to_all(split_up(shard, dim, count), axis, 0, 0, tiled=True)
    return jnp.sum(pieces, axis=0)


def sum_by_axis(shard, axes, dim):
    far, near = axes
    own = sent_and_summed(split_up(shard, dim, lax.axis_size(far)), near, dim + 1)
    return jnp.sum(lax.all_to_all(own, far, 0, 0, tiled=True), axis=0)


def sent_to_all(shard, axis):
    count = lax.axis_size(axis)
    return lax.all_to_all(
        jnp.broadcast_to(shard[None], (count, *shard.shape)), axis, 0, 0, tiled=True
    )


def of_everyone(shard, axis):
    return sent_to_all(shard, axis).sum(axis=0)


def packed_total(arrays, axis):
    ends = [0]
    for a in arrays:
        ends.append(ends[-1] + a.size)
    total = of_everyone(jnp.concatenate([a.ravel() for a in arrays]), axis)
    return tuple((total[b:e].reshape(a.shape) for a, b, e in zip(arrays, ends, ends[1:])))


def grid_cover(extent):
    side_len = math.isqrt(extent)
    if side_len * side_len < extent:
        side_len = side_len + 1
    pair_list = []
    for differ in range(1, extent // 2 + 1):
        step_count = (differ + side_len - 1) // side_len
        upper_off = side_len * step_count % extent
        lower_off = side_len * step_count - differ
        pair_list.append((upper_off, lower_off))
    return pair_list


def sigmoid_weights(scores, positive, negatives):
    return 2.0 * jnp.where(positive, -jax.nn.sigmoid(-scores), jax.nn.sigmoid(scores) / negatives)


def positive_mask(pos_rows, pos_cols, row_block, col_block, half_rows):
    local_ids = jnp.arange(half_rows, dtype=jnp.int32)
    upper_right = (
        pos_rows[:, :, None] == col_block[:, None, None] * half_rows + local_ids[None, None, :]
    )
    lower_left = (
        pos_cols[:, None, :] == row_block[:, None, None] * half_rows + local_ids[None, :, None]
    )
    blank = jnp.zeros_like(upper_right)
    top_half = jnp.concatenate([blank, upper_right], axis=2)
    bottom_half = jnp.concatenate([lower_left, blank], axis=2)
    return jnp.concatenate([top_half, bottom_half], axis=1)


def local(feats, pos, w_one, b_one, w_two):
    half_rows = feats.shape[2]
    feat_width = feats.shape[3]
    blocks_count = lax.axis_size(BLK)
    graph_count = lax.axis_size("sub")
    my_block = lax.axis_index(BLK)
    rows_in = feats[0].reshape(2 * half_rows, feat_width)
    pre_act = jnp.dot(rows_in, w_one, preferred_element_type=jnp.float32) + b_one
    hidden = jax.nn.elu(pre_act).astype(jnp.bfloat16)
    projected = jnp.dot(hidden, w_two, preferred_element_type=jnp.float32)
    radius = jnp.sqrt(jnp.sum(projected * projected, axis=1, keepdims=True) + epsilon)
    unit_rows = projected / radius
    sent_rows = unit_rows.astype(jnp.bfloat16)
    negatives = 2.0 * half_rows * blocks_count - 2.0
    pair_list = grid_cover(blocks_count)
    used_offsets = sorted(
        set((offset_val for pair_item in pair_list for offset_val in pair_item if offset_val != 0))
    )
    offsets = [0] + used_offsets
    slot_of = {}
    sent_list = []
    pos_list = []
    block_ids = []
    for offset_val in offsets:
        if offset_val == 0:
            fetched = sent_rows
        else:
            fetched = passed_along(sent_rows, BLK, -offset_val)
        block_id = (my_block + offset_val) % blocks_count
        slot_of[offset_val] = len(sent_list)
        sent_list.append(fetched)
        block_ids.append(block_id)
        pos_list.append(lax.dynamic_slice_in_dim(pos[0], block_id * half_rows, half_rows))
    self_scores = (
        lax.dot_general(
            sent_rows, sent_rows, (((1,), (1,)), ((), ())), preferred_element_type=jnp.float32
        )
        / temper
    )
    self_positive = positive_mask(
        pos_list[0][None], pos_list[0][None], my_block[None], my_block[None], half_rows
    )[0]
    self_coef = sigmoid_weights(self_scores, self_positive, negatives)
    self_coef = jnp.where(jnp.eye(2 * half_rows, dtype=bool), 0.0, self_coef).astype(jnp.bfloat16)
    accumulated = [jnp.zeros((2 * half_rows, feat_width), jnp.float32) for offset_val in offsets]
    accumulated[0] = jnp.dot(self_coef, sent_rows, preferred_element_type=jnp.float32)
    group_size = 8
    for start_at in range(0, len(pair_list), group_size):
        batch_pairs = pair_list[start_at : start_at + group_size]
        row_slots = [slot_of[pair_item[1]] for pair_item in batch_pairs]
        col_slots = [slot_of[pair_item[0]] for pair_item in batch_pairs]
        row_sent = jnp.stack([sent_list[slot_number] for slot_number in row_slots])
        col_sent = jnp.stack([sent_list[slot_number] for slot_number in col_slots])
        row_pos = jnp.stack([pos_list[slot_number] for slot_number in row_slots])
        col_pos = jnp.stack([pos_list[slot_number] for slot_number in col_slots])
        row_ids = jnp.stack([block_ids[slot_number] for slot_number in row_slots])
        col_ids = jnp.stack([block_ids[slot_number] for slot_number in col_slots])
        scores = (
            jnp.einsum("nad,nbd->nab", row_sent, col_sent, preferred_element_type=jnp.float32)
            / temper
        )
        positive = positive_mask(row_pos, col_pos, row_ids, col_ids, half_rows)
        tile_coef = sigmoid_weights(scores, positive, negatives).astype(jnp.bfloat16)
        row_grad = jnp.einsum(
            "nab,nbd->nad", tile_coef, col_sent, preferred_element_type=jnp.float32
        )
        col_grad = jnp.einsum(
            "nab,nad->nbd", tile_coef, row_sent, preferred_element_type=jnp.float32
        )
        for position in range(len(batch_pairs)):
            upper_off, lower_off = batch_pairs[position]
            accumulated[slot_of[lower_off]] = accumulated[slot_of[lower_off]] + row_grad[position]
            if (upper_off - lower_off) % blocks_count != blocks_count // 2:
                accumulated[slot_of[upper_off]] = (
                    accumulated[slot_of[upper_off]] + col_grad[position]
                )
    grad_unit = accumulated[0]
    for offset_val in used_offsets:
        grad_unit = grad_unit + passed_along(accumulated[slot_of[offset_val]], BLK, offset_val)
    grad_unit = grad_unit / temper
    inner_prod = jnp.sum(unit_rows * grad_unit, axis=1, keepdims=True)
    grad_proj = ((grad_unit - unit_rows * inner_prod) / radius).astype(jnp.bfloat16)
    grad_hidden = lax.dot_general(
        grad_proj, w_two, (((1,), (1,)), ((), ())), preferred_element_type=jnp.float32
    )
    elu_slope = jnp.where(pre_act > 0, 1.0, jnp.exp(jnp.minimum(pre_act, 0.0)))
    grad_pre = (grad_hidden * elu_slope).astype(jnp.bfloat16)
    grad_rows = lax.dot_general(
        grad_pre, w_one, (((1,), (1,)), ((), ())), preferred_element_type=jnp.float32
    )
    grad_feats = grad_rows.astype(jnp.bfloat16).reshape(1, 2, half_rows, feat_width)
    part_two = lax.dot_general(
        hidden, grad_proj, (((0,), (0,)), ((), ())), preferred_element_type=jnp.float32
    )
    part_one = lax.dot_general(
        rows_in, grad_pre, (((0,), (0,)), ((), ())), preferred_element_type=jnp.float32
    )
    part_bias = jnp.sum(grad_pre.astype(jnp.float32), axis=0)
    local_one, local_bias, local_two = (
        sum_by_axis(part_one, ("blk_0", ("blk_1", "blk_2")), 0),
        sum_by_axis(part_bias, ("blk_0", ("blk_1", "blk_2")), 0),
        sum_by_axis(part_two, ("blk_0", ("blk_1", "blk_2")), 0),
    )
    share_one, share_bias, share_two = packed_total((local_one, local_bias, local_two), "sub")
    mean_scale = 1.0 / (2.0 * half_rows * blocks_count * graph_count)
    return (grad_feats, share_one * mean_scale, share_bias * mean_scale, share_two * mean_scale)


def solution(mesh):
    torus = Mesh(
        mesh.devices.reshape(mesh.shape["sub"], 2, 4, 8), ("sub", "blk_0", "blk_1", "blk_2")
    )
    in_specs = (P("sub", None, BLK, None), P("sub", None), P(), P(), P())
    out_specs = (P("sub", None, BLK, None), P(BLK, None), P(BLK), P(BLK, None))
    return jax.shard_map(local, mesh=torus, in_specs=in_specs, out_specs=out_specs, check_vma=False)
```

profile of v0, /device:TPU:1, one launch (start us, length us, event | category | flops | bytes accessed | tf_op | source)
XLA Modules:
  0.0 363.6 jit_solution(4374392433490473943)
XLA Ops:
  2.5 12.3 %collective-permute-start = (bf16[128,512]{1,0:T(8,128)(2,1)S(1)}, bf16[128,512]{1,0:T(8,128)(2,1)S(1)}, u32[]{:S(2)}, u32[]{:S(2)}) collective-permute-start(bf16[128,512]{1,0:T(8,128)(2,1)S(1)} %fusion.65), channel_id=1, source_target_pairs={{0,57},{1,58},{2,59},{3,60},{4,61},{5,62},{6,63},{7,0},{8,1},{9,2}... | collective-permute-start | bytes 393224 | tf_op jit(solution)/shard_map/ppermute | solution.py:18
  14.8 6.1 %collective-permute-start.1 = (bf16[128,512]{1,0:T(8,128)(2,1)S(1)}, bf16[128,512]{1,0:T(8,128)(2,1)S(1)}, u32[]{:S(2)}, u32[]{:S(2)}) collective-permute-start(bf16[128,512]{1,0:T(8,128)(2,1)S(1)} %fusion.65), channel_id=1, source_target_pairs={{0,58},{1,59},{2,60},{3,61},{4,62},{5,63},{6,0},{7,1},{8,2},{9,3},... | collective-permute-start | bytes 393224 | tf_op jit(solution)/shard_map/ppermute | solution.py:18
  20.8 7.0 %collective-permute-start.2 = (bf16[128,512]{1,0:T(8,128)(2,1)S(1)}, bf16[128,512]{1,0:T(8,128)(2,1)S(1)}, u32[]{:S(2)}, u32[]{:S(2)}) collective-permute-start(bf16[128,512]{1,0:T(8,128)(2,1)S(1)} %fusion.65), channel_id=1, source_target_pairs={{0,59},{1,60},{2,61},{3,62},{4,63},{5,0},{6,1},{7,2},{8,3},{9,4},{... | collective-permute-start | bytes 393224 | tf_op jit(solution)/shard_map/ppermute | solution.py:18
  30.7 6.3 %collective-permute-start.4 = (bf16[128,512]{1,0:T(8,128)(2,1)S(1)}, bf16[128,512]{1,0:T(8,128)(2,1)S(1)}, u32[]{:S(2)}, u32[]{:S(2)}) collective-permute-start(bf16[128,512]{1,0:T(8,128)(2,1)S(1)} %fusion.65), channel_id=1, source_target_pairs={{0,61},{1,62},{2,63},{3,0},{4,1},{5,2},{6,3},{7,4},{8,5},{9,6},{10... | collective-permute-start | bytes 393224 | tf_op jit(solution)/shard_map/ppermute | solution.py:18
  38.8 3.4 collective-permute-start.5
  48.8 5.8 %collective-permute-start.9 = (bf16[128,512]{1,0:T(8,128)(2,1)S(1)}, bf16[128,512]{1,0:T(8,128)(2,1)S(1)}, u32[]{:S(2)}, u32[]{:S(2)}) collective-permute-start(bf16[128,512]{1,0:T(8,128)(2,1)S(1)} %fusion.65), channel_id=1, source_target_pairs={{0,40},{1,41},{2,42},{3,43},{4,44},{5,45},{6,46},{7,47},{8,48},{9,... | collective-permute-start | bytes 393224 | tf_op jit(solution)/shard_map/ppermute | solution.py:18
  55.8 2.9 collective-permute-start.8
  64.8 4.3 %collective-permute-done.10 = bf16[128,512]{1,0:T(8,128)(2,1)S(1)} collective-permute-done((bf16[128,512]{1,0:T(8,128)(2,1)S(1)}, bf16[128,512]{1,0:T(8,128)(2,1)S(1)}, u32[]{:S(2)}, u32[]{:S(2)}) %collective-permute-start.10) | collective-permute-done | bytes 131104 | tf_op jit(solution)/shard_map/ppermute | solution.py:18
  70.3 8.0 %collective-permute-start.21 = (f32[128,512]{1,0:T(8,128)S(1)}, f32[128,512]{1,0:T(8,128)S(1)}, u32[]{:S(2)}, u32[]{:S(2)}) collective-permute-start(f32[128,512]{1,0:T(8,128)S(1)} %fusion.15), channel_id=1, source_target_pairs={{0,32},{1,33},{2,34},{3,35},{4,36},{5,37},{6,38},{7,39},{8,40},{9,... | collective-permute-start | bytes 786440 | tf_op jit(solution)/shard_map/ppermute | solution.py:18
  82.7 4.5 %collective-permute-start.19 = (f32[128,512]{1,0:T(8,128)S(1)}, f32[128,512]{1,0:T(8,128)}, u32[]{:S(2)}, u32[]{:S(2)}) collective-permute-start(f32[128,512]{1,0:T(8,128)S(1)} %fusion.17), channel_id=1, source_target_pairs={{0,16},{1,17},{2,18},{3,19},{4,20},{5,21},{6,22},{7,23},{8,24},{9,... | collective-permute-start | bytes 786440 | tf_op jit(solution)/shard_map/ppermute | solution.py:18
  87.3 7.4 %collective-permute-done.7 = bf16[128,512]{1,0:T(8,128)(2,1)S(1)} collective-permute-done((bf16[128,512]{1,0:T(8,128)(2,1)S(1)}, bf16[128,512]{1,0:T(8,128)(2,1)S(1)}, u32[]{:S(2)}, u32[]{:S(2)}) %collective-permute-start.7) | collective-permute-done | bytes 131104 | tf_op jit(solution)/shard_map/ppermute | solution.py:18
  101.4 8.0 %collective-permute-start.17 = (f32[128,512]{1,0:T(8,128)S(1)}, f32[128,512]{1,0:T(8,128)}, u32[]{:S(2)}, u32[]{:S(2)}) collective-permute-start(f32[128,512]{1,0:T(8,128)S(1)} %get-tuple-element.7), channel_id=1, source_target_pairs={{0,7},{1,8},{2,9},{3,10},{4,11},{5,12},{6,13},{7,14},{8,15},{9,16}... | collective-permute-start | bytes 786440 | tf_op jit(solution)/shard_map/ppermute | solution.py:18
  115.2 11.1 %collective-permute-start.14 = (f32[128,512]{1,0:T(8,128)}, f32[128,512]{1,0:T(8,128)}, u32[]{:S(2)}, u32[]{:S(2)}) collective-permute-start(f32[128,512]{1,0:T(8,128)} %get-tuple-element.11), channel_id=1, source_target_pairs={{0,4},{1,5},{2,6},{3,7},{4,8},{5,9},{6,10},{7,11},{8,12},{9,13},{1... | collective-permute-start | bytes 786440 | tf_op jit(solution)/shard_map/ppermute | solution.py:18
  128.3 3.8 %collective-permute-done.17 = f32[128,512]{1,0:T(8,128)} collective-permute-done((f32[128,512]{1,0:T(8,128)S(1)}, f32[128,512]{1,0:T(8,128)}, u32[]{:S(2)}, u32[]{:S(2)}) %collective-permute-start.17) | collective-permute-done | bytes 262176 | tf_op jit(solution)/shard_map/ppermute | solution.py:18
  134.0 4.1 %collective-permute-done.16 = f32[128,512]{1,0:T(8,128)} collective-permute-done((f32[128,512]{1,0:T(8,128)S(1)}, f32[128,512]{1,0:T(8,128)}, u32[]{:S(2)}, u32[]{:S(2)}) %collective-permute-start.16) | collective-permute-done | bytes 262176 | tf_op jit(solution)/shard_map/ppermute | solution.py:18
  138.1 8.8 %collective-permute-start.11 = (f32[128,512]{1,0:T(8,128)}, f32[128,512]{1,0:T(8,128)}, u32[]{:S(2)}, u32[]{:S(2)}) collective-permute-start(f32[128,512]{1,0:T(8,128)} %get-tuple-element.6), channel_id=1, source_target_pairs={{0,1},{1,2},{2,3},{3,4},{4,5},{5,6},{6,7},{7,8},{8,9},{9,10},{10,1... | collective-permute-start | bytes 786440 | tf_op jit(solution)/shard_map/ppermute | solution.py:18
  154.6 26.3 %collective-permute-done.13 = f32[128,512]{1,0:T(8,128)} collective-permute-done((f32[128,512]{1,0:T(8,128)}, f32[128,512]{1,0:T(8,128)}, u32[]{:S(2)}, u32[]{:S(2)}) %collective-permute-start.13) | collective-permute-done | bytes 262176 | tf_op jit(solution)/shard_map/ppermute | solution.py:18
  180.8 29.1 %collective-permute-done.12 = f32[128,512]{1,0:T(8,128)} collective-permute-done((f32[128,512]{1,0:T(8,128)}, f32[128,512]{1,0:T(8,128)}, u32[]{:S(2)}, u32[]{:S(2)}) %collective-permute-start.12) | collective-permute-done | bytes 262176 | tf_op jit(solution)/shard_map/ppermute | solution.py:18
  216.7 21.4 %all-to-all-start.2 = ((f32[32,2,8]{2,1,0:T(2,128)}), f32[32,2,8]{2,1,0:T(2,128)S(1)}, u32[]{:S(2)}, u32[]{:S(2)}) async-start(f32[32,2,8]{2,1,0:T(2,128)} %copy.38), calls=%async_computation.2 | async-start | bytes 65536 | tf_op jit(solution)/shard_map/all_to_all | solution.py:28
  238.4 8.4 %all-to-all-done.2 = f32[32,2,8]{2,1,0:T(2,128)S(1)} async-done(((f32[32,2,8]{2,1,0:T(2,128)}), f32[32,2,8]{2,1,0:T(2,128)S(1)}, u32[]{:S(2)}, u32[]{:S(2)}) %all-to-all-start.2) | async-done | bytes 2080 | tf_op jit(solution)/shard_map/all_to_all | solution.py:28
  247.4 9.2 %all-to-all-start.3 = ((f32[2,1,8]{2,1,0:T(1,128)}), f32[2,1,8]{2,1,0:T(1,128)S(1)}, u32[]{:S(2)}, u32[]{:S(2)}) async-start(f32[2,1,8]{2,1,0:T(1,128)} %bitcast.44), calls=%async_computation.3 | async-start | bytes 2048 | tf_op jit(solution)/shard_map/all_to_all | solution.py:35
  257.7 5.3 %all-to-all-done.3 = f32[2,1,8]{2,1,0:T(1,128)S(1)} async-done(((f32[2,1,8]{2,1,0:T(1,128)}), f32[2,1,8]{2,1,0:T(1,128)S(1)}, u32[]{:S(2)}, u32[]{:S(2)}) %all-to-all-start.3) | async-done | bytes 96 | tf_op jit(solution)/shard_map/all_to_all | solution.py:35
  263.1 3.9 %all-to-all-start = ((f32[32,2,8,512]{3,2,1,0:T(8,128)}), f32[32,2,8,512]{3,2,1,0:T(8,128)S(1)}, u32[]{:S(2)}, u32[]{:S(2)}) async-start(f32[32,2,8,512]{3,2,1,0:T(8,128)} %bitcast.156), calls=%async_computation | async-start | bytes 2097152 | tf_op jit(solution)/shard_map/all_to_all | solution.py:28
  268.5 18.9 %all-to-all-done = f32[32,2,8,512]{3,2,1,0:T(8,128)S(1)} async-done(((f32[32,2,8,512]{3,2,1,0:T(8,128)}), f32[32,2,8,512]{3,2,1,0:T(8,128)S(1)}, u32[]{:S(2)}, u32[]{:S(2)}) %all-to-all-start) | async-done | bytes 1048608 | tf_op jit(solution)/shard_map/all_to_all | solution.py:28
  287.4 9.3 %all-to-all-start.4 = ((f32[32,2,8,512]{3,2,1,0:T(8,128)}), f32[32,2,8,512]{3,2,1,0:T(8,128)S(1)}, u32[]{:S(2)}, u32[]{:S(2)}) async-start(f32[32,2,8,512]{3,2,1,0:T(8,128)} %bitcast.158), calls=%async_computation.4 | async-start | bytes 2097152 | tf_op jit(solution)/shard_map/all_to_all | solution.py:28
  297.5 18.7 %all-to-all-done.4 = f32[32,2,8,512]{3,2,1,0:T(8,128)S(1)} async-done(((f32[32,2,8,512]{3,2,1,0:T(8,128)}), f32[32,2,8,512]{3,2,1,0:T(8,128)S(1)}, u32[]{:S(2)}, u32[]{:S(2)}) %all-to-all-start.4) | async-done | bytes 1048608 | tf_op jit(solution)/shard_map/all_to_all | solution.py:28
  316.1 3.3 all-to-all-start.1
  320.1 6.0 %all-to-all-done.1 = f32[2,8,512]{2,1,0:T(8,128)S(1)} async-done(((f32[2,8,512]{2,1,0:T(8,128)}), f32[2,8,512]{2,1,0:T(8,128)S(1)}, u32[]{:S(2)}, u32[]{:S(2)}) %all-to-all-start.1) | async-done | bytes 32800 | tf_op jit(solution)/shard_map/all_to_all | solution.py:35
  326.1 3.3 all-to-all-start.5
  329.4 6.8 %all-to-all-done.5 = f32[2,8,512]{2,1,0:T(8,128)S(1)} async-done(((f32[2,8,512]{2,1,0:T(8,128)}), f32[2,8,512]{2,1,0:T(8,128)S(1)}, u32[]{:S(2)}, u32[]{:S(2)}) %all-to-all-start.5) | async-done | bytes 32800 | tf_op jit(solution)/shard_map/all_to_all | solution.py:35
  337.1 15.7 %all-to-all-start.6 = ((f32[8,1,8200]{2,1,0:T(1,128)}), f32[8,1,8200]{2,1,0:T(1,128)S(1)}, u32[]{:S(2)}, u32[]{:S(2)}) async-start(f32[8,1,8200]{2,1,0:T(1,128)} %broadcast_in_dim.14), calls=%async_computation.6 | async-start | bytes 532480 | tf_op jit(solution)/shard_map/all_to_all | solution.py:40
  353.8 7.8 %all-to-all-done.6 = f32[8,1,8200]{2,1,0:T(1,128)S(1)} async-done(((f32[8,1,8200]{2,1,0:T(1,128)}), f32[8,1,8200]{2,1,0:T(1,128)S(1)}, u32[]{:S(2)}, u32[]{:S(2)}) %all-to-all-start.6) | async-done | bytes 262432 | tf_op jit(solution)/shard_map/all_to_all | solution.py:40
  (108 shorter events, 64.9 us)
Async XLA Ops:
  2.5 36.3 %collective-permute-start = (bf16[128,512]{1,0:T(8,128)(2,1)S(1)}, bf16[128,512]{1,0:T(8,128)(2,1)S(1)}, u32[]{:S(2)}, u32[]{:S(2)}) collective-permute-start(bf16[128,512]{1,0:T(8,128)(2,1)S(1)} %fusion.65), channel_id=1, source_target_pairs={{0,57},{1,58},{2,59},{3,60},{4,61},{5,62},{6,63},{7,0},{8,1},{9,2}... | collective-permute-start | bytes 393224 | tf_op jit(solution)/shard_map/ppermute | solution.py:18
  14.8 27.5 %collective-permute-start.1 = (bf16[128,512]{1,0:T(8,128)(2,1)S(1)}, bf16[128,512]{1,0:T(8,128)(2,1)S(1)}, u32[]{:S(2)}, u32[]{:S(2)}) collective-permute-start(bf16[128,512]{1,0:T(8,128)(2,1)S(1)} %fusion.65), channel_id=1, source_target_pairs={{0,58},{1,59},{2,60},{3,61},{4,62},{5,63},{6,0},{7,1},{8,2},{9,3},... | collective-permute-start | bytes 393224 | tf_op jit(solution)/shard_map/ppermute | solution.py:18
  20.8 23.6 %collective-permute-start.2 = (bf16[128,512]{1,0:T(8,128)(2,1)S(1)}, bf16[128,512]{1,0:T(8,128)(2,1)S(1)}, u32[]{:S(2)}, u32[]{:S(2)}) collective-permute-start(bf16[128,512]{1,0:T(8,128)(2,1)S(1)} %fusion.65), channel_id=1, source_target_pairs={{0,59},{1,60},{2,61},{3,62},{4,63},{5,0},{6,1},{7,2},{8,3},{9,4},{... | collective-permute-start | bytes 393224 | tf_op jit(solution)/shard_map/ppermute | solution.py:18
  27.9 21.0 %collective-permute-start.3 = (bf16[128,512]{1,0:T(8,128)(2,1)S(1)}, bf16[128,512]{1,0:T(8,128)(2,1)S(1)}, u32[]{:S(2)}, u32[]{:S(2)}) collective-permute-start(bf16[128,512]{1,0:T(8,128)(2,1)S(1)} %fusion.65), channel_id=1, source_target_pairs={{0,60},{1,61},{2,62},{3,63},{4,0},{5,1},{6,2},{7,3},{8,4},{9,5},{1... | collective-permute-start | bytes 393224 | tf_op jit(solution)/shard_map/ppermute | solution.py:18
  30.7 25.1 %collective-permute-start.4 = (bf16[128,512]{1,0:T(8,128)(2,1)S(1)}, bf16[128,512]{1,0:T(8,128)(2,1)S(1)}, u32[]{:S(2)}, u32[]{:S(2)}) collective-permute-start(bf16[128,512]{1,0:T(8,128)(2,1)S(1)} %fusion.65), channel_id=1, source_target_pairs={{0,61},{1,62},{2,63},{3,0},{4,1},{5,2},{6,3},{7,4},{8,5},{9,6},{10... | collective-permute-start | bytes 393224 | tf_op jit(solution)/shard_map/ppermute | solution.py:18
  38.8 21.2 %collective-permute-start.5 = (bf16[128,512]{1,0:T(8,128)(2,1)S(1)}, bf16[128,512]{1,0:T(8,128)(2,1)S(1)}, u32[]{:S(2)}, u32[]{:S(2)}) collective-permute-start(bf16[128,512]{1,0:T(8,128)(2,1)S(1)} %fusion.65), channel_id=1, source_target_pairs={{0,62},{1,63},{2,0},{3,1},{4,2},{5,3},{6,4},{7,5},{8,6},{9,7},{10,... | collective-permute-start | bytes 393224 | tf_op jit(solution)/shard_map/ppermute | solution.py:18
  42.3 22.4 %collective-permute-start.6 = (bf16[128,512]{1,0:T(8,128)(2,1)S(1)}, bf16[128,512]{1,0:T(8,128)(2,1)S(1)}, u32[]{:S(2)}, u32[]{:S(2)}) collective-permute-start(bf16[128,512]{1,0:T(8,128)(2,1)S(1)} %fusion.65), channel_id=1, source_target_pairs={{0,63},{1,0},{2,1},{3,2},{4,3},{5,4},{6,5},{7,6},{8,7},{9,8},{10,9... | collective-permute-start | bytes 393224 | tf_op jit(solution)/shard_map/ppermute | solution.py:18
  44.5 24.6 %collective-permute-start.10 = (bf16[128,512]{1,0:T(8,128)(2,1)S(1)}, bf16[128,512]{1,0:T(8,128)(2,1)S(1)}, u32[]{:S(2)}, u32[]{:S(2)}) collective-permute-start(bf16[128,512]{1,0:T(8,128)(2,1)S(1)} %fusion.65), channel_id=1, source_target_pairs={{0,32},{1,33},{2,34},{3,35},{4,36},{5,37},{6,38},{7,39},{8,40},{9,... | collective-permute-start | bytes 393224 | tf_op jit(solution)/shard_map/ppermute | solution.py:18
  48.8 29.5 %collective-permute-start.9 = (bf16[128,512]{1,0:T(8,128)(2,1)S(1)}, bf16[128,512]{1,0:T(8,128)(2,1)S(1)}, u32[]{:S(2)}, u32[]{:S(2)}) collective-permute-start(bf16[128,512]{1,0:T(8,128)(2,1)S(1)} %fusion.65), channel_id=1, source_target_pairs={{0,40},{1,41},{2,42},{3,43},{4,44},{5,45},{6,46},{7,47},{8,48},{9,... | collective-permute-start | bytes 393224 | tf_op jit(solution)/shard_map/ppermute | solution.py:18
  55.8 25.7 %collective-permute-start.8 = (bf16[128,512]{1,0:T(8,128)(2,1)S(1)}, bf16[128,512]{1,0:T(8,128)(2,1)S(1)}, u32[]{:S(2)}, u32[]{:S(2)}) collective-permute-start(bf16[128,512]{1,0:T(8,128)(2,1)S(1)} %fusion.65), channel_id=1, source_target_pairs={{0,48},{1,49},{2,50},{3,51},{4,52},{5,53},{6,54},{7,55},{8,56},{9,... | collective-permute-start | bytes 393224 | tf_op jit(solution)/shard_map/ppermute | solution.py:18
  60.0 34.6 %collective-permute-start.7 = (bf16[128,512]{1,0:T(8,128)(2,1)S(1)}, bf16[128,512]{1,0:T(8,128)(2,1)S(1)}, u32[]{:S(2)}, u32[]{:S(2)}) collective-permute-start(bf16[128,512]{1,0:T(8,128)(2,1)S(1)} %fusion.65), channel_id=1, source_target_pairs={{0,56},{1,57},{2,58},{3,59},{4,60},{5,61},{6,62},{7,63},{8,0},{9,1... | collective-permute-start | bytes 393224 | tf_op jit(solution)/shard_map/ppermute | solution.py:18
  70.3 39.1 %collective-permute-start.21 = (f32[128,512]{1,0:T(8,128)S(1)}, f32[128,512]{1,0:T(8,128)S(1)}, u32[]{:S(2)}, u32[]{:S(2)}) collective-permute-start(f32[128,512]{1,0:T(8,128)S(1)} %fusion.15), channel_id=1, source_target_pairs={{0,32},{1,33},{2,34},{3,35},{4,36},{5,37},{6,38},{7,39},{8,40},{9,... | collective-permute-start | bytes 786440 | tf_op jit(solution)/shard_map/ppermute | solution.py:18
  79.6 33.4 %collective-permute-start.20 = (f32[128,512]{1,0:T(8,128)S(1)}, f32[128,512]{1,0:T(8,128)}, u32[]{:S(2)}, u32[]{:S(2)}) collective-permute-start(f32[128,512]{1,0:T(8,128)S(1)} %fusion.16), channel_id=1, source_target_pairs={{0,24},{1,25},{2,26},{3,27},{4,28},{5,29},{6,30},{7,31},{8,32},{9,... | collective-permute-start | bytes 786440 | tf_op jit(solution)/shard_map/ppermute | solution.py:18
  82.7 32.5 %collective-permute-start.19 = (f32[128,512]{1,0:T(8,128)S(1)}, f32[128,512]{1,0:T(8,128)}, u32[]{:S(2)}, u32[]{:S(2)}) collective-permute-start(f32[128,512]{1,0:T(8,128)S(1)} %fusion.17), channel_id=1, source_target_pairs={{0,16},{1,17},{2,18},{3,19},{4,20},{5,21},{6,22},{7,23},{8,24},{9,... | collective-permute-start | bytes 786440 | tf_op jit(solution)/shard_map/ppermute | solution.py:18
  95.9 30.5 %collective-permute-start.18 = (f32[128,512]{1,0:T(8,128)S(1)}, f32[128,512]{1,0:T(8,128)}, u32[]{:S(2)}, u32[]{:S(2)}) collective-permute-start(f32[128,512]{1,0:T(8,128)S(1)} %fusion.18), channel_id=1, source_target_pairs={{0,8},{1,9},{2,10},{3,11},{4,12},{5,13},{6,14},{7,15},{8,16},{9,17... | collective-permute-start | bytes 786440 | tf_op jit(solution)/shard_map/ppermute | solution.py:18
  98.7 13.2 %copy-start.1 = (f32[8,128,512]{2,1,0:T(8,128)}, f32[8,128,512]{2,1,0:T(8,128)S(1)}, u32[]{:S(2)}) copy-start(f32[8,128,512]{2,1,0:T(8,128)S(1)} %fusion.4) | copy-start | bytes 6291460
  101.4 30.7 %collective-permute-start.17 = (f32[128,512]{1,0:T(8,128)S(1)}, f32[128,512]{1,0:T(8,128)}, u32[]{:S(2)}, u32[]{:S(2)}) collective-permute-start(f32[128,512]{1,0:T(8,128)S(1)} %get-tuple-element.7), channel_id=1, source_target_pairs={{0,7},{1,8},{2,9},{3,10},{4,11},{5,12},{6,13},{7,14},{8,15},{9,16}... | collective-permute-start | bytes 786440 | tf_op jit(solution)/shard_map/ppermute | solution.py:18
  109.4 28.7 %collective-permute-start.16 = (f32[128,512]{1,0:T(8,128)S(1)}, f32[128,512]{1,0:T(8,128)}, u32[]{:S(2)}, u32[]{:S(2)}) collective-permute-start(f32[128,512]{1,0:T(8,128)S(1)} %get-tuple-element.8), channel_id=1, source_target_pairs={{0,6},{1,7},{2,8},{3,9},{4,10},{5,11},{6,12},{7,13},{8,14},{9,15},... | collective-permute-start | bytes 786440 | tf_op jit(solution)/shard_map/ppermute | solution.py:18
  113.0 39.2 %collective-permute-start.15 = (f32[128,512]{1,0:T(8,128)}, f32[128,512]{1,0:T(8,128)}, u32[]{:S(2)}, u32[]{:S(2)}) collective-permute-start(f32[128,512]{1,0:T(8,128)} %get-tuple-element.9), channel_id=1, source_target_pairs={{0,5},{1,6},{2,7},{3,8},{4,9},{5,10},{6,11},{7,12},{8,13},{9,14},{... | collective-permute-start | bytes 786440 | tf_op jit(solution)/shard_map/ppermute | solution.py:18
  115.2 39.3 %collective-permute-start.14 = (f32[128,512]{1,0:T(8,128)}, f32[128,512]{1,0:T(8,128)}, u32[]{:S(2)}, u32[]{:S(2)}) collective-permute-start(f32[128,512]{1,0:T(8,128)} %get-tuple-element.11), channel_id=1, source_target_pairs={{0,4},{1,5},{2,6},{3,7},{4,8},{5,9},{6,10},{7,11},{8,12},{9,13},{1... | collective-permute-start | bytes 786440 | tf_op jit(solution)/shard_map/ppermute | solution.py:18
  126.4 54.4 %collective-permute-start.13 = (f32[128,512]{1,0:T(8,128)}, f32[128,512]{1,0:T(8,128)}, u32[]{:S(2)}, u32[]{:S(2)}) collective-permute-start(f32[128,512]{1,0:T(8,128)} %get-tuple-element.12), channel_id=1, source_target_pairs={{0,3},{1,4},{2,5},{3,6},{4,7},{5,8},{6,9},{7,10},{8,11},{9,12},{10... | collective-permute-start | bytes 786440 | tf_op jit(solution)/shard_map/ppermute | solution.py:18
  132.1 77.8 %collective-permute-start.12 = (f32[128,512]{1,0:T(8,128)}, f32[128,512]{1,0:T(8,128)}, u32[]{:S(2)}, u32[]{:S(2)}) collective-permute-start(f32[128,512]{1,0:T(8,128)} %get-tuple-element.10), channel_id=1, source_target_pairs={{0,2},{1,3},{2,4},{3,5},{4,6},{5,7},{6,8},{7,9},{8,10},{9,11},{10,... | collective-permute-start | bytes 786440 | tf_op jit(solution)/shard_map/ppermute | solution.py:18
  138.1 74.5 %collective-permute-start.11 = (f32[128,512]{1,0:T(8,128)}, f32[128,512]{1,0:T(8,128)}, u32[]{:S(2)}, u32[]{:S(2)}) collective-permute-start(f32[128,512]{1,0:T(8,128)} %get-tuple-element.6), channel_id=1, source_target_pairs={{0,1},{1,2},{2,3},{3,4},{4,5},{5,6},{6,7},{7,8},{8,9},{9,10},{10,1... | collective-permute-start | bytes 786440 | tf_op jit(solution)/shard_map/ppermute | solution.py:18
  214.9 23.2 %copy-start.5 = (bf16[1,2,64,512]{3,2,1,0:T(8,128)(2,1)S(1)}, bf16[1,2,64,512]{3,2,1,0:T(8,128)(2,1)}, u32[]{:S(2)}) copy-start(bf16[1,2,64,512]{3,2,1,0:T(8,128)(2,1)} %param.5) | copy-start | bytes 393220
  216.7 30.1 %all-to-all-start.2 = ((f32[32,2,8]{2,1,0:T(2,128)}), f32[32,2,8]{2,1,0:T(2,128)S(1)}, u32[]{:S(2)}, u32[]{:S(2)}) async-start(f32[32,2,8]{2,1,0:T(2,128)} %copy.38), calls=%async_computation.2 | async-start | bytes 65536 | tf_op jit(solution)/shard_map/all_to_all | solution.py:28
  247.4 15.7 %all-to-all-start.3 = ((f32[2,1,8]{2,1,0:T(1,128)}), f32[2,1,8]{2,1,0:T(1,128)S(1)}, u32[]{:S(2)}, u32[]{:S(2)}) async-start(f32[2,1,8]{2,1,0:T(1,128)} %bitcast.44), calls=%async_computation.3 | async-start | bytes 2048 | tf_op jit(solution)/shard_map/all_to_all | solution.py:35
  263.1 24.3 %all-to-all-start = ((f32[32,2,8,512]{3,2,1,0:T(8,128)}), f32[32,2,8,512]{3,2,1,0:T(8,128)S(1)}, u32[]{:S(2)}, u32[]{:S(2)}) async-start(f32[32,2,8,512]{3,2,1,0:T(8,128)} %bitcast.156), calls=%async_computation | async-start | bytes 2097152 | tf_op jit(solution)/shard_map/all_to_all | solution.py:28
  287.4 28.7 %all-to-all-start.4 = ((f32[32,2,8,512]{3,2,1,0:T(8,128)}), f32[32,2,8,512]{3,2,1,0:T(8,128)S(1)}, u32[]{:S(2)}, u32[]{:S(2)}) async-start(f32[32,2,8,512]{3,2,1,0:T(8,128)} %bitcast.158), calls=%async_computation.4 | async-start | bytes 2097152 | tf_op jit(solution)/shard_map/all_to_all | solution.py:28
  296.8 56.1 %copy-start.4 = (bf16[512,512]{1,0:T(8,128)(2,1)S(1)}, bf16[512,512]{1,0:T(8,128)(2,1)}, u32[]{:S(2)}) copy-start(bf16[512,512]{1,0:T(8,128)(2,1)} %param.7) | copy-start | bytes 1572868
  316.1 10.0 %all-to-all-start.1 = ((f32[2,8,512]{2,1,0:T(8,128)}), f32[2,8,512]{2,1,0:T(8,128)S(1)}, u32[]{:S(2)}, u32[]{:S(2)}) async-start(f32[2,8,512]{2,1,0:T(8,128)} %reduce_sum.92), calls=%async_computation.1 | async-start | bytes 65536 | tf_op jit(solution)/shard_map/all_to_all | solution.py:35
  326.1 10.1 %all-to-all-start.5 = ((f32[2,8,512]{2,1,0:T(8,128)}), f32[2,8,512]{2,1,0:T(8,128)S(1)}, u32[]{:S(2)}, u32[]{:S(2)}) async-start(f32[2,8,512]{2,1,0:T(8,128)} %reduce_sum.97), calls=%async_computation.5 | async-start | bytes 65536 | tf_op jit(solution)/shard_map/all_to_all | solution.py:35
  337.1 24.5 %all-to-all-start.6 = ((f32[8,1,8200]{2,1,0:T(1,128)}), f32[8,1,8200]{2,1,0:T(1,128)S(1)}, u32[]{:S(2)}, u32[]{:S(2)}) async-start(f32[8,1,8200]{2,1,0:T(1,128)} %broadcast_in_dim.14), calls=%async_computation.6 | async-start | bytes 532480 | tf_op jit(solution)/shard_map/all_to_all | solution.py:40
  (5 other events, 37.7 us)
where the time goes:
time: 365 us; the launch traced here: 364 us
  starting transfers between devices  172 us (47%)
  waiting for transfers between devices  162 us (44%)
  matrix products  11.2 us (3%)
  other arithmetic  10.2 us (3%)
  local copies, waits for them, and re-layouts  6.88 us (2%)
    ppermute x22, starting transfers between devices, passed_along(): lax.ppermute(shard, axis, [(i, (i + by) % count) for i in range(count)])  105 us
    ppermute x22, waiting for transfers between devices, passed_along(): lax.ppermute(shard, axis, [(i, (i + by) % count) for i in range(count)])  90.3 us
    all_to_all x3, waiting for transfers between devices, sent_and_summed(): pieces = lax.all_to_all(split_up(shard, dim, count), axis, 0, 0, tiled=True)  46 us
    all_to_all x3, starting transfers between devices, sent_and_summed(): pieces = lax.all_to_all(split_up(shard, dim, count), axis, 0, 0, tiled=True)  34.6 us
    all_to_all x3, waiting for transfers between devices, sum_by_axis(): return jnp.sum(lax.all_to_all(own, far, 0, 0, tiled=True), axis=0)  18.2 us
    all_to_all x3, starting transfers between devices, sum_by_axis(): return jnp.sum(lax.all_to_all(own, far, 0, 0, tiled=True), axis=0)  15.7 us
    all_to_all x1, starting transfers between devices, sent_to_all(): lax.all_to_all(jnp.broadcast_to(shard[None], (count, *shard.shape)), axis...  15.7 us
    all_to_all x1, waiting for transfers between devices, sent_to_all(): lax.all_to_all(jnp.broadcast_to(shard[None], (count, *shard.shape)), axis...  7.81 us
  transfers between devices with their start and end apart: 29, of which 20 were waited for; matrix products, arithmetic and copies ran while one was open for 5% of the time, Pallas kernels for 0%

commit v1 on v0

v1 whole, which is shorter than its diff:
```python
import jax
import jax.numpy as jnp
from jax import lax
from jax.experimental import pallas as pl
from jax.experimental.pallas import tpu as pltpu
from jax.sharding import Mesh
from jax.sharding import PartitionSpec as P

BLK = ("yh", "x", "z")
SUB = ("yl", "co")
temper = 0.2
epsilon = 1e-06
LANES = 128


def shifted(value, axis, by):
    count = lax.axis_size(axis)
    return lax.ppermute(value, axis, [((i + by) % count, i) for i in range(count)])


def dot_nn(a, b):
    return lax.dot_general(a, b, (((1,), (0,)), ((), ())), preferred_element_type=jnp.float32)


def dot_nt(a, b):
    return lax.dot_general(a, b, (((1,), (1,)), ((), ())), preferred_element_type=jnp.float32)


def dot_tn(a, b):
    return lax.dot_general(a, b, (((0,), (0,)), ((), ())), preferred_element_type=jnp.float32)


def tile_kernel(*refs, nz, nx, ny, half, width, negatives):
    cols_count = nx * ny
    rows_ref = refs[0]
    col_refs = refs[1 : 1 + cols_count]
    w_one_ref, w_two_ref, b_one_ref, rid_ref, rpos_ref, cid_ref, cpos_ref, z_ref = refs[
        1 + cols_count : 9 + cols_count
    ]
    feats_out, weights_out, cols_s, hid_s, gp_s, pre_s = refs[9 + cols_count :]
    my_z = z_ref[0]
    for i in range(cols_count):
        for v in range(2):
            cols_s[v, i * half : (i + 1) * half, :] = col_refs[i][v * half : (v + 1) * half, :]
    w_one = w_one_ref[...]
    w_two = w_two_ref[...]
    per = 256 // half
    chunk = per * half
    for v in range(2):
        for k in range(nz // per):
            x = rows_ref[k * per : (k + 1) * per, v].reshape(chunk, width)
            row_at = slice(k * chunk, (k + 1) * chunk)
            stack_at = slice((v * nz * half) + k * chunk, (v * nz * half) + (k + 1) * chunk)
            pre = dot_nn(x, w_one) + b_one_ref[...]
            grow = jnp.exp(jnp.minimum(pre, 0.0))
            above = pre > 0
            hidden = jnp.where(above, pre, grow - 1.0).astype(jnp.bfloat16)
            slope = jnp.where(above, 1.0, grow)
            projected = dot_nn(hidden, w_two)
            radius = jnp.sqrt(jnp.sum(projected * projected, axis=1, keepdims=True) + epsilon)
            unit = projected / radius
            sent = unit.astype(jnp.bfloat16)
            rid = rid_ref[row_at, :]
            rpos = rpos_ref[row_at, :]
            total = None
            for cv in range(2):
                col = cols_s[cv]
                scores = dot_nt(sent, col) / temper
                g = jax.nn.sigmoid(scores)
                base = g * (2.0 / negatives)
                if v == cv:
                    coef = jnp.where(rid == cid_ref[...], 0.0, base)
                elif v == 0:
                    coef = jnp.where(rpos == cid_ref[...], 2.0 * g - 2.0, base)
                else:
                    coef = jnp.where(rid == cpos_ref[...], 2.0 * g - 2.0, base)
                part = dot_nn(coef.astype(jnp.bfloat16), col)
                total = part if total is None else total + part
            grad_unit = total / temper
            inner = jnp.sum(unit * grad_unit, axis=1, keepdims=True)
            grad_proj = ((grad_unit - unit * inner) / radius).astype(jnp.bfloat16)
            grad_pre = (dot_nt(grad_proj, w_two) * slope).astype(jnp.bfloat16)
            grad_rows = dot_nt(grad_pre, w_one).astype(jnp.bfloat16)
            hid_s[stack_at, :] = hidden
            gp_s[stack_at, :] = grad_proj
            pre_s[stack_at, :] = grad_pre
            for j in range(per):
                block = k * per + j
                feats_out[lax.rem(block + nz - my_z, nz), v] = grad_rows[j * half : (j + 1) * half]
    rows_all = jnp.concatenate(
        [rows_ref[:, v].reshape(nz * half, width) for v in range(2)], axis=0
    )
    part_one = dot_tn(rows_all, pre_s[...]).astype(jnp.bfloat16)
    part_two = dot_tn(hid_s[...], gp_s[...]).astype(jnp.bfloat16)
    ones = jnp.ones((2 * nz * half, LANES), jnp.bfloat16)
    part_bias = dot_tn(pre_s[...], ones).astype(jnp.bfloat16)
    per_x = width // (ny * nx)
    for yh in range(ny):
        for x in range(nx):
            source = slice((yh * nx + x) * per_x, (yh * nx + x + 1) * per_x)
            target = slice((x * ny + yh) * per_x, (x * ny + yh + 1) * per_x)
            weights_out[0, target, :width] = part_one[source]
            weights_out[0, target, width:] = part_bias[source]
            weights_out[1, target, :width] = part_two[source]
            weights_out[1, target, width:] = jnp.zeros((per_x, LANES), jnp.bfloat16)


def local(feats, pos, w_one, b_one, w_two):
    half = feats.shape[2]
    width = feats.shape[3]
    nz, nx, ny = lax.axis_size("z"), lax.axis_size("x"), lax.axis_size("yh")
    blocks = nz * nx * ny
    my_z, my_x, my_y = lax.axis_index("z"), lax.axis_index("x"), lax.axis_index("yh")
    negatives = 2.0 * half * blocks - 2.0
    own = feats[0]
    rows = lax.all_to_all(jnp.broadcast_to(own[None], (nz, *own.shape)), "z", 0, 0, tiled=True)

    flat = own.reshape(2 * half, width)
    pre_act = dot_nn(flat, w_one) + b_one
    hidden = jax.nn.elu(pre_act).astype(jnp.bfloat16)
    projected = dot_nn(hidden, w_two)
    radius = jnp.sqrt(jnp.sum(projected * projected, axis=1, keepdims=True) + epsilon)
    sent = (projected / radius).astype(jnp.bfloat16)

    cols = [sent]
    for d in range(1, ny):
        cols.append(shifted(sent, "yh", d))
    cols = [c for got in cols for c in [got] + [shifted(got, "x", d) for d in range(1, nx)]]
    col_blocks = jnp.stack(
        [((my_y + dy) % ny) * nx + (my_x + dx) % nx for dy in range(ny) for dx in range(nx)]
    )
    nodes = jnp.arange(half, dtype=jnp.int32)
    cid = ((col_blocks[:, None] * nz + my_z) * half + nodes[None, :]).reshape(1, -1)
    pos_blocks = pos[0].reshape(ny * nx, nz, half)
    cpos = lax.dynamic_index_in_dim(pos_blocks, my_z, 1, keepdims=False)[col_blocks].reshape(1, -1)
    my_yx = my_y * nx + my_x
    rid = (my_yx * (nz * half) + jnp.arange(nz * half, dtype=jnp.int32))[:, None]
    rpos = lax.dynamic_slice_in_dim(pos[0], my_yx * (nz * half), nz * half)[:, None]

    vmem = pl.BlockSpec(memory_space=pltpu.VMEM)
    count = len(cols)
    shares, weights = pl.pallas_call(
        lambda *refs: tile_kernel(
            *refs, nz=nz, nx=nx, ny=ny, half=half, width=width, negatives=negatives
        ),
        in_specs=[vmem] * (count + 8) + [pl.BlockSpec(memory_space=pltpu.SMEM)],
        out_specs=[vmem, vmem],
        out_shape=[
            jax.ShapeDtypeStruct((nz, 2, half, width), jnp.bfloat16),
            jax.ShapeDtypeStruct((2, width, width + LANES), jnp.bfloat16),
        ],
        scratch_shapes=[
            pltpu.VMEM((2, count * half, width), jnp.bfloat16),
            pltpu.VMEM((2 * nz * half, width), jnp.bfloat16),
            pltpu.VMEM((2 * nz * half, width), jnp.bfloat16),
            pltpu.VMEM((2 * nz * half, width), jnp.bfloat16),
        ],
        name="tile",
    )(rows, *cols, w_one, w_two, b_one[None], rid, rpos, cid, cpos, my_z[None])

    pieces = [shares[0]]
    for d in range(1, nz):
        pieces.append(shifted(shares[d], "z", -d))
    grad = pieces[0].astype(jnp.float32)
    for piece in pieces[1:]:
        grad = grad + piece.astype(jnp.float32)
    grad_feats = grad.astype(jnp.bfloat16)[None]

    got = lax.all_to_all(weights, "co", 0, 0, tiled=True)
    got = jnp.sum(got.astype(jnp.float32), axis=0).astype(jnp.bfloat16)
    got = lax.all_to_all(got.reshape(nx, -1, width + LANES), "x", 0, 0, tiled=True)
    got = jnp.sum(got.astype(jnp.float32), axis=0)
    got = lax.all_to_all(got.reshape(ny * nz, -1, width + LANES), ("yh", "z"), 0, 0, tiled=True)
    got = jnp.sum(got, axis=0)
    got = lax.all_to_all(
        jnp.broadcast_to(got[None], (lax.axis_size(SUB), *got.shape)), SUB, 0, 0, tiled=True
    )
    got = jnp.sum(got.reshape(lax.axis_size("yl"), 2, *got.shape[1:]), axis=0)
    got = got * (1.0 / (2.0 * half * blocks * lax.axis_size(SUB)))
    return (grad_feats, got[0, :, :width], got[0, :, width], got[1, :, :width])


def solution(mesh):
    torus = Mesh(mesh.devices.reshape(4, 2, 2, 4, 8), ("yl", "co", "yh", "x", "z"))
    in_specs = (P(SUB, None, BLK, None), P(SUB, None), P(), P(), P())
    out_specs = (P(SUB, None, BLK, None), P(BLK, None), P(BLK), P(BLK, None))
    return jax.shard_map(local, mesh=torus, in_specs=in_specs, out_specs=out_specs, check_vma=False)
```

time: 365 us -> 136 us (0.37)
  waiting for transfers between devices: 162 us -> 5.45 us
  starting transfers between devices: 172 us -> 81.3 us
  blocking collectives: 0 us -> 21.9 us
  Pallas kernels: 0 us -> 11.7 us
  matrix products: 11.2 us -> 0.57 us
  other arithmetic: 10.2 us -> 3.86 us
    ppermute x22 -> x14, waiting for transfers between devices: 90.3 us -> 2.35 us  [shifted(): lax.ppermute(value, axis, [((i + by) % count, i) for i in range(count)])]
    all_to_all x7 -> x3, waiting for transfers between devices: 72 us -> 3.1 us  [the longest x1 3.09 us: local(): lax.all_to_all(jnp.broadcast_to(got[None], (lax.axis_size(SUB), *got.shap...]
    ppermute x22 -> x14, starting transfers between devices: 105 us -> 54.6 us  [shifted(): lax.ppermute(value, axis, [((i + by) % count, i) for i in range(count)])]
    all_to_all x7 -> x3, starting transfers between devices: 66.1 us -> 26.7 us  [the longest x1 11 us: local(): lax.all_to_all(jnp.broadcast_to(own[None], (nz, *own.shape)), 'z', 0, 0,...]
    all_to_all x0 -> x2, blocking collectives: none -> 21.9 us  [the longest x1 13.7 us: local(): lax.all_to_all(got.reshape(nx, -1, width + LANES), 'x', 0, 0, tiled=True)]
    pallas_call x0 -> x1, Pallas kernels: none -> 11.7 us  [local(): pl.pallas_call(lambda *refs: tile_kernel(*refs, nz=nz, nx=nx, ny=ny, half...]
    dot_general x19 -> x1, matrix products: 11.2 us -> 0.57 us  [dot_nn(): lax.dot_general(a, b, (((1,), (0,)), ((), ())), preferred_element_type=jn...]
  transfers between devices with their start and end apart: 29 -> 17, of which waited for: 20 -> 4; matrix products, arithmetic and copies ran while one was open for 5% -> 5% of each run, Pallas kernels for 0% -> 0%
where the time goes in v1:
time: 136 us; the launch traced here: 135 us
  starting transfers between devices  81.3 us (60%)
  blocking collectives  21.9 us (16%)
  Pallas kernels  11.7 us (9%)
  local copies, waits for them, and re-layouts  8.55 us (6%)
  waiting for transfers between devices  5.45 us (4%)
  other arithmetic  3.86 us (3%)
    ppermute x14, starting transfers between devices, shifted(): lax.ppermute(value, axis, [((i + by) % count, i) for i in range(count)])  54.6 us
    all_to_all x1, blocking collectives, local(): lax.all_to_all(got.reshape(nx, -1, width + LANES), 'x', 0, 0, tiled=True)  13.7 us
    pallas_call x1, Pallas kernels, local(): pl.pallas_call(lambda *refs: tile_kernel(*refs, nz=nz, nx=nx, ny=ny, half...  11.7 us
    all_to_all x1, starting transfers between devices, local(): lax.all_to_all(jnp.broadcast_to(own[None], (nz, *own.shape)), 'z', 0, 0,...  11 us
    all_to_all x1, starting transfers between devices, local(): lax.all_to_all(jnp.broadcast_to(got[None], (lax.axis_size(SUB), *got.shap...  8.73 us
    all_to_all x1, blocking collectives, local(): got = lax.all_to_all(weights, 'co', 0, 0, tiled=True)  8.21 us
    all_to_all x1, starting transfers between devices, local(): lax.all_to_all(got.reshape(ny * nz, -1, width + LANES), ('yh', 'z'), 0, 0...  7.02 us
    all_to_all x1, waiting for transfers between devices, local(): lax.all_to_all(jnp.broadcast_to(got[None], (lax.axis_size(SUB), *got.shap...  3.09 us
  transfers between devices with their start and end apart: 17, of which 4 were waited for; matrix products, arithmetic and copies ran while one was open for 5% of the time, Pallas kernels for 0%

profile of v1, /device:TPU:1, one launch (start us, length us, event | category | flops | bytes accessed | tf_op | source)
XLA Modules:
  0.0 134.5 jit_solution(1610281228193099720)
XLA Ops:
  0.6 2.0 %broadcast_in_dim.18 = bf16[8,2,64,512]{3,2,1,0:T(8,128)(2,1)} broadcast(bf16[2,64,512]{2,1,0:T(8,128)(2,1)} %bitcast.59), dimensions={1,2,3} | broadcast | bytes 1179648 | tf_op jit(solution)/shard_map/broadcast_in_dim | solution.py:116
  2.6 11.0 %all-to-all-start = ((bf16[8,2,64,512]{3,2,1,0:T(8,128)(2,1)}), bf16[8,2,64,512]{3,2,1,0:T(8,128)(2,1)S(1)}, u32[]{:S(2)}, u32[]{:S(2)}) async-start(bf16[8,2,64,512]{3,2,1,0:T(8,128)(2,1)} %broadcast_in_dim.18), calls=%async_computation | async-start | bytes 2097152 | tf_op jit(solution)/shard_map/all_to_all | solution.py:116
  14.4 7.5 %collective-permute-start.3 = (bf16[128,512]{1,0:T(8,128)(2,1)S(1)}, bf16[128,512]{1,0:T(8,128)(2,1)S(1)}, u32[]{:S(2)}, u32[]{:S(2)}) collective-permute-start(bf16[128,512]{1,0:T(8,128)(2,1)S(1)} %divide_convert_fusion.refs_1_), channel_id=1, source_target_pairs={{32,0},{0,32},{33,1},{1,33},{34,2},{2,34},{35,3},{3,35},{36,4},{4,... | collective-permute-start | bytes 393224 | tf_op jit(solution)/shard_map/ppermute | solution.py:18
  21.8 3.1 %collective-permute-start.2 = (bf16[128,512]{1,0:T(8,128)(2,1)S(1)}, bf16[128,512]{1,0:T(8,128)(2,1)S(1)}, u32[]{:S(2)}, u32[]{:S(2)}) collective-permute-start(bf16[128,512]{1,0:T(8,128)(2,1)S(1)} %divide_convert_fusion.refs_1_), channel_id=1, source_target_pairs={{24,0},{0,8},{8,16},{16,24},{25,1},{1,9},{9,17},{17,25},{26,2},{2,... | collective-permute-start | bytes 393224 | tf_op jit(solution)/shard_map/ppermute | solution.py:18
  25.0 4.4 %collective-permute-start.1 = (bf16[128,512]{1,0:T(8,128)(2,1)S(1)}, bf16[128,512]{1,0:T(8,128)(2,1)S(1)}, u32[]{:S(2)}, u32[]{:S(2)}) collective-permute-start(bf16[128,512]{1,0:T(8,128)(2,1)S(1)} %divide_convert_fusion.refs_1_), channel_id=1, source_target_pairs={{16,0},{24,8},{0,16},{8,24},{17,1},{25,9},{1,17},{9,25},{18,2},{26... | collective-permute-start | bytes 393224 | tf_op jit(solution)/shard_map/ppermute | solution.py:18
  29.3 3.1 %collective-permute-start = (bf16[128,512]{1,0:T(8,128)(2,1)S(1)}, bf16[128,512]{1,0:T(8,128)(2,1)S(1)}, u32[]{:S(2)}, u32[]{:S(2)}) collective-permute-start(bf16[128,512]{1,0:T(8,128)(2,1)S(1)} %divide_convert_fusion.refs_1_), channel_id=1, source_target_pairs={{8,0},{16,8},{24,16},{0,24},{9,1},{17,9},{25,17},{1,25},{10,2},{18... | collective-permute-start | bytes 393224 | tf_op jit(solution)/shard_map/ppermute | solution.py:18
  33.3 0.7 reduce.6
  34.1 2.2 %collective-permute-start.6 = (bf16[128,512]{1,0:T(8,128)(2,1)S(1)}, bf16[128,512]{1,0:T(8,128)(2,1)S(1)}, u32[]{:S(2)}, u32[]{:S(2)}) collective-permute-start(bf16[128,512]{1,0:T(8,128)(2,1)S(1)} %collective-permute-done.3.refs_5_), channel_id=1, source_target_pairs={{24,0},{0,8},{8,16},{16,24},{25,1},{1,9},{9,17},{17,25},{26,2},{2,... | collective-permute-start | bytes 393224 | tf_op jit(solution)/shard_map/ppermute | solution.py:18
  36.3 2.8 %collective-permute-start.5 = (bf16[128,512]{1,0:T(8,128)(2,1)S(1)}, bf16[128,512]{1,0:T(8,128)(2,1)S(1)}, u32[]{:S(2)}, u32[]{:S(2)}) collective-permute-start(bf16[128,512]{1,0:T(8,128)(2,1)S(1)} %collective-permute-done.3.refs_5_), channel_id=1, source_target_pairs={{16,0},{24,8},{0,16},{8,24},{17,1},{25,9},{1,17},{9,25},{18,2},{26... | collective-permute-start | bytes 393224 | tf_op jit(solution)/shard_map/ppermute | solution.py:18
  39.1 3.4 %collective-permute-start.4 = (bf16[128,512]{1,0:T(8,128)(2,1)S(1)}, bf16[128,512]{1,0:T(8,128)(2,1)S(1)}, u32[]{:S(2)}, u32[]{:S(2)}) collective-permute-start(bf16[128,512]{1,0:T(8,128)(2,1)S(1)} %collective-permute-done.3.refs_5_), channel_id=1, source_target_pairs={{8,0},{16,8},{24,16},{0,24},{9,1},{17,9},{25,17},{1,25},{10,2},{18... | collective-permute-start | bytes 393224 | tf_op jit(solution)/shard_map/ppermute | solution.py:18
  42.6 0.7 add.209.refs_14_
  43.8 0.7 reshape.445.refs_15_
  44.4 0.9 copy.13.refs_13_
  45.3 0.7 iota_add_fusion.refs_12_
  47.3 11.7 %tile.1 = (bf16[8,2,64,512]{3,2,1,0:T(8,128)(2,1)}, bf16[2,512,640]{2,1,0:T(8,128)(2,1)}) custom-call(bf16[8,2,64,512]{3,2,1,0:T(8,128)(2,1)} %copy-done, bf16[128,512]{1,0:T(8,128)(2,1)} %copy-done.2, bf16[128,512]{1,0:T(8,128)(2,1)} %copy-done.9, bf16[128,512]{1,0:T(8,128)(2,1)} %copy-done.8, bf16[128,512]{1,0:T(8,128)(2,1)} %copy-done.7, ...), custom_call_target="tpu_custom_call" | custom-call | tf_op jit(solution)/shard_map/tile/pallas_call | solution.py:142
  59.1 8.2 %all_to_all.25 = bf16[2,512,640]{2,1,0:T(8,128)(2,1)S(1)} all-to-all(bf16[2,512,640]{2,1,0:T(8,128)(2,1)} %get-tuple-element.7), channel_id=1, replica_groups=mesh['yl'=4,'co'=2,'yh'=2,'x'=4,'z'=8] {'co'}, dimensions={0} | all-to-all | bytes 2621440 | tf_op jit(solution)/shard_map/all_to_all | solution.py:169
  67.9 13.7 %all_to_all.26 = bf16[4,128,640]{2,1,0:T(8,128)(2,1)S(1)} all-to-all(bf16[4,128,640]{2,1,0:T(8,128)(2,1)S(1)} %bitcast.56), channel_id=1, replica_groups=mesh['yl'=4,'co'=2,'yh'=2,'x'=4,'z'=8] {'x'}, dimensions={0} | all-to-all | bytes 1310720 | tf_op jit(solution)/shard_map/all_to_all | solution.py:171
  81.6 0.8 convert_reduce_fusion
  82.4 7.0 %all-to-all-start.3 = ((f32[16,8,640]{2,1,0:T(8,128)}), f32[16,8,640]{2,1,0:T(8,128)S(1)}, u32[]{:S(2)}, u32[]{:S(2)}) async-start(f32[16,8,640]{2,1,0:T(8,128)} %bitcast.33), calls=%async_computation.3 | async-start | bytes 655360 | tf_op jit(solution)/shard_map/all_to_all | solution.py:173
  89.5 3.3 %collective-permute-start.7 = (bf16[2,64,512]{2,1,0:T(8,128)(2,1)S(1)}, bf16[2,64,512]{2,1,0:T(8,128)(2,1)S(1)}, u32[]{:S(2)}, u32[]{:S(2)}) collective-permute-start(bf16[2,64,512]{2,1,0:T(8,128)(2,1)S(1)} %get-tuple-element.8), channel_id=1, source_target_pairs={{7,0},{0,1},{1,2},{2,3},{3,4},{4,5},{5,6},{6,7},{15,8},{8,9},{9,10... | collective-permute-start | bytes 393224 | tf_op jit(solution)/shard_map/ppermute | solution.py:18
  92.8 3.2 %collective-permute-start.13 = (bf16[2,64,512]{2,1,0:T(8,128)(2,1)S(1)}, bf16[2,64,512]{2,1,0:T(8,128)(2,1)S(1)}, u32[]{:S(2)}, u32[]{:S(2)}) collective-permute-start(bf16[2,64,512]{2,1,0:T(8,128)(2,1)S(1)} %get-tuple-element.9), channel_id=1, source_target_pairs={{1,0},{2,1},{3,2},{4,3},{5,4},{6,5},{7,6},{0,7},{9,8},{10,9},{11,1... | collective-permute-start | bytes 393224 | tf_op jit(solution)/shard_map/ppermute | solution.py:18
  96.0 4.2 %collective-permute-start.12 = (bf16[2,64,512]{2,1,0:T(8,128)(2,1)S(1)}, bf16[2,64,512]{2,1,0:T(8,128)(2,1)S(1)}, u32[]{:S(2)}, u32[]{:S(2)}) collective-permute-start(bf16[2,64,512]{2,1,0:T(8,128)(2,1)S(1)} %get-tuple-element.10), channel_id=1, source_target_pairs={{2,0},{3,1},{4,2},{5,3},{6,4},{7,5},{0,6},{1,7},{10,8},{11,9},{12,... | collective-permute-start | bytes 393224 | tf_op jit(solution)/shard_map/ppermute | solution.py:18
  100.2 4.9 %collective-permute-start.11 = (bf16[2,64,512]{2,1,0:T(8,128)(2,1)S(1)}, bf16[2,64,512]{2,1,0:T(8,128)(2,1)S(1)}, u32[]{:S(2)}, u32[]{:S(2)}) collective-permute-start(bf16[2,64,512]{2,1,0:T(8,128)(2,1)S(1)} %get-tuple-element.11), channel_id=1, source_target_pairs={{3,0},{4,1},{5,2},{6,3},{7,4},{0,5},{1,6},{2,7},{11,8},{12,9},{13,... | collective-permute-start | bytes 393224 | tf_op jit(solution)/shard_map/ppermute | solution.py:18
  105.2 3.4 %collective-permute-start.10 = (bf16[2,64,512]{2,1,0:T(8,128)(2,1)S(1)}, bf16[2,64,512]{2,1,0:T(8,128)(2,1)S(1)}, u32[]{:S(2)}, u32[]{:S(2)}) collective-permute-start(bf16[2,64,512]{2,1,0:T(8,128)(2,1)S(1)} %get-tuple-element.12), channel_id=1, source_target_pairs={{4,0},{5,1},{6,2},{7,3},{0,4},{1,5},{2,6},{3,7},{12,8},{13,9},{14,... | collective-permute-start | bytes 393224 | tf_op jit(solution)/shard_map/ppermute | solution.py:18
  108.5 3.7 %collective-permute-start.9 = (bf16[2,64,512]{2,1,0:T(8,128)(2,1)S(1)}, bf16[2,64,512]{2,1,0:T(8,128)(2,1)S(1)}, u32[]{:S(2)}, u32[]{:S(2)}) collective-permute-start(bf16[2,64,512]{2,1,0:T(8,128)(2,1)S(1)} %get-tuple-element.13), channel_id=1, source_target_pairs={{5,0},{6,1},{7,2},{0,3},{1,4},{2,5},{3,6},{4,7},{13,8},{14,9},{15,... | collective-permute-start | bytes 393224 | tf_op jit(solution)/shard_map/ppermute | solution.py:18
  112.3 5.5 %collective-permute-start.8 = (bf16[2,64,512]{2,1,0:T(8,128)(2,1)S(1)}, bf16[2,64,512]{2,1,0:T(8,128)(2,1)S(1)}, u32[]{:S(2)}, u32[]{:S(2)}) collective-permute-start(bf16[2,64,512]{2,1,0:T(8,128)(2,1)S(1)} %get-tuple-element.14), channel_id=1, source_target_pairs={{6,0},{7,1},{0,2},{1,3},{2,4},{3,5},{4,6},{5,7},{14,8},{15,9},{8,1... | collective-permute-start | bytes 393224 | tf_op jit(solution)/shard_map/ppermute | solution.py:18
  117.8 0.7 broadcast_in_dim.40
  118.5 8.7 %all-to-all-start.4 = ((f32[8,8,640]{2,1,0:T(8,128)}), f32[8,8,640]{2,1,0:T(8,128)S(1)}, u32[]{:S(2)}, u32[]{:S(2)}) async-start(f32[8,8,640]{2,1,0:T(8,128)} %broadcast_in_dim.40), calls=%async_computation.4 | async-start | bytes 327680 | tf_op jit(solution)/shard_map/all_to_all | solution.py:175
  127.5 1.8 %collective-permute-done.8 = bf16[2,64,512]{2,1,0:T(8,128)(2,1)S(1)} collective-permute-done((bf16[2,64,512]{2,1,0:T(8,128)(2,1)S(1)}, bf16[2,64,512]{2,1,0:T(8,128)(2,1)S(1)}, u32[]{:S(2)}, u32[]{:S(2)}) %collective-permute-start.8) | collective-permute-done | bytes 131104 | tf_op jit(solution)/shard_map/ppermute | solution.py:18
  129.4 0.8 fusion.10
  130.2 3.1 %all-to-all-done.4 = f32[8,8,640]{2,1,0:T(8,128)S(1)} async-done(((f32[8,8,640]{2,1,0:T(8,128)}), f32[8,8,640]{2,1,0:T(8,128)S(1)}, u32[]{:S(2)}, u32[]{:S(2)}) %all-to-all-start.4) | async-done | bytes 163872 | tf_op jit(solution)/shard_map/all_to_all | solution.py:175
  133.3 0.6 slice_reduce_fusion
  (65 shorter events, 5.0 us)
Async XLA Ops:
  2.6 11.0 %copy-start.3 = (bf16[512,512]{1,0:T(8,128)(2,1)S(1)}, bf16[512,512]{1,0:T(8,128)(2,1)}, u32[]{:S(2)}) copy-start(bf16[512,512]{1,0:T(8,128)(2,1)} %refs_10_.1) | copy-start | bytes 1572868
  2.6 11.0 %copy-start.4 = (bf16[512,512]{1,0:T(8,128)(2,1)S(1)}, bf16[512,512]{1,0:T(8,128)(2,1)}, u32[]{:S(2)}) copy-start(bf16[512,512]{1,0:T(8,128)(2,1)} %refs_9_.1) | copy-start | bytes 1572868
  2.6 11.0 %copy-start.5 = (bf16[1,2,64,512]{3,2,1,0:T(8,128)(2,1)S(1)}, bf16[1,2,64,512]{3,2,1,0:T(8,128)(2,1)}, u32[]{:S(2)}) copy-start(bf16[1,2,64,512]{3,2,1,0:T(8,128)(2,1)} %param.5) | copy-start | bytes 393220
  2.6 11.0 %copy-start.14 = (f32[512]{0:T(512)S(1)}, f32[512]{0:T(512)}, u32[]{:S(2)}) copy-start(f32[512]{0:T(512)} %param.8) | copy-start | bytes 6148
  2.6 43.6 %all-to-all-start = ((bf16[8,2,64,512]{3,2,1,0:T(8,128)(2,1)}), bf16[8,2,64,512]{3,2,1,0:T(8,128)(2,1)S(1)}, u32[]{:S(2)}, u32[]{:S(2)}) async-start(bf16[8,2,64,512]{3,2,1,0:T(8,128)(2,1)} %broadcast_in_dim.18), calls=%async_computation | async-start | bytes 2097152 | tf_op jit(solution)/shard_map/all_to_all | solution.py:116
  13.6 19.6 %copy-start.13 = (s32[1,4096]{1,0:T(1,128)S(1)}, s32[1,4096]{1,0:T(1,128)}, u32[]{:S(2)}) copy-start(s32[1,4096]{1,0:T(1,128)} %param.6) | copy-start | bytes 49156
  14.4 31.9 %copy-start.2 = (bf16[128,512]{1,0:T(8,128)(2,1)}, bf16[128,512]{1,0:T(8,128)(2,1)S(1)}, u32[]{:S(2)}) copy-start(bf16[128,512]{1,0:T(8,128)(2,1)S(1)} %divide_convert_fusion.refs_1_) | copy-start | bytes 393220
  14.4 19.7 %collective-permute-start.3 = (bf16[128,512]{1,0:T(8,128)(2,1)S(1)}, bf16[128,512]{1,0:T(8,128)(2,1)S(1)}, u32[]{:S(2)}, u32[]{:S(2)}) collective-permute-start(bf16[128,512]{1,0:T(8,128)(2,1)S(1)} %divide_convert_fusion.refs_1_), channel_id=1, source_target_pairs={{32,0},{0,32},{33,1},{1,33},{34,2},{2,34},{35,3},{3,35},{36,4},{4,... | collective-permute-start | bytes 393224 | tf_op jit(solution)/shard_map/ppermute | solution.py:18
  21.8 17.3 %collective-permute-start.2 = (bf16[128,512]{1,0:T(8,128)(2,1)S(1)}, bf16[128,512]{1,0:T(8,128)(2,1)S(1)}, u32[]{:S(2)}, u32[]{:S(2)}) collective-permute-start(bf16[128,512]{1,0:T(8,128)(2,1)S(1)} %divide_convert_fusion.refs_1_), channel_id=1, source_target_pairs={{24,0},{0,8},{8,16},{16,24},{25,1},{1,9},{9,17},{17,25},{26,2},{2,... | collective-permute-start | bytes 393224 | tf_op jit(solution)/shard_map/ppermute | solution.py:18
  25.0 21.1 %collective-permute-start.1 = (bf16[128,512]{1,0:T(8,128)(2,1)S(1)}, bf16[128,512]{1,0:T(8,128)(2,1)S(1)}, u32[]{:S(2)}, u32[]{:S(2)}) collective-permute-start(bf16[128,512]{1,0:T(8,128)(2,1)S(1)} %divide_convert_fusion.refs_1_), channel_id=1, source_target_pairs={{16,0},{24,8},{0,16},{8,24},{17,1},{25,9},{1,17},{9,25},{18,2},{26... | collective-permute-start | bytes 393224 | tf_op jit(solution)/shard_map/ppermute | solution.py:18
  29.3 16.7 %collective-permute-start = (bf16[128,512]{1,0:T(8,128)(2,1)S(1)}, bf16[128,512]{1,0:T(8,128)(2,1)S(1)}, u32[]{:S(2)}, u32[]{:S(2)}) collective-permute-start(bf16[128,512]{1,0:T(8,128)(2,1)S(1)} %divide_convert_fusion.refs_1_), channel_id=1, source_target_pairs={{8,0},{16,8},{24,16},{0,24},{9,1},{17,9},{25,17},{1,25},{10,2},{18... | collective-permute-start | bytes 393224 | tf_op jit(solution)/shard_map/ppermute | solution.py:18
  34.1 12.2 %copy-start.6 = (bf16[128,512]{1,0:T(8,128)(2,1)}, bf16[128,512]{1,0:T(8,128)(2,1)S(1)}, u32[]{:S(2)}) copy-start(bf16[128,512]{1,0:T(8,128)(2,1)S(1)} %collective-permute-done.3.refs_5_) | copy-start | bytes 393220
  34.1 12.0 %collective-permute-start.6 = (bf16[128,512]{1,0:T(8,128)(2,1)S(1)}, bf16[128,512]{1,0:T(8,128)(2,1)S(1)}, u32[]{:S(2)}, u32[]{:S(2)}) collective-permute-start(bf16[128,512]{1,0:T(8,128)(2,1)S(1)} %collective-permute-done.3.refs_5_), channel_id=1, source_target_pairs={{24,0},{0,8},{8,16},{16,24},{25,1},{1,9},{9,17},{17,25},{26,2},{2,... | collective-permute-start | bytes 393224 | tf_op jit(solution)/shard_map/ppermute | solution.py:18
  36.3 9.8 %collective-permute-start.5 = (bf16[128,512]{1,0:T(8,128)(2,1)S(1)}, bf16[128,512]{1,0:T(8,128)(2,1)S(1)}, u32[]{:S(2)}, u32[]{:S(2)}) collective-permute-start(bf16[128,512]{1,0:T(8,128)(2,1)S(1)} %collective-permute-done.3.refs_5_), channel_id=1, source_target_pairs={{16,0},{24,8},{0,16},{8,24},{17,1},{25,9},{1,17},{9,25},{18,2},{26... | collective-permute-start | bytes 393224 | tf_op jit(solution)/shard_map/ppermute | solution.py:18
  39.1 7.2 %copy-start.7 = (bf16[128,512]{1,0:T(8,128)(2,1)}, bf16[128,512]{1,0:T(8,128)(2,1)S(1)}, u32[]{:S(2)}) copy-start(bf16[128,512]{1,0:T(8,128)(2,1)S(1)} %collective-permute-done.2.refs_4_) | copy-start | bytes 393220
  39.1 7.1 %collective-permute-start.4 = (bf16[128,512]{1,0:T(8,128)(2,1)S(1)}, bf16[128,512]{1,0:T(8,128)(2,1)S(1)}, u32[]{:S(2)}, u32[]{:S(2)}) collective-permute-start(bf16[128,512]{1,0:T(8,128)(2,1)S(1)} %collective-permute-done.3.refs_5_), channel_id=1, source_target_pairs={{8,0},{16,8},{24,16},{0,24},{9,1},{17,9},{25,17},{1,25},{10,2},{18... | collective-permute-start | bytes 393224 | tf_op jit(solution)/shard_map/ppermute | solution.py:18
  46.0 0.6 copy-start.8
  46.0 0.7 copy-start.9
  46.1 0.7 copy-start.10
  46.1 0.8 copy-start.11
  46.3 0.7 copy-start.12
  46.3 1.0 copy-start
  67.9 21.6 %copy-start.1 = (bf16[8,2,64,512]{3,2,1,0:T(8,128)(2,1)S(1)}, bf16[8,2,64,512]{3,2,1,0:T(8,128)(2,1)}, u32[]{:S(2)}) copy-start(bf16[8,2,64,512]{3,2,1,0:T(8,128)(2,1)} %get-tuple-element.6) | copy-start | bytes 3145732
  82.4 35.3 %all-to-all-start.3 = ((f32[16,8,640]{2,1,0:T(8,128)}), f32[16,8,640]{2,1,0:T(8,128)S(1)}, u32[]{:S(2)}, u32[]{:S(2)}) async-start(f32[16,8,640]{2,1,0:T(8,128)} %bitcast.33), calls=%async_computation.3 | async-start | bytes 655360 | tf_op jit(solution)/shard_map/all_to_all | solution.py:173
  89.5 19.0 %collective-permute-start.7 = (bf16[2,64,512]{2,1,0:T(8,128)(2,1)S(1)}, bf16[2,64,512]{2,1,0:T(8,128)(2,1)S(1)}, u32[]{:S(2)}, u32[]{:S(2)}) collective-permute-start(bf16[2,64,512]{2,1,0:T(8,128)(2,1)S(1)} %get-tuple-element.8), channel_id=1, source_target_pairs={{7,0},{0,1},{1,2},{2,3},{3,4},{4,5},{5,6},{6,7},{15,8},{8,9},{9,10... | collective-permute-start | bytes 393224 | tf_op jit(solution)/shard_map/ppermute | solution.py:18
  92.8 19.5 %collective-permute-start.13 = (bf16[2,64,512]{2,1,0:T(8,128)(2,1)S(1)}, bf16[2,64,512]{2,1,0:T(8,128)(2,1)S(1)}, u32[]{:S(2)}, u32[]{:S(2)}) collective-permute-start(bf16[2,64,512]{2,1,0:T(8,128)(2,1)S(1)} %get-tuple-element.9), channel_id=1, source_target_pairs={{1,0},{2,1},{3,2},{4,3},{5,4},{6,5},{7,6},{0,7},{9,8},{10,9},{11,1... | collective-permute-start | bytes 393224 | tf_op jit(solution)/shard_map/ppermute | solution.py:18
  96.0 31.2 %collective-permute-start.12 = (bf16[2,64,512]{2,1,0:T(8,128)(2,1)S(1)}, bf16[2,64,512]{2,1,0:T(8,128)(2,1)S(1)}, u32[]{:S(2)}, u32[]{:S(2)}) collective-permute-start(bf16[2,64,512]{2,1,0:T(8,128)(2,1)S(1)} %get-tuple-element.10), channel_id=1, source_target_pairs={{2,0},{3,1},{4,2},{5,3},{6,4},{7,5},{0,6},{1,7},{10,8},{11,9},{12,... | collective-permute-start | bytes 393224 | tf_op jit(solution)/shard_map/ppermute | solution.py:18
  100.2 27.0 %collective-permute-start.11 = (bf16[2,64,512]{2,1,0:T(8,128)(2,1)S(1)}, bf16[2,64,512]{2,1,0:T(8,128)(2,1)S(1)}, u32[]{:S(2)}, u32[]{:S(2)}) collective-permute-start(bf16[2,64,512]{2,1,0:T(8,128)(2,1)S(1)} %get-tuple-element.11), channel_id=1, source_target_pairs={{3,0},{4,1},{5,2},{6,3},{7,4},{0,5},{1,6},{2,7},{11,8},{12,9},{13,... | collective-permute-start | bytes 393224 | tf_op jit(solution)/shard_map/ppermute | solution.py:18
  105.2 22.1 %collective-permute-start.10 = (bf16[2,64,512]{2,1,0:T(8,128)(2,1)S(1)}, bf16[2,64,512]{2,1,0:T(8,128)(2,1)S(1)}, u32[]{:S(2)}, u32[]{:S(2)}) collective-permute-start(bf16[2,64,512]{2,1,0:T(8,128)(2,1)S(1)} %get-tuple-element.12), channel_id=1, source_target_pairs={{4,0},{5,1},{6,2},{7,3},{0,4},{1,5},{2,6},{3,7},{12,8},{13,9},{14,... | collective-permute-start | bytes 393224 | tf_op jit(solution)/shard_map/ppermute | solution.py:18
  108.5 19.0 %collective-permute-start.9 = (bf16[2,64,512]{2,1,0:T(8,128)(2,1)S(1)}, bf16[2,64,512]{2,1,0:T(8,128)(2,1)S(1)}, u32[]{:S(2)}, u32[]{:S(2)}) collective-permute-start(bf16[2,64,512]{2,1,0:T(8,128)(2,1)S(1)} %get-tuple-element.13), channel_id=1, source_target_pairs={{5,0},{6,1},{7,2},{0,3},{1,4},{2,5},{3,6},{4,7},{13,8},{14,9},{15,... | collective-permute-start | bytes 393224 | tf_op jit(solution)/shard_map/ppermute | solution.py:18
  112.3 17.1 %collective-permute-start.8 = (bf16[2,64,512]{2,1,0:T(8,128)(2,1)S(1)}, bf16[2,64,512]{2,1,0:T(8,128)(2,1)S(1)}, u32[]{:S(2)}, u32[]{:S(2)}) collective-permute-start(bf16[2,64,512]{2,1,0:T(8,128)(2,1)S(1)} %get-tuple-element.14), channel_id=1, source_target_pairs={{6,0},{7,1},{0,2},{1,3},{2,4},{3,5},{4,6},{5,7},{14,8},{15,9},{8,1... | collective-permute-start | bytes 393224 | tf_op jit(solution)/shard_map/ppermute | solution.py:18
  118.5 14.8 %all-to-all-start.4 = ((f32[8,8,640]{2,1,0:T(8,128)}), f32[8,8,640]{2,1,0:T(8,128)S(1)}, u32[]{:S(2)}, u32[]{:S(2)}) async-start(f32[8,8,640]{2,1,0:T(8,128)} %broadcast_in_dim.40), calls=%async_computation.4 | async-start | bytes 327680 | tf_op jit(solution)/shard_map/all_to_all | solution.py:175

commit v2 on v1

v2 whole, which is shorter than its diff:
```python
import functools

import jax
import jax.numpy as jnp
from jax import lax
from jax.experimental import pallas as pl
from jax.experimental.pallas import tpu as pltpu
from jax.sharding import Mesh
from jax.sharding import PartitionSpec as P

BLK = ("yh", "x", "z")
SUB = ("yl", "co")
temper = 0.2
epsilon = 1e-06
LANES = 128


def shifted(value, axis, by):
    count = lax.axis_size(axis)
    return lax.ppermute(value, axis, [((i + by) % count, i) for i in range(count)])


def dot_nn(a, b):
    return lax.dot_general(a, b, (((1,), (0,)), ((), ())), preferred_element_type=jnp.float32)


def dot_nt(a, b):
    return lax.dot_general(a, b, (((1,), (1,)), ((), ())), preferred_element_type=jnp.float32)


def dot_tn(a, b):
    return lax.dot_general(a, b, (((0,), (0,)), ((), ())), preferred_element_type=jnp.float32)


def tile_kernel(*refs, nz, nx, ny, half, width, negatives, order):
    groups = 6
    rows_ref = refs[0]
    col_refs = refs[1 : 1 + groups]
    w_one_ref, w_two_ref, b_one_ref, pos_ref, pos_t_ref = refs[1 + groups : 6 + groups]
    feats_out, weights_out, cols_s, hid_s, gp_s, pre_s, cpos_s = refs[6 + groups :]
    my_z, my_x, my_y = lax.axis_index("z"), lax.axis_index("x"), lax.axis_index("yh")
    my_yx = my_y * nx + my_x
    count = len(order)
    at = 0
    for ref in col_refs:
        for i in range(ref.shape[0]):
            for v in range(2):
                cols_s[v, at * half : (at + 1) * half, :] = ref[i, v * half : (v + 1) * half, :]
            at += 1
    lane = lax.broadcasted_iota(jnp.int32, (1, count * half), 1)
    cid = lax.rem(lane, half)
    for j, (dy, dx) in enumerate(order):
        block = (lax.rem(my_y + dy, ny) * nx + lax.rem(my_x + dx, nx)) * nz + my_z
        cid = cid + jnp.where(lane // half == j, block * half, 0)
        cpos_s[:, j * half : (j + 1) * half] = pos_ref[pl.ds(block, 1), :]
    cpos = cpos_s[...]
    w_one = w_one_ref[...]
    w_two = w_two_ref[...]
    per = 256 // half
    chunk = per * half
    bias = jnp.zeros((1, width), jnp.float32)
    block_lane = lax.broadcasted_iota(jnp.int32, pos_t_ref.shape, 1)
    for v in range(2):
        for k in range(nz // per):
            x = rows_ref[k * per : (k + 1) * per, v].reshape(chunk, width)
            stack_at = slice((v * nz * half) + k * chunk, (v * nz * half) + (k + 1) * chunk)
            pre = dot_nn(x, w_one) + b_one_ref[...]
            grow = jnp.exp(jnp.minimum(pre, 0.0))
            above = pre > 0
            hidden = jnp.where(above, pre, grow - 1.0).astype(jnp.bfloat16)
            slope = jnp.where(above, 1.0, grow)
            projected = dot_nn(hidden, w_two)
            radius = jnp.sqrt(jnp.sum(projected * projected, axis=1, keepdims=True) + epsilon)
            unit = projected / radius
            sent = unit.astype(jnp.bfloat16)
            first_row = (my_yx * nz + k * per) * half
            rid = first_row + lax.broadcasted_iota(jnp.int32, (chunk, 1), 0)
            if v == 0:
                rpos = jnp.concatenate(
                    [
                        jnp.sum(
                            jnp.where(block_lane == my_yx * nz + k * per + j, pos_t_ref[...], 0),
                            axis=1,
                            keepdims=True,
                        )
                        for j in range(per)
                    ],
                    axis=0,
                )
            total = None
            for cv in range(2):
                col = cols_s[cv]
                scores = dot_nt(sent, col) / temper
                g = jax.nn.sigmoid(scores)
                base = g * (2.0 / negatives)
                if v == cv:
                    coef = jnp.where(rid == cid, 0.0, base)
                elif v == 0:
                    coef = jnp.where(rpos == cid, 2.0 * g - 2.0, base)
                else:
                    coef = jnp.where(rid == cpos, 2.0 * g - 2.0, base)
                part = dot_nn(coef.astype(jnp.bfloat16), col)
                total = part if total is None else total + part
            grad_unit = total / temper
            inner = jnp.sum(unit * grad_unit, axis=1, keepdims=True)
            grad_proj = ((grad_unit - unit * inner) / radius).astype(jnp.bfloat16)
            grad_pre = (dot_nt(grad_proj, w_two) * slope).astype(jnp.bfloat16)
            grad_rows = dot_nt(grad_pre, w_one).astype(jnp.bfloat16)
            bias = bias + jnp.sum(grad_pre.astype(jnp.float32), axis=0, keepdims=True)
            hid_s[stack_at, :] = hidden
            gp_s[stack_at, :] = grad_proj
            pre_s[stack_at, :] = grad_pre
            for j in range(per):
                block = k * per + j
                feats_out[lax.rem(block + nz - my_z, nz), v] = grad_rows[j * half : (j + 1) * half]
    rows_all = jnp.concatenate(
        [rows_ref[:, v].reshape(nz * half, width) for v in range(2)], axis=0
    )
    parts = (
        dot_tn(rows_all, pre_s[...]).astype(jnp.bfloat16),
        dot_tn(hid_s[...], gp_s[...]).astype(jnp.bfloat16),
    )
    per_x = width // (ny * nx)
    rows_x = ny * per_x
    tiles = width // LANES
    tile_lane = lax.broadcasted_iota(jnp.int32, (8, LANES), 1)
    for c in range(2):
        for x in range(nx):
            piece = c * nx + x
            for t in range(tiles):
                for y in range(ny):
                    source = (y * nx + x) * per_x
                    target = t * rows_x + y * per_x
                    weights_out[piece, target : target + per_x, :] = parts[c][
                        source : source + per_x, t * LANES : (t + 1) * LANES
                    ]
            picked = []
            for y in range(ny):
                source = (y * nx + x) * per_x
                low = source // LANES * LANES
                part = jnp.broadcast_to(bias[:, low : low + LANES], (8, LANES))
                turn = (y * per_x - source) % LANES
                picked.append(pltpu.roll(part, turn, 1) if turn else part)
            row = jnp.where(tile_lane < per_x, picked[0], picked[1])
            weights_out[piece, tiles * rows_x :, :] = row.astype(jnp.bfloat16)


def first_sum(got_ref, out_ref, *, tiles, per_block, receivers):
    total = got_ref[0].astype(jnp.float32)
    for i in range(1, got_ref.shape[0]):
        total = total + got_ref[i].astype(jnp.float32)
    rows_x = receivers * per_block
    for r in range(receivers):
        picked = [
            total[t * rows_x + r * per_block : t * rows_x + (r + 1) * per_block]
            for t in range(tiles)
        ]
        picked.append(total[tiles * rows_x :])
        out_ref[r] = jnp.concatenate(picked, axis=0).astype(jnp.bfloat16)


def second_sum(got_ref, out_ref):
    total = got_ref[0].astype(jnp.float32)
    for i in range(1, got_ref.shape[0]):
        total = total + got_ref[i].astype(jnp.float32)
    for i in range(out_ref.shape[0]):
        out_ref[i] = total


def third_sum(got_ref, one_ref, two_ref, bias_ref, *, tiles, per_block, nz, scale):
    for c, ref in enumerate((one_ref, two_ref)):
        total = got_ref[c]
        for i in range(2 + c, got_ref.shape[0], 2):
            total = total + got_ref[i]
        total = total * scale
        for t in range(tiles):
            ref[:, t * LANES : (t + 1) * LANES] = total[t * per_block : (t + 1) * per_block]
        if c == 0:
            start = (lax.axis_index("yh") * nz + lax.axis_index("z")) * per_block
            last = jnp.broadcast_to(total[tiles * per_block : tiles * per_block + 1], (8, LANES))
            bias_ref[...] = pltpu.roll(last, lax.rem(LANES - start, LANES), 1)[:1]


def step(feats, pos, w_one, b_one, w_two):
    half = feats.shape[2]
    width = feats.shape[3]
    nz, nx, ny = lax.axis_size("z"), lax.axis_size("x"), lax.axis_size("yh")
    subs = lax.axis_size(SUB)
    blocks = nz * nx * ny
    negatives = 2.0 * half * blocks - 2.0
    own = feats[0]
    rows = lax.all_to_all(jnp.broadcast_to(own[None], (nz, *own.shape)), "z", 0, 0, tiled=True)

    flat = own.reshape(2 * half, width)
    pre_act = dot_nn(flat, w_one) + b_one
    hidden = jax.nn.elu(pre_act).astype(jnp.bfloat16)
    projected = dot_nn(hidden, w_two)
    radius = jnp.sqrt(jnp.sum(projected * projected, axis=1, keepdims=True) + epsilon)
    sent = (projected / radius).astype(jnp.bfloat16)[None]

    across = shifted(sent, "yh", 1)
    own_far = shifted(sent, "x", 2)
    both = jnp.concatenate([sent, across], axis=0)
    both_next = shifted(both, "x", 1)
    both_last = shifted(both, "x", 3)
    across_far = shifted(across, "x", 2)
    cols = [sent, across, both_next, both_last, own_far, across_far]
    order = [(0, 0), (1, 0), (0, 1), (1, 1), (0, 3), (1, 3), (0, 2), (1, 2)]
    pos_square = pos[0].reshape(blocks, half)

    vmem = pl.BlockSpec(memory_space=pltpu.VMEM)
    piece_rows = width // nx // 2 * 2 * (width // LANES) + 8
    shares, weights = pl.pallas_call(
        lambda *refs: tile_kernel(
            *refs, nz=nz, nx=nx, ny=ny, half=half, width=width, negatives=negatives, order=order
        ),
        in_specs=[vmem] * (len(cols) + 6),
        out_specs=[vmem, vmem],
        out_shape=[
            jax.ShapeDtypeStruct((nz, 2, half, width), jnp.bfloat16),
            jax.ShapeDtypeStruct((2 * nx, piece_rows, LANES), jnp.bfloat16),
        ],
        scratch_shapes=[
            pltpu.VMEM((2, len(order) * half, width), jnp.bfloat16),
            pltpu.VMEM((2 * nz * half, width), jnp.bfloat16),
            pltpu.VMEM((2 * nz * half, width), jnp.bfloat16),
            pltpu.VMEM((2 * nz * half, width), jnp.bfloat16),
            pltpu.VMEM((1, len(order) * half), jnp.int32),
        ],
        name="tile",
    )(rows, *cols, w_one, w_two, b_one[None], pos_square, pos_square.T)

    tiles = width // LANES
    per_block = width // blocks
    receivers = ny * nz
    short = tiles * per_block + 8
    got = lax.all_to_all(weights, ("co", "x"), 0, 0, tiled=True)
    got = pl.pallas_call(
        functools.partial(first_sum, tiles=tiles, per_block=per_block, receivers=receivers),
        in_specs=[vmem],
        out_specs=vmem,
        out_shape=jax.ShapeDtypeStruct((receivers, short, LANES), jnp.bfloat16),
        name="first_sum",
    )(got)
    got = lax.all_to_all(got, ("yh", "z"), 0, 0, tiled=True)
    got = pl.pallas_call(
        second_sum,
        in_specs=[vmem],
        out_specs=vmem,
        out_shape=jax.ShapeDtypeStruct((subs, short, LANES), jnp.float32),
        name="second_sum",
    )(got)
    got = lax.all_to_all(got, SUB, 0, 0, tiled=True)
    share_one, share_two, share_bias = pl.pallas_call(
        functools.partial(
            third_sum,
            tiles=tiles,
            per_block=per_block,
            nz=nz,
            scale=1.0 / (2.0 * half * blocks * subs),
        ),
        in_specs=[vmem],
        out_specs=[vmem] * 3,
        out_shape=[
            jax.ShapeDtypeStruct((per_block, width), jnp.float32),
            jax.ShapeDtypeStruct((per_block, width), jnp.float32),
            jax.ShapeDtypeStruct((1, LANES), jnp.float32),
        ],
        name="third_sum",
    )(got)
    share_bias = share_bias[0, :per_block]

    pieces = [shares[0]]
    for d in range(1, nz):
        pieces.append(shifted(shares[d], "z", -d))
    grad = pieces[0].astype(jnp.float32)
    for piece in pieces[1:]:
        grad = grad + piece.astype(jnp.float32)
    grad_feats = grad.astype(jnp.bfloat16)[None]
    return (grad_feats, share_one, share_bias, share_two)


def solution(mesh):
    torus = Mesh(mesh.devices.reshape(4, 2, 2, 4, 8), ("yl", "co", "yh", "x", "z"))
    in_specs = (P(SUB, None, BLK, None), P(SUB, None), P(), P(), P())
    out_specs = (P(SUB, None, BLK, None), P(BLK, None), P(BLK), P(BLK, None))
    return jax.shard_map(step, mesh=torus, in_specs=in_specs, out_specs=out_specs, check_vma=False)
```

time: 136 us -> 142 us (1.044)
  waiting for transfers between devices: 5.45 us -> 11 us
  Pallas kernels: 11.7 us -> 16.5 us
  other arithmetic: 3.86 us -> 1.61 us
  local copies, waits for them, and re-layouts: 8.55 us -> 6.89 us
    ppermute x14 -> x12, waiting for transfers between devices: 2.35 us -> 9.43 us  [shifted(): lax.ppermute(value, axis, [((i + by) % count, i) for i in range(count)])]
    ppermute x14 -> x12, starting transfers between devices: 54.6 us -> 48.9 us  [shifted(): lax.ppermute(value, axis, [((i + by) % count, i) for i in range(count)])]
    all_to_all x3, starting transfers between devices: 26.7 us -> 31.9 us  [the longest x1 14.7 us: step(): got = lax.all_to_all(got, ('yh', 'z'), 0, 0, tiled=True)]
    pallas_call x1 -> x4, Pallas kernels: 11.7 us -> 16.5 us  [the longest x1 11.3 us: step(): pl.pallas_call(lambda *refs: tile_kernel(*refs, nz=nz, nx=nx, ny=ny, half...]
    broadcast_in_dim x4 -> x1, local copies, waits for them, and re-layouts: 3.55 us -> 1.99 us  [step(): jnp.broadcast_to(own[None], (nz, *own.shape))]
    all_to_all x3, waiting for transfers between devices: 3.1 us -> 1.56 us  [the longest x1 1.55 us: step(): got = lax.all_to_all(got, SUB, 0, 0, tiled=True)]
    reduce_sum x4 -> x0, other arithmetic: 1.46 us -> none  [the longest x1 0.8 us: local(): got = jnp.sum(got.astype(jnp.float32), axis=0)]
    unnamed x31 -> x33, local copies, waits for them, and re-layouts: 1.57 us -> 2.96 us
  transfers between devices with their start and end apart: 17 -> 15, of which waited for: 4 -> 5; matrix products, arithmetic and copies ran while one was open for 5% -> 2% of each run, Pallas kernels for 0% -> 1%
where the time goes in v2:
time: 142 us; the launch traced here: 141 us
  starting transfers between devices  80.8 us (57%)
  blocking collectives  22.6 us (16%)
  Pallas kernels  16.5 us (12%)
  waiting for transfers between devices  11 us (8%)
  local copies, waits for them, and re-layouts  6.89 us (5%)
  other arithmetic  1.61 us (1%)
    ppermute x12, starting transfers between devices, shifted(): lax.ppermute(value, axis, [((i + by) % count, i) for i in range(count)])  48.9 us
    all_to_all x1, blocking collectives, step(): got = lax.all_to_all(weights, ('co', 'x'), 0, 0, tiled=True)  22.6 us
    all_to_all x1, starting transfers between devices, step(): got = lax.all_to_all(got, ('yh', 'z'), 0, 0, tiled=True)  14.7 us
    pallas_call x1, Pallas kernels, step(): pl.pallas_call(lambda *refs: tile_kernel(*refs, nz=nz, nx=nx, ny=ny, half...  11.3 us
    all_to_all x1, starting transfers between devices, step(): lax.all_to_all(jnp.broadcast_to(own[None], (nz, *own.shape)), 'z', 0, 0,...  11 us
    ppermute x12, waiting for transfers between devices, shifted(): lax.ppermute(value, axis, [((i + by) % count, i) for i in range(count)])  9.43 us
    all_to_all x1, starting transfers between devices, step(): got = lax.all_to_all(got, SUB, 0, 0, tiled=True)  6.2 us
    unnamed x33, local copies, waits for them, and re-layouts  2.96 us
  transfers between devices with their start and end apart: 15, of which 5 were waited for; matrix products, arithmetic and copies ran while one was open for 2% of the time, Pallas kernels for 1%

profile of v2, /device:TPU:1, one launch (start us, length us, event | category | flops | bytes accessed | tf_op | source)
XLA Modules:
  0.0 140.9 jit_solution(15193665313266176305)
XLA Ops:
  0.6 2.0 %broadcast_in_dim.22 = bf16[8,2,64,512]{3,2,1,0:T(8,128)(2,1)} broadcast(bf16[2,64,512]{2,1,0:T(8,128)(2,1)} %bitcast.31), dimensions={1,2,3} | broadcast | bytes 1179648 | tf_op jit(solution)/shard_map/broadcast_in_dim | solution.py:192
  2.6 11.0 %all-to-all-start = ((bf16[8,2,64,512]{3,2,1,0:T(8,128)(2,1)}), bf16[8,2,64,512]{3,2,1,0:T(8,128)(2,1)S(1)}, u32[]{:S(2)}, u32[]{:S(2)}) async-start(bf16[8,2,64,512]{3,2,1,0:T(8,128)(2,1)} %broadcast_in_dim.22), calls=%async_computation | async-start | bytes 2097152 | tf_op jit(solution)/shard_map/all_to_all | solution.py:192
  14.4 7.5 %collective-permute-start = (bf16[1,128,512]{2,1,0:T(8,128)(2,1)S(1)}, bf16[1,128,512]{2,1,0:T(8,128)(2,1)S(1)}, u32[]{:S(2)}, u32[]{:S(2)}) collective-permute-start(bf16[1,128,512]{2,1,0:T(8,128)(2,1)S(1)} %fusion.13.refs_1_), channel_id=1, source_target_pairs={{32,0},{0,32},{33,1},{1,33},{34,2},{2,34},{35,3},{3,35},{36,4},{4,... | collective-permute-start | bytes 393224 | tf_op jit(solution)/shard_map/ppermute | solution.py:20
  21.8 2.8 %collective-permute-done.refs_2_ = bf16[1,128,512]{2,1,0:T(8,128)(2,1)S(1)} collective-permute-done((bf16[1,128,512]{2,1,0:T(8,128)(2,1)S(1)}, bf16[1,128,512]{2,1,0:T(8,128)(2,1)S(1)}, u32[]{:S(2)}, u32[]{:S(2)}) %collective-permute-start) | collective-permute-done | bytes 131104 | tf_op jit(solution)/shard_map/ppermute | solution.py:20
  24.7 3.1 %collective-permute-start.2 = (bf16[2,128,512]{2,1,0:T(8,128)(2,1)S(1)}, bf16[2,128,512]{2,1,0:T(8,128)(2,1)S(1)}, u32[]{:S(2)}, u32[]{:S(2)}) collective-permute-start(bf16[2,128,512]{2,1,0:T(8,128)(2,1)S(1)} %pad_maximum_fusion), channel_id=1, source_target_pairs={{24,0},{0,8},{8,16},{16,24},{25,1},{1,9},{9,17},{17,25},{26,2},{2,... | collective-permute-start | bytes 786440 | tf_op jit(solution)/shard_map/ppermute | solution.py:20
  27.8 3.4 %collective-permute-start.1 = (bf16[2,128,512]{2,1,0:T(8,128)(2,1)S(1)}, bf16[2,128,512]{2,1,0:T(8,128)(2,1)S(1)}, u32[]{:S(2)}, u32[]{:S(2)}) collective-permute-start(bf16[2,128,512]{2,1,0:T(8,128)(2,1)S(1)} %pad_maximum_fusion), channel_id=1, source_target_pairs={{8,0},{16,8},{24,16},{0,24},{9,1},{17,9},{25,17},{1,25},{10,2},{18... | collective-permute-start | bytes 786440 | tf_op jit(solution)/shard_map/ppermute | solution.py:20
  31.2 3.4 %collective-permute-start.3 = (bf16[1,128,512]{2,1,0:T(8,128)(2,1)S(1)}, bf16[1,128,512]{2,1,0:T(8,128)(2,1)S(1)}, u32[]{:S(2)}, u32[]{:S(2)}) collective-permute-start(bf16[1,128,512]{2,1,0:T(8,128)(2,1)S(1)} %fusion.13.refs_1_), channel_id=1, source_target_pairs={{16,0},{24,8},{0,16},{8,24},{17,1},{25,9},{1,17},{9,25},{18,2},{26... | collective-permute-start | bytes 393224 | tf_op jit(solution)/shard_map/ppermute | solution.py:20
  34.6 3.3 %collective-permute-start.4 = (bf16[1,128,512]{2,1,0:T(8,128)(2,1)S(1)}, bf16[1,128,512]{2,1,0:T(8,128)(2,1)S(1)}, u32[]{:S(2)}, u32[]{:S(2)}) collective-permute-start(bf16[1,128,512]{2,1,0:T(8,128)(2,1)S(1)} %collective-permute-done.refs_2_), channel_id=1, source_target_pairs={{16,0},{24,8},{0,16},{8,24},{17,1},{25,9},{1,17},{9,25},{18,2},{26... | collective-permute-start | bytes 393224 | tf_op jit(solution)/shard_map/ppermute | solution.py:20
  38.5 0.7 reduce.3
  39.3 0.7 copy.10
  40.0 2.9 %collective-permute-done.4.refs_6_ = bf16[1,128,512]{2,1,0:T(8,128)(2,1)S(1)} collective-permute-done((bf16[1,128,512]{2,1,0:T(8,128)(2,1)S(1)}, bf16[1,128,512]{2,1,0:T(8,128)(2,1)S(1)}, u32[]{:S(2)}, u32[]{:S(2)}) %collective-permute-start.4) | collective-permute-done | bytes 131104 | tf_op jit(solution)/shard_map/ppermute | solution.py:20
  44.0 11.3 %tile.1 = (bf16[8,2,64,512]{3,2,1,0:T(8,128)(2,1)}, bf16[8,520,128]{2,1,0:T(8,128)(2,1)}) custom-call(bf16[8,2,64,512]{3,2,1,0:T(8,128)(2,1)} %copy-done, bf16[1,128,512]{2,1,0:T(8,128)(2,1)} %copy-done.1, bf16[1,128,512]{2,1,0:T(8,128)(2,1)} %copy-done.5, bf16[2,128,512]{2,1,0:T(8,128)(2,1)} %copy-done.10, bf16[2,128,512]{2,1,0:T(8,128)(2,1)} %copy-done.9, ...), custom_call_target="tpu_custom_call" | custom-call | tf_op jit(solution)/shard_map/tile/pallas_call | solution.py:213
  55.3 22.6 %all_to_all.20.got_ref = bf16[8,520,128]{2,1,0:T(8,128)(2,1)} all-to-all(bf16[8,520,128]{2,1,0:T(8,128)(2,1)} %get-tuple-element.10), channel_id=1, replica_groups=mesh['yl'=4,'co'=2,'yh'=2,'x'=4,'z'=8] {'co','x'}, dimensions={0} | all-to-all | bytes 2129920 | tf_op jit(solution)/shard_map/all_to_all | solution.py:237
  77.9 2.1 %first_sum.1 = bf16[16,40,128]{2,1,0:T(8,128)(2,1)} custom-call(bf16[8,520,128]{2,1,0:T(8,128)(2,1)} %all_to_all.20.got_ref), custom_call_target="tpu_custom_call" | custom-call | tf_op jit(solution)/shard_map/first_sum/pallas_call | solution.py:238
  80.0 14.7 %all-to-all-start.2 = ((bf16[16,40,128]{2,1,0:T(8,128)(2,1)}), bf16[16,40,128]{2,1,0:T(8,128)(2,1)S(1)}, u32[]{:S(2)}, u32[]{:S(2)}) async-start(bf16[16,40,128]{2,1,0:T(8,128)(2,1)} %first_sum.1), calls=%async_computation.2 | async-start | bytes 327680 | tf_op jit(solution)/shard_map/all_to_all | solution.py:245
  94.8 3.3 %collective-permute-start.5 = (bf16[2,64,512]{2,1,0:T(8,128)(2,1)S(1)}, bf16[2,64,512]{2,1,0:T(8,128)(2,1)S(1)}, u32[]{:S(2)}, u32[]{:S(2)}) collective-permute-start(bf16[2,64,512]{2,1,0:T(8,128)(2,1)S(1)} %get-tuple-element.14), channel_id=1, source_target_pairs={{7,0},{0,1},{1,2},{2,3},{3,4},{4,5},{5,6},{6,7},{15,8},{8,9},{9,10... | collective-permute-start | bytes 393224 | tf_op jit(solution)/shard_map/ppermute | solution.py:20
  98.1 3.2 %collective-permute-start.11 = (bf16[2,64,512]{2,1,0:T(8,128)(2,1)S(1)}, bf16[2,64,512]{2,1,0:T(8,128)(2,1)S(1)}, u32[]{:S(2)}, u32[]{:S(2)}) collective-permute-start(bf16[2,64,512]{2,1,0:T(8,128)(2,1)S(1)} %get-tuple-element.15), channel_id=1, source_target_pairs={{1,0},{2,1},{3,2},{4,3},{5,4},{6,5},{7,6},{0,7},{9,8},{10,9},{11,1... | collective-permute-start | bytes 393224 | tf_op jit(solution)/shard_map/ppermute | solution.py:20
  101.3 4.2 %collective-permute-start.10 = (bf16[2,64,512]{2,1,0:T(8,128)(2,1)S(1)}, bf16[2,64,512]{2,1,0:T(8,128)(2,1)S(1)}, u32[]{:S(2)}, u32[]{:S(2)}) collective-permute-start(bf16[2,64,512]{2,1,0:T(8,128)(2,1)S(1)} %get-tuple-element.16), channel_id=1, source_target_pairs={{2,0},{3,1},{4,2},{5,3},{6,4},{7,5},{0,6},{1,7},{10,8},{11,9},{12,... | collective-permute-start | bytes 393224 | tf_op jit(solution)/shard_map/ppermute | solution.py:20
  105.5 4.9 %collective-permute-start.9 = (bf16[2,64,512]{2,1,0:T(8,128)(2,1)S(1)}, bf16[2,64,512]{2,1,0:T(8,128)(2,1)S(1)}, u32[]{:S(2)}, u32[]{:S(2)}) collective-permute-start(bf16[2,64,512]{2,1,0:T(8,128)(2,1)S(1)} %get-tuple-element.17), channel_id=1, source_target_pairs={{3,0},{4,1},{5,2},{6,3},{7,4},{0,5},{1,6},{2,7},{11,8},{12,9},{13,... | collective-permute-start | bytes 393224 | tf_op jit(solution)/shard_map/ppermute | solution.py:20
  110.4 3.4 %collective-permute-start.8 = (bf16[2,64,512]{2,1,0:T(8,128)(2,1)S(1)}, bf16[2,64,512]{2,1,0:T(8,128)(2,1)S(1)}, u32[]{:S(2)}, u32[]{:S(2)}) collective-permute-start(bf16[2,64,512]{2,1,0:T(8,128)(2,1)S(1)} %get-tuple-element.18), channel_id=1, source_target_pairs={{4,0},{5,1},{6,2},{7,3},{0,4},{1,5},{2,6},{3,7},{12,8},{13,9},{14,... | collective-permute-start | bytes 393224 | tf_op jit(solution)/shard_map/ppermute | solution.py:20
  113.8 3.7 %collective-permute-start.7 = (bf16[2,64,512]{2,1,0:T(8,128)(2,1)S(1)}, bf16[2,64,512]{2,1,0:T(8,128)(2,1)S(1)}, u32[]{:S(2)}, u32[]{:S(2)}) collective-permute-start(bf16[2,64,512]{2,1,0:T(8,128)(2,1)S(1)} %get-tuple-element.19), channel_id=1, source_target_pairs={{5,0},{6,1},{7,2},{0,3},{1,4},{2,5},{3,6},{4,7},{13,8},{14,9},{15,... | collective-permute-start | bytes 393224 | tf_op jit(solution)/shard_map/ppermute | solution.py:20
  117.5 5.5 %collective-permute-start.6 = (bf16[2,64,512]{2,1,0:T(8,128)(2,1)S(1)}, bf16[2,64,512]{2,1,0:T(8,128)(2,1)S(1)}, u32[]{:S(2)}, u32[]{:S(2)}) collective-permute-start(bf16[2,64,512]{2,1,0:T(8,128)(2,1)S(1)} %get-tuple-element.20), channel_id=1, source_target_pairs={{6,0},{7,1},{0,2},{1,3},{2,4},{3,5},{4,6},{5,7},{14,8},{15,9},{8,1... | collective-permute-start | bytes 393224 | tf_op jit(solution)/shard_map/ppermute | solution.py:20
  123.0 0.7 copy-done.3
  123.7 1.6 %second_sum.1 = f32[8,40,128]{2,1,0:T(8,128)} custom-call(bf16[16,40,128]{2,1,0:T(8,128)(2,1)} %copy-done.3), custom_call_target="tpu_custom_call" | custom-call | tf_op jit(solution)/shard_map/second_sum/pallas_call | solution.py:246
  125.3 6.2 %all-to-all-start.3 = ((f32[8,40,128]{2,1,0:T(8,128)}), f32[8,40,128]{2,1,0:T(8,128)S(1)}, u32[]{:S(2)}, u32[]{:S(2)}) async-start(f32[8,40,128]{2,1,0:T(8,128)} %second_sum.1), calls=%async_computation.3 | async-start | bytes 327680 | tf_op jit(solution)/shard_map/all_to_all | solution.py:253
  131.5 0.8 collective-permute-done.7
  132.3 2.9 %collective-permute-done.6 = bf16[2,64,512]{2,1,0:T(8,128)(2,1)S(1)} collective-permute-done((bf16[2,64,512]{2,1,0:T(8,128)(2,1)S(1)}, bf16[2,64,512]{2,1,0:T(8,128)(2,1)S(1)}, u32[]{:S(2)}, u32[]{:S(2)}) %collective-permute-start.6) | collective-permute-done | bytes 131104 | tf_op jit(solution)/shard_map/ppermute | solution.py:20
  135.2 0.8 fusion.10
  136.0 1.6 %all-to-all-done.3.got_ref = f32[8,40,128]{2,1,0:T(8,128)S(1)} async-done(((f32[8,40,128]{2,1,0:T(8,128)}), f32[8,40,128]{2,1,0:T(8,128)S(1)}, u32[]{:S(2)}, u32[]{:S(2)}) %all-to-all-start.3) | async-done | bytes 163872 | tf_op jit(solution)/shard_map/all_to_all | solution.py:253
  137.6 0.7 copy-done.4
  138.2 1.5 %third_sum.1 = (f32[8,512]{1,0:T(8,128)}, f32[8,512]{1,0:T(8,128)}, f32[1,128]{1,0:T(1,128)}) custom-call(f32[8,40,128]{2,1,0:T(8,128)} %copy-done.4), custom_call_target="tpu_custom_call" | custom-call | tf_op jit(solution)/shard_map/third_sum/pallas_call | solution.py:254
  139.8 1.1 slice_bitcast_fusion.7
  (47 shorter events, 2.5 us)
Async XLA Ops:
  2.6 11.0 %copy-start.6 = (bf16[512,512]{1,0:T(8,128)(2,1)S(1)}, bf16[512,512]{1,0:T(8,128)(2,1)}, u32[]{:S(2)}) copy-start(bf16[512,512]{1,0:T(8,128)(2,1)} %refs_8_.1) | copy-start | bytes 1572868
  2.6 11.0 %copy-start.7 = (bf16[512,512]{1,0:T(8,128)(2,1)S(1)}, bf16[512,512]{1,0:T(8,128)(2,1)}, u32[]{:S(2)}) copy-start(bf16[512,512]{1,0:T(8,128)(2,1)} %refs_7_.1) | copy-start | bytes 1572868
  2.6 11.0 %copy-start.11 = (bf16[1,2,64,512]{3,2,1,0:T(8,128)(2,1)S(1)}, bf16[1,2,64,512]{3,2,1,0:T(8,128)(2,1)}, u32[]{:S(2)}) copy-start(bf16[1,2,64,512]{3,2,1,0:T(8,128)(2,1)} %param.5) | copy-start | bytes 393220
  2.6 11.0 %copy-start.15 = (f32[512]{0:T(512)S(1)}, f32[512]{0:T(512)}, u32[]{:S(2)}) copy-start(f32[512]{0:T(512)} %param.8) | copy-start | bytes 6148
  2.6 40.2 %all-to-all-start = ((bf16[8,2,64,512]{3,2,1,0:T(8,128)(2,1)}), bf16[8,2,64,512]{3,2,1,0:T(8,128)(2,1)S(1)}, u32[]{:S(2)}, u32[]{:S(2)}) async-start(bf16[8,2,64,512]{3,2,1,0:T(8,128)(2,1)} %broadcast_in_dim.22), calls=%async_computation | async-start | bytes 2097152 | tf_op jit(solution)/shard_map/all_to_all | solution.py:192
  13.7 24.8 %copy-start.14 = (s32[1,4096]{1,0:T(1,128)S(1)}, s32[1,4096]{1,0:T(1,128)}, u32[]{:S(2)}) copy-start(s32[1,4096]{1,0:T(1,128)} %param.6) | copy-start | bytes 49156
  14.4 28.5 %copy-start.1 = (bf16[1,128,512]{2,1,0:T(8,128)(2,1)}, bf16[1,128,512]{2,1,0:T(8,128)(2,1)S(1)}, u32[]{:S(2)}) copy-start(bf16[1,128,512]{2,1,0:T(8,128)(2,1)S(1)} %fusion.13.refs_1_) | copy-start | bytes 393220
  14.4 10.3 %collective-permute-start = (bf16[1,128,512]{2,1,0:T(8,128)(2,1)S(1)}, bf16[1,128,512]{2,1,0:T(8,128)(2,1)S(1)}, u32[]{:S(2)}, u32[]{:S(2)}) collective-permute-start(bf16[1,128,512]{2,1,0:T(8,128)(2,1)S(1)} %fusion.13.refs_1_), channel_id=1, source_target_pairs={{32,0},{0,32},{33,1},{1,33},{34,2},{2,34},{35,3},{3,35},{36,4},{4,... | collective-permute-start | bytes 393224 | tf_op jit(solution)/shard_map/ppermute | solution.py:20
  24.6 18.3 %copy-start.5 = (bf16[1,128,512]{2,1,0:T(8,128)(2,1)}, bf16[1,128,512]{2,1,0:T(8,128)(2,1)S(1)}, u32[]{:S(2)}) copy-start(bf16[1,128,512]{2,1,0:T(8,128)(2,1)S(1)} %collective-permute-done.refs_2_) | copy-start | bytes 393220
  24.7 18.2 %collective-permute-start.2 = (bf16[2,128,512]{2,1,0:T(8,128)(2,1)S(1)}, bf16[2,128,512]{2,1,0:T(8,128)(2,1)S(1)}, u32[]{:S(2)}, u32[]{:S(2)}) collective-permute-start(bf16[2,128,512]{2,1,0:T(8,128)(2,1)S(1)} %pad_maximum_fusion), channel_id=1, source_target_pairs={{24,0},{0,8},{8,16},{16,24},{25,1},{1,9},{9,17},{17,25},{26,2},{2,... | collective-permute-start | bytes 786440 | tf_op jit(solution)/shard_map/ppermute | solution.py:20
  27.8 15.1 %collective-permute-start.1 = (bf16[2,128,512]{2,1,0:T(8,128)(2,1)S(1)}, bf16[2,128,512]{2,1,0:T(8,128)(2,1)S(1)}, u32[]{:S(2)}, u32[]{:S(2)}) collective-permute-start(bf16[2,128,512]{2,1,0:T(8,128)(2,1)S(1)} %pad_maximum_fusion), channel_id=1, source_target_pairs={{8,0},{16,8},{24,16},{0,24},{9,1},{17,9},{25,17},{1,25},{10,2},{18... | collective-permute-start | bytes 786440 | tf_op jit(solution)/shard_map/ppermute | solution.py:20
  31.2 8.8 %collective-permute-start.3 = (bf16[1,128,512]{2,1,0:T(8,128)(2,1)S(1)}, bf16[1,128,512]{2,1,0:T(8,128)(2,1)S(1)}, u32[]{:S(2)}, u32[]{:S(2)}) collective-permute-start(bf16[1,128,512]{2,1,0:T(8,128)(2,1)S(1)} %fusion.13.refs_1_), channel_id=1, source_target_pairs={{16,0},{24,8},{0,16},{8,24},{17,1},{25,9},{1,17},{9,25},{18,2},{26... | collective-permute-start | bytes 393224 | tf_op jit(solution)/shard_map/ppermute | solution.py:20
  34.6 8.2 %collective-permute-start.4 = (bf16[1,128,512]{2,1,0:T(8,128)(2,1)S(1)}, bf16[1,128,512]{2,1,0:T(8,128)(2,1)S(1)}, u32[]{:S(2)}, u32[]{:S(2)}) collective-permute-start(bf16[1,128,512]{2,1,0:T(8,128)(2,1)S(1)} %collective-permute-done.refs_2_), channel_id=1, source_target_pairs={{16,0},{24,8},{0,16},{8,24},{17,1},{25,9},{1,17},{9,25},{18,2},{26... | collective-permute-start | bytes 393224 | tf_op jit(solution)/shard_map/ppermute | solution.py:20
  39.3 3.6 %copy-start.8 = (s32[64,64]{1,0:T(8,128)}, s32[64,64]{1,0:T(8,128)S(1)}, u32[]{:S(2)}) copy-start(s32[64,64]{1,0:T(8,128)S(1)} %reshape_squeeze.7.refs_10_) | copy-start | bytes 49156
  40.0 3.0 %copy-start.12 = (bf16[1,128,512]{2,1,0:T(8,128)(2,1)}, bf16[1,128,512]{2,1,0:T(8,128)(2,1)S(1)}, u32[]{:S(2)}) copy-start(bf16[1,128,512]{2,1,0:T(8,128)(2,1)S(1)} %collective-permute-done.3.refs_5_) | copy-start | bytes 393220
  42.9 0.7 copy-start.13
  42.9 0.8 copy-start.9
  42.9 0.9 copy-start.10
  42.9 1.1 copy-start
  77.9 16.8 %copy-start.2 = (bf16[8,2,64,512]{3,2,1,0:T(8,128)(2,1)S(1)}, bf16[8,2,64,512]{3,2,1,0:T(8,128)(2,1)}, u32[]{:S(2)}) copy-start(bf16[8,2,64,512]{3,2,1,0:T(8,128)(2,1)} %get-tuple-element.9) | copy-start | bytes 3145732
  80.0 43.0 %all-to-all-start.2 = ((bf16[16,40,128]{2,1,0:T(8,128)(2,1)}), bf16[16,40,128]{2,1,0:T(8,128)(2,1)S(1)}, u32[]{:S(2)}, u32[]{:S(2)}) async-start(bf16[16,40,128]{2,1,0:T(8,128)(2,1)} %first_sum.1), calls=%async_computation.2 | async-start | bytes 327680 | tf_op jit(solution)/shard_map/all_to_all | solution.py:245
  94.8 19.0 %collective-permute-start.5 = (bf16[2,64,512]{2,1,0:T(8,128)(2,1)S(1)}, bf16[2,64,512]{2,1,0:T(8,128)(2,1)S(1)}, u32[]{:S(2)}, u32[]{:S(2)}) collective-permute-start(bf16[2,64,512]{2,1,0:T(8,128)(2,1)S(1)} %get-tuple-element.14), channel_id=1, source_target_pairs={{7,0},{0,1},{1,2},{2,3},{3,4},{4,5},{5,6},{6,7},{15,8},{8,9},{9,10... | collective-permute-start | bytes 393224 | tf_op jit(solution)/shard_map/ppermute | solution.py:20
  98.1 19.5 %collective-permute-start.11 = (bf16[2,64,512]{2,1,0:T(8,128)(2,1)S(1)}, bf16[2,64,512]{2,1,0:T(8,128)(2,1)S(1)}, u32[]{:S(2)}, u32[]{:S(2)}) collective-permute-start(bf16[2,64,512]{2,1,0:T(8,128)(2,1)S(1)} %get-tuple-element.15), channel_id=1, source_target_pairs={{1,0},{2,1},{3,2},{4,3},{5,4},{6,5},{7,6},{0,7},{9,8},{10,9},{11,1... | collective-permute-start | bytes 393224 | tf_op jit(solution)/shard_map/ppermute | solution.py:20
  101.3 30.2 %collective-permute-start.10 = (bf16[2,64,512]{2,1,0:T(8,128)(2,1)S(1)}, bf16[2,64,512]{2,1,0:T(8,128)(2,1)S(1)}, u32[]{:S(2)}, u32[]{:S(2)}) collective-permute-start(bf16[2,64,512]{2,1,0:T(8,128)(2,1)S(1)} %get-tuple-element.16), channel_id=1, source_target_pairs={{2,0},{3,1},{4,2},{5,3},{6,4},{7,5},{0,6},{1,7},{10,8},{11,9},{12,... | collective-permute-start | bytes 393224 | tf_op jit(solution)/shard_map/ppermute | solution.py:20
  105.5 26.0 %collective-permute-start.9 = (bf16[2,64,512]{2,1,0:T(8,128)(2,1)S(1)}, bf16[2,64,512]{2,1,0:T(8,128)(2,1)S(1)}, u32[]{:S(2)}, u32[]{:S(2)}) collective-permute-start(bf16[2,64,512]{2,1,0:T(8,128)(2,1)S(1)} %get-tuple-element.17), channel_id=1, source_target_pairs={{3,0},{4,1},{5,2},{6,3},{7,4},{0,5},{1,6},{2,7},{11,8},{12,9},{13,... | collective-permute-start | bytes 393224 | tf_op jit(solution)/shard_map/ppermute | solution.py:20
  110.4 21.1 %collective-permute-start.8 = (bf16[2,64,512]{2,1,0:T(8,128)(2,1)S(1)}, bf16[2,64,512]{2,1,0:T(8,128)(2,1)S(1)}, u32[]{:S(2)}, u32[]{:S(2)}) collective-permute-start(bf16[2,64,512]{2,1,0:T(8,128)(2,1)S(1)} %get-tuple-element.18), channel_id=1, source_target_pairs={{4,0},{5,1},{6,2},{7,3},{0,4},{1,5},{2,6},{3,7},{12,8},{13,9},{14,... | collective-permute-start | bytes 393224 | tf_op jit(solution)/shard_map/ppermute | solution.py:20
  113.8 18.5 %collective-permute-start.7 = (bf16[2,64,512]{2,1,0:T(8,128)(2,1)S(1)}, bf16[2,64,512]{2,1,0:T(8,128)(2,1)S(1)}, u32[]{:S(2)}, u32[]{:S(2)}) collective-permute-start(bf16[2,64,512]{2,1,0:T(8,128)(2,1)S(1)} %get-tuple-element.19), channel_id=1, source_target_pairs={{5,0},{6,1},{7,2},{0,3},{1,4},{2,5},{3,6},{4,7},{13,8},{14,9},{15,... | collective-permute-start | bytes 393224 | tf_op jit(solution)/shard_map/ppermute | solution.py:20
  117.5 17.7 %collective-permute-start.6 = (bf16[2,64,512]{2,1,0:T(8,128)(2,1)S(1)}, bf16[2,64,512]{2,1,0:T(8,128)(2,1)S(1)}, u32[]{:S(2)}, u32[]{:S(2)}) collective-permute-start(bf16[2,64,512]{2,1,0:T(8,128)(2,1)S(1)} %get-tuple-element.20), channel_id=1, source_target_pairs={{6,0},{7,1},{0,2},{1,3},{2,4},{3,5},{4,6},{5,7},{14,8},{15,9},{8,1... | collective-permute-start | bytes 393224 | tf_op jit(solution)/shard_map/ppermute | solution.py:20
  123.0 0.7 copy-start.3
  125.3 12.3 %all-to-all-start.3 = ((f32[8,40,128]{2,1,0:T(8,128)}), f32[8,40,128]{2,1,0:T(8,128)S(1)}, u32[]{:S(2)}, u32[]{:S(2)}) async-start(f32[8,40,128]{2,1,0:T(8,128)} %second_sum.1), calls=%async_computation.3 | async-start | bytes 327680 | tf_op jit(solution)/shard_map/all_to_all | solution.py:253
  137.6 0.7 copy-start.4

commit v3 on v2

--- a/solution.py
+++ b/solution.py
@@ -13,11 +13,18 @@
 temper = 0.2
 epsilon = 1e-06
 LANES = 128
+RETURN_ORDER = (0, 3, 7, 4, 1, 6, 2, 5)
 
 
 def shifted(value, axis, by):
     count = lax.axis_size(axis)
     return lax.ppermute(value, axis, [((i + by) % count, i) for i in range(count)])
+
+
+def swapped(value, axis, step_by):
+    count = lax.axis_size(axis)
+    pairs = [(i, (i + step_by * (1 - 2 * (i % 2))) % count) for i in range(count)]
+    return lax.ppermute(value, axis, pairs)
 
 
 def dot_nn(a, b):
@@ -37,7 +44,7 @@
     rows_ref = refs[0]
     col_refs = refs[1 : 1 + groups]
     w_one_ref, w_two_ref, b_one_ref, pos_ref, pos_t_ref = refs[1 + groups : 6 + groups]
-    feats_out, weights_out, cols_s, hid_s, gp_s, pre_s, cpos_s = refs[6 + groups :]
+    kept_out, sent_out, weights_out, x_s, cols_s, hid_s, gp_s, pre_s, cpos_s = refs[6 + groups :]
     my_z, my_x, my_y = lax.axis_index("z"), lax.axis_index("x"), lax.axis_index("yh")
     my_yx = my_y * nx + my_x
     count = len(order)
@@ -60,9 +67,13 @@
     chunk = per * half
     bias = jnp.zeros((1, width), jnp.float32)
     block_lane = lax.broadcasted_iota(jnp.int32, pos_t_ref.shape, 1)
+    turn = 1 - 2 * lax.rem(my_z, 2)
+    held = [lax.rem(my_z + turn * d + nz, nz) for d in RETURN_ORDER]
+    half_iota = lax.broadcasted_iota(jnp.int32, (half, 1), 0)
     for v in range(2):
         for k in range(nz // per):
-            x = rows_ref[k * per : (k + 1) * per, v].reshape(chunk, width)
+            blocks = held[k * per : (k + 1) * per]
+            x = jnp.concatenate([rows_ref[b, v] for b in blocks], axis=0)
             stack_at = slice((v * nz * half) + k * chunk, (v * nz * half) + (k + 1) * chunk)
             pre = dot_nn(x, w_one) + b_one_ref[...]
             grow = jnp.exp(jnp.minimum(pre, 0.0))
@@ -73,17 +84,16 @@
             radius = jnp.sqrt(jnp.sum(projected * projected, axis=1, keepdims=True) + epsilon)
             unit = projected / radius
             sent = unit.astype(jnp.bfloat16)
-            first_row = (my_yx * nz + k * per) * half
-            rid = first_row + lax.broadcasted_iota(jnp.int32, (chunk, 1), 0)
+            rid = jnp.concatenate([(my_yx * nz + b) * half + half_iota for b in blocks], axis=0)
             if v == 0:
                 rpos = jnp.concatenate(
                     [
                         jnp.sum(
-                            jnp.where(block_lane == my_yx * nz + k * per + j, pos_t_ref[...], 0),
+                            jnp.where(block_lane == my_yx * nz + b, pos_t_ref[...], 0),
                             axis=1,
                             keepdims=True,
                         )
-                        for j in range(per)
+                        for b in blocks
                     ],
                     axis=0,
                 )
@@ -107,17 +117,15 @@
             grad_pre = (dot_nt(grad_proj, w_two) * slope).astype(jnp.bfloat16)
             grad_rows = dot_nt(grad_pre, w_one).astype(jnp.bfloat16)
             bias = bias + jnp.sum(grad_pre.astype(jnp.float32), axis=0, keepdims=True)
+            x_s[stack_at, :] = x
             hid_s[stack_at, :] = hidden
             gp_s[stack_at, :] = grad_proj
             pre_s[stack_at, :] = grad_pre
             for j in range(per):
-                block = k * per + j
-                feats_out[lax.rem(block + nz - my_z, nz), v] = grad_rows[j * half : (j + 1) * half]
-    rows_all = jnp.concatenate(
-        [rows_ref[:, v].reshape(nz * half, width) for v in range(2)], axis=0
-    )
+                place = (kept_out, sent_out)[(k * per + j) * 2 // nz]
+                place[(k * per + j) % (nz // 2), v] = grad_rows[j * half : (j + 1) * half]
     parts = (
-        dot_tn(rows_all, pre_s[...]).astype(jnp.bfloat16),
+        dot_tn(x_s[...], pre_s[...]).astype(jnp.bfloat16),
         dot_tn(hid_s[...], gp_s[...]).astype(jnp.bfloat16),
     )
     per_x = width // (ny * nx)
@@ -139,8 +147,8 @@
                 source = (y * nx + x) * per_x
                 low = source // LANES * LANES
                 part = jnp.broadcast_to(bias[:, low : low + LANES], (8, LANES))
-                turn = (y * per_x - source) % LANES
-                picked.append(pltpu.roll(part, turn, 1) if turn else part)
+                by = (y * per_x - source) % LANES
+                picked.append(pltpu.roll(part, by, 1) if by else part)
             row = jnp.where(tile_lane < per_x, picked[0], picked[1])
             weights_out[piece, tiles * rows_x :, :] = row.astype(jnp.bfloat16)
 
@@ -210,17 +218,19 @@
 
     vmem = pl.BlockSpec(memory_space=pltpu.VMEM)
     piece_rows = width // nx // 2 * 2 * (width // LANES) + 8
-    shares, weights = pl.pallas_call(
+    kept, sent_back, weights = pl.pallas_call(
         lambda *refs: tile_kernel(
             *refs, nz=nz, nx=nx, ny=ny, half=half, width=width, negatives=negatives, order=order
         ),
         in_specs=[vmem] * (len(cols) + 6),
-        out_specs=[vmem, vmem],
+        out_specs=[vmem, vmem, vmem],
         out_shape=[
-            jax.ShapeDtypeStruct((nz, 2, half, width), jnp.bfloat16),
+            jax.ShapeDtypeStruct((nz // 2, 2, half, width), jnp.bfloat16),
+            jax.ShapeDtypeStruct((nz // 2, 2, half, width), jnp.bfloat16),
             jax.ShapeDtypeStruct((2 * nx, piece_rows, LANES), jnp.bfloat16),
         ],
         scratch_shapes=[
+            pltpu.VMEM((2 * nz * half, width), jnp.bfloat16),
             pltpu.VMEM((2, len(order) * half, width), jnp.bfloat16),
             pltpu.VMEM((2 * nz * half, width), jnp.bfloat16),
             pltpu.VMEM((2 * nz * half, width), jnp.bfloat16),
@@ -270,13 +280,15 @@
     )(got)
     share_bias = share_bias[0, :per_block]
 
-    pieces = [shares[0]]
-    for d in range(1, nz):
-        pieces.append(shifted(shares[d], "z", -d))
-    grad = pieces[0].astype(jnp.float32)
-    for piece in pieces[1:]:
-        grad = grad + piece.astype(jnp.float32)
-    grad_feats = grad.astype(jnp.bfloat16)[None]
+    grad = kept
+    moved = sent_back
+    for i, step_by in enumerate((1, -1, 3)):
+        moved = swapped(moved, "z", step_by)
+        grad = grad.astype(jnp.float32) + moved.astype(jnp.float32)
+        if i < 2:
+            moved = grad[grad.shape[0] // 2 :].astype(jnp.bfloat16)
+            grad = grad[: grad.shape[0] // 2]
+    grad_feats = grad.astype(jnp.bfloat16)
     return (grad_feats, share_one, share_bias, share_two)
 
 

time: 142 us -> 127 us (0.89)
  blocking collectives: 22.6 us -> 0 us
  waiting for transfers between devices: 11 us -> 29.1 us
  starting transfers between devices: 80.8 us -> 69 us
    ppermute x12 -> x5, starting transfers between devices: 48.9 us -> 20.7 us  [shifted(): lax.ppermute(value, axis, [((i + by) % count, i) for i in range(count)])]
    all_to_all x1 -> x0, blocking collectives: 22.6 us -> none  [step(): got = lax.all_to_all(weights, ('co', 'x'), 0, 0, tiled=True)]
    ppermute x0 -> x3, starting transfers between devices: none -> 11.6 us  [swapped(): return lax.ppermute(value, axis, pairs)]
    all_to_all x0 -> x1, waiting for transfers between devices: none -> 10.6 us  [step(): got = lax.all_to_all(weights, ('co', 'x'), 0, 0, tiled=True)]
    all_to_all x0 -> x1, starting transfers between devices: none -> 9.9 us  [step(): got = lax.all_to_all(weights, ('co', 'x'), 0, 0, tiled=True)]
    all_to_all x1, waiting for transfers between devices: 0.01 us -> 7.34 us  [step(): got = lax.all_to_all(got, ('yh', 'z'), 0, 0, tiled=True)]
    all_to_all x1, waiting for transfers between devices: 1.55 us -> 5.4 us  [step(): got = lax.all_to_all(got, SUB, 0, 0, tiled=True)]
    ppermute x12 -> x5, waiting for transfers between devices: 9.43 us -> 5.7 us  [shifted(): lax.ppermute(value, axis, [((i + by) % count, i) for i in range(count)])]
  transfers between devices with their start and end apart: 15 -> 12, of which waited for: 5 -> 5; matrix products, arithmetic and copies ran while one was open for 2% -> 3% of each run, Pallas kernels for 1% -> 3%
where the time goes in v3:
time: 127 us; the launch traced here: 126 us
  starting transfers between devices  69 us (54%)
  waiting for transfers between devices  29.1 us (23%)
  Pallas kernels  16.5 us (13%)
  local copies, waits for them, and re-layouts  7.97 us (6%)
  other arithmetic  1.73 us (1%)
    ppermute x5, starting transfers between devices, shifted(): lax.ppermute(value, axis, [((i + by) % count, i) for i in range(count)])  20.7 us
    ppermute x3, starting transfers between devices, swapped(): return lax.ppermute(value, axis, pairs)  11.6 us
    all_to_all x1, starting transfers between devices, step(): got = lax.all_to_all(got, ('yh', 'z'), 0, 0, tiled=True)  11.4 us
    pallas_call x1, Pallas kernels, step(): pl.pallas_call(lambda *refs: tile_kernel(*refs, nz=nz, nx=nx, ny=ny, half...  11.3 us
    all_to_all x1, starting transfers between devices, step(): lax.all_to_all(jnp.broadcast_to(own[None], (nz, *own.shape)), 'z', 0, 0,...  11 us
    all_to_all x1, waiting for transfers between devices, step(): got = lax.all_to_all(weights, ('co', 'x'), 0, 0, tiled=True)  10.6 us
    all_to_all x1, starting transfers between devices, step(): got = lax.all_to_all(weights, ('co', 'x'), 0, 0, tiled=True)  9.9 us
    all_to_all x1, waiting for transfers between devices, step(): got = lax.all_to_all(got, ('yh', 'z'), 0, 0, tiled=True)  7.34 us
  transfers between devices with their start and end apart: 12, of which 5 were waited for; matrix products, arithmetic and copies ran while one was open for 3% of the time, Pallas kernels for 3%

profile of v3, /device:TPU:1, one launch (start us, length us, event | category | flops | bytes accessed | tf_op | source)
XLA Modules:
  0.0 125.8 jit_solution(17697147612980603793)
XLA Ops:
  0.6 2.0 %broadcast_in_dim.19 = bf16[8,2,64,512]{3,2,1,0:T(8,128)(2,1)} broadcast(bf16[2,64,512]{2,1,0:T(8,128)(2,1)} %bitcast.12), dimensions={1,2,3} | broadcast | bytes 1179648 | tf_op jit(solution)/shard_map/broadcast_in_dim | solution.py:200
  2.6 11.0 %all-to-all-start = ((bf16[8,2,64,512]{3,2,1,0:T(8,128)(2,1)}), bf16[8,2,64,512]{3,2,1,0:T(8,128)(2,1)S(1)}, u32[]{:S(2)}, u32[]{:S(2)}) async-start(bf16[8,2,64,512]{3,2,1,0:T(8,128)(2,1)} %broadcast_in_dim.19), calls=%async_computation | async-start | bytes 2097152 | tf_op jit(solution)/shard_map/all_to_all | solution.py:200
  13.7 0.6 multiply_reduce_fusion
  14.4 7.5 %collective-permute-start = (bf16[1,128,512]{2,1,0:T(8,128)(2,1)S(1)}, bf16[1,128,512]{2,1,0:T(8,128)(2,1)S(1)}, u32[]{:S(2)}, u32[]{:S(2)}) collective-permute-start(bf16[1,128,512]{2,1,0:T(8,128)(2,1)S(1)} %fusion.6.refs_1_), channel_id=1, source_target_pairs={{32,0},{0,32},{33,1},{1,33},{34,2},{2,34},{35,3},{3,35},{36,4},{4,... | collective-permute-start | bytes 393224 | tf_op jit(solution)/shard_map/ppermute | solution.py:21
  21.8 2.8 %collective-permute-done.refs_2_ = bf16[1,128,512]{2,1,0:T(8,128)(2,1)S(1)} collective-permute-done((bf16[1,128,512]{2,1,0:T(8,128)(2,1)S(1)}, bf16[1,128,512]{2,1,0:T(8,128)(2,1)S(1)}, u32[]{:S(2)}, u32[]{:S(2)}) %collective-permute-start) | collective-permute-done | bytes 131104 | tf_op jit(solution)/shard_map/ppermute | solution.py:21
  24.7 3.1 %collective-permute-start.2 = (bf16[2,128,512]{2,1,0:T(8,128)(2,1)S(1)}, bf16[2,128,512]{2,1,0:T(8,128)(2,1)S(1)}, u32[]{:S(2)}, u32[]{:S(2)}) collective-permute-start(bf16[2,128,512]{2,1,0:T(8,128)(2,1)S(1)} %pad_maximum_fusion), channel_id=1, source_target_pairs={{24,0},{0,8},{8,16},{16,24},{25,1},{1,9},{9,17},{17,25},{26,2},{2,... | collective-permute-start | bytes 786440 | tf_op jit(solution)/shard_map/ppermute | solution.py:21
  27.8 3.4 %collective-permute-start.1 = (bf16[2,128,512]{2,1,0:T(8,128)(2,1)S(1)}, bf16[2,128,512]{2,1,0:T(8,128)(2,1)S(1)}, u32[]{:S(2)}, u32[]{:S(2)}) collective-permute-start(bf16[2,128,512]{2,1,0:T(8,128)(2,1)S(1)} %pad_maximum_fusion), channel_id=1, source_target_pairs={{8,0},{16,8},{24,16},{0,24},{9,1},{17,9},{25,17},{1,25},{10,2},{18... | collective-permute-start | bytes 786440 | tf_op jit(solution)/shard_map/ppermute | solution.py:21
  31.2 3.4 %collective-permute-start.3 = (bf16[1,128,512]{2,1,0:T(8,128)(2,1)S(1)}, bf16[1,128,512]{2,1,0:T(8,128)(2,1)S(1)}, u32[]{:S(2)}, u32[]{:S(2)}) collective-permute-start(bf16[1,128,512]{2,1,0:T(8,128)(2,1)S(1)} %fusion.6.refs_1_), channel_id=1, source_target_pairs={{16,0},{24,8},{0,16},{8,24},{17,1},{25,9},{1,17},{9,25},{18,2},{26... | collective-permute-start | bytes 393224 | tf_op jit(solution)/shard_map/ppermute | solution.py:21
  34.6 3.3 %collective-permute-start.4 = (bf16[1,128,512]{2,1,0:T(8,128)(2,1)S(1)}, bf16[1,128,512]{2,1,0:T(8,128)(2,1)S(1)}, u32[]{:S(2)}, u32[]{:S(2)}) collective-permute-start(bf16[1,128,512]{2,1,0:T(8,128)(2,1)S(1)} %collective-permute-done.refs_2_), channel_id=1, source_target_pairs={{16,0},{24,8},{0,16},{8,24},{17,1},{25,9},{1,17},{9,25},{18,2},{26... | collective-permute-start | bytes 393224 | tf_op jit(solution)/shard_map/ppermute | solution.py:21
  38.0 0.5 broadcast.11
  38.5 0.7 reduce.3
  39.3 0.7 copy.10
  40.0 2.9 %collective-permute-done.4.refs_6_ = bf16[1,128,512]{2,1,0:T(8,128)(2,1)S(1)} collective-permute-done((bf16[1,128,512]{2,1,0:T(8,128)(2,1)S(1)}, bf16[1,128,512]{2,1,0:T(8,128)(2,1)S(1)}, u32[]{:S(2)}, u32[]{:S(2)}) %collective-permute-start.4) | collective-permute-done | bytes 131104 | tf_op jit(solution)/shard_map/ppermute | solution.py:21
  42.9 0.6 copy-done.14
  44.1 11.3 %tile.1 = (bf16[4,2,64,512]{3,2,1,0:T(8,128)(2,1)}, bf16[4,2,64,512]{3,2,1,0:T(8,128)(2,1)}, bf16[8,520,128]{2,1,0:T(8,128)(2,1)}) custom-call(bf16[8,2,64,512]{3,2,1,0:T(8,128)(2,1)} %copy-done.1, bf16[1,128,512]{2,1,0:T(8,128)(2,1)} %copy-done.2, bf16[1,128,512]{2,1,0:T(8,128)(2,1)} %copy-done.5, bf16[2,128,512]{2,1,0:T(8,128)(2,1)} %copy-done.11, ...), custom_call_target="tpu_custom_call" | custom-call | tf_op jit(solution)/shard_map/tile/pallas_call | solution.py:221
  55.3 2.2 %collective-permute-start.5 = (bf16[4,2,64,512]{3,2,1,0:T(8,128)(2,1)}, bf16[4,2,64,512]{3,2,1,0:T(8,128)(2,1)S(1)}, u32[]{:S(2)}, u32[]{:S(2)}) collective-permute-start(bf16[4,2,64,512]{3,2,1,0:T(8,128)(2,1)} %get-tuple-element.11), channel_id=1, source_target_pairs={{0,1},{1,0},{2,3},{3,2},{4,5},{5,4},{6,7},{7,6},{8,9},{9,8},{10,11... | collective-permute-start | bytes 1572872 | tf_op jit(solution)/shard_map/ppermute | solution.py:27
  57.6 9.9 %all-to-all-start.1 = ((bf16[8,520,128]{2,1,0:T(8,128)(2,1)}), bf16[8,520,128]{2,1,0:T(8,128)(2,1)S(1)}, u32[]{:S(2)}, u32[]{:S(2)}) async-start(bf16[8,520,128]{2,1,0:T(8,128)(2,1)} %get-tuple-element.12), calls=%async_computation.1 | async-start | bytes 2129920 | tf_op jit(solution)/shard_map/all_to_all | solution.py:247
  67.7 4.3 %collective-permute-start.6 = (bf16[2,2,64,512]{3,2,1,0:T(8,128)(2,1)S(1)}, bf16[2,2,64,512]{3,2,1,0:T(8,128)(2,1)S(1)}, u32[]{:S(2)}, u32[]{:S(2)}) collective-permute-start(bf16[2,2,64,512]{3,2,1,0:T(8,128)(2,1)S(1)} %slice.33), channel_id=1, source_target_pairs={{0,7},{1,2},{2,1},{3,4},{4,3},{5,6},{6,5},{7,0},{8,15},{9,10},{10,... | collective-permute-start | bytes 786440 | tf_op jit(solution)/shard_map/ppermute | solution.py:27
  72.0 10.6 %all-to-all-done.1.got_ref = bf16[8,520,128]{2,1,0:T(8,128)(2,1)S(1)} async-done(((bf16[8,520,128]{2,1,0:T(8,128)(2,1)}), bf16[8,520,128]{2,1,0:T(8,128)(2,1)S(1)}, u32[]{:S(2)}, u32[]{:S(2)}) %all-to-all-start.1) | async-done | bytes 1064992 | tf_op jit(solution)/shard_map/all_to_all | solution.py:247
  82.7 1.0 copy-done
  83.7 2.0 %first_sum.1 = bf16[16,40,128]{2,1,0:T(8,128)(2,1)} custom-call(bf16[8,520,128]{2,1,0:T(8,128)(2,1)} %copy-done), custom_call_target="tpu_custom_call" | custom-call | tf_op jit(solution)/shard_map/first_sum/pallas_call | solution.py:248
  85.7 11.4 %all-to-all-start.2 = ((bf16[16,40,128]{2,1,0:T(8,128)(2,1)}), bf16[16,40,128]{2,1,0:T(8,128)(2,1)S(1)}, u32[]{:S(2)}, u32[]{:S(2)}) async-start(bf16[16,40,128]{2,1,0:T(8,128)(2,1)} %first_sum.1), calls=%async_computation.2 | async-start | bytes 327680 | tf_op jit(solution)/shard_map/all_to_all | solution.py:255
  97.2 5.1 %collective-permute-start.7 = (bf16[1,2,64,512]{3,2,1,0:T(8,128)(2,1)S(1)}, bf16[1,2,64,512]{3,2,1,0:T(8,128)(2,1)S(1)}, u32[]{:S(2)}, u32[]{:S(2)}) collective-permute-start(bf16[1,2,64,512]{3,2,1,0:T(8,128)(2,1)S(1)} %slice.34), channel_id=1, source_target_pairs={{0,3},{1,6},{2,5},{3,0},{4,7},{5,2},{6,1},{7,4},{8,11},{9,14},{10,... | collective-permute-start | bytes 393224 | tf_op jit(solution)/shard_map/ppermute | solution.py:27
  102.3 7.3 %all-to-all-done.2.got_ref = bf16[16,40,128]{2,1,0:T(8,128)(2,1)S(1)} async-done(((bf16[16,40,128]{2,1,0:T(8,128)(2,1)}), bf16[16,40,128]{2,1,0:T(8,128)(2,1)S(1)}, u32[]{:S(2)}, u32[]{:S(2)}) %all-to-all-start.2) | async-done | bytes 163872 | tf_op jit(solution)/shard_map/all_to_all | solution.py:255
  109.6 0.7 copy-done.3
  110.3 1.6 %second_sum.1 = f32[8,40,128]{2,1,0:T(8,128)} custom-call(bf16[16,40,128]{2,1,0:T(8,128)(2,1)} %copy-done.3), custom_call_target="tpu_custom_call" | custom-call | tf_op jit(solution)/shard_map/second_sum/pallas_call | solution.py:256
  111.9 4.4 %all-to-all-start.3 = ((f32[8,40,128]{2,1,0:T(8,128)}), f32[8,40,128]{2,1,0:T(8,128)S(1)}, u32[]{:S(2)}, u32[]{:S(2)}) async-start(f32[8,40,128]{2,1,0:T(8,128)} %second_sum.1), calls=%async_computation.3 | async-start | bytes 327680 | tf_op jit(solution)/shard_map/all_to_all | solution.py:263
  116.3 0.7 fusion.3
  117.0 5.4 %all-to-all-done.3.got_ref = f32[8,40,128]{2,1,0:T(8,128)S(1)} async-done(((f32[8,40,128]{2,1,0:T(8,128)}), f32[8,40,128]{2,1,0:T(8,128)S(1)}, u32[]{:S(2)}, u32[]{:S(2)}) %all-to-all-start.3) | async-done | bytes 163872 | tf_op jit(solution)/shard_map/all_to_all | solution.py:263
  122.4 0.7 copy-done.4
  123.0 1.6 %third_sum.1 = (f32[8,512]{1,0:T(8,128)}, f32[8,512]{1,0:T(8,128)}, f32[1,128]{1,0:T(1,128)}) custom-call(f32[8,40,128]{2,1,0:T(8,128)} %copy-done.4), custom_call_target="tpu_custom_call" | custom-call | tf_op jit(solution)/shard_map/third_sum/pallas_call | solution.py:264
  124.6 1.2 slice_bitcast_fusion
  (45 shorter events, 1.1 us)
Async XLA Ops:
  2.6 11.0 %copy-start.6 = (bf16[512,512]{1,0:T(8,128)(2,1)S(1)}, bf16[512,512]{1,0:T(8,128)(2,1)}, u32[]{:S(2)}) copy-start(bf16[512,512]{1,0:T(8,128)(2,1)} %refs_8_.1) | copy-start | bytes 1572868
  2.6 11.0 %copy-start.7 = (bf16[512,512]{1,0:T(8,128)(2,1)S(1)}, bf16[512,512]{1,0:T(8,128)(2,1)}, u32[]{:S(2)}) copy-start(bf16[512,512]{1,0:T(8,128)(2,1)} %refs_7_.1) | copy-start | bytes 1572868
  2.6 11.0 %copy-start.12 = (bf16[1,2,64,512]{3,2,1,0:T(8,128)(2,1)S(1)}, bf16[1,2,64,512]{3,2,1,0:T(8,128)(2,1)}, u32[]{:S(2)}) copy-start(bf16[1,2,64,512]{3,2,1,0:T(8,128)(2,1)} %param.5) | copy-start | bytes 393220
  2.6 11.0 %copy-start.16 = (f32[512]{0:T(512)S(1)}, f32[512]{0:T(512)}, u32[]{:S(2)}) copy-start(f32[512]{0:T(512)} %param.8) | copy-start | bytes 6148
  2.6 40.3 %all-to-all-start = ((bf16[8,2,64,512]{3,2,1,0:T(8,128)(2,1)}), bf16[8,2,64,512]{3,2,1,0:T(8,128)(2,1)S(1)}, u32[]{:S(2)}, u32[]{:S(2)}) async-start(bf16[8,2,64,512]{3,2,1,0:T(8,128)(2,1)} %broadcast_in_dim.19), calls=%async_computation | async-start | bytes 2097152 | tf_op jit(solution)/shard_map/all_to_all | solution.py:200
  13.7 24.8 %copy-start.15 = (s32[1,4096]{1,0:T(1,128)S(1)}, s32[1,4096]{1,0:T(1,128)}, u32[]{:S(2)}) copy-start(s32[1,4096]{1,0:T(1,128)} %param.6) | copy-start | bytes 49156
  14.4 28.5 %copy-start.2 = (bf16[1,128,512]{2,1,0:T(8,128)(2,1)}, bf16[1,128,512]{2,1,0:T(8,128)(2,1)S(1)}, u32[]{:S(2)}) copy-start(bf16[1,128,512]{2,1,0:T(8,128)(2,1)S(1)} %fusion.6.refs_1_) | copy-start | bytes 393220
  14.4 10.3 %collective-permute-start = (bf16[1,128,512]{2,1,0:T(8,128)(2,1)S(1)}, bf16[1,128,512]{2,1,0:T(8,128)(2,1)S(1)}, u32[]{:S(2)}, u32[]{:S(2)}) collective-permute-start(bf16[1,128,512]{2,1,0:T(8,128)(2,1)S(1)} %fusion.6.refs_1_), channel_id=1, source_target_pairs={{32,0},{0,32},{33,1},{1,33},{34,2},{2,34},{35,3},{3,35},{36,4},{4,... | collective-permute-start | bytes 393224 | tf_op jit(solution)/shard_map/ppermute | solution.py:21
  24.7 18.3 %copy-start.5 = (bf16[1,128,512]{2,1,0:T(8,128)(2,1)}, bf16[1,128,512]{2,1,0:T(8,128)(2,1)S(1)}, u32[]{:S(2)}) copy-start(bf16[1,128,512]{2,1,0:T(8,128)(2,1)S(1)} %collective-permute-done.refs_2_) | copy-start | bytes 393220
  24.7 18.2 %collective-permute-start.2 = (bf16[2,128,512]{2,1,0:T(8,128)(2,1)S(1)}, bf16[2,128,512]{2,1,0:T(8,128)(2,1)S(1)}, u32[]{:S(2)}, u32[]{:S(2)}) collective-permute-start(bf16[2,128,512]{2,1,0:T(8,128)(2,1)S(1)} %pad_maximum_fusion), channel_id=1, source_target_pairs={{24,0},{0,8},{8,16},{16,24},{25,1},{1,9},{9,17},{17,25},{26,2},{2,... | collective-permute-start | bytes 786440 | tf_op jit(solution)/shard_map/ppermute | solution.py:21
  27.8 15.1 %collective-permute-start.1 = (bf16[2,128,512]{2,1,0:T(8,128)(2,1)S(1)}, bf16[2,128,512]{2,1,0:T(8,128)(2,1)S(1)}, u32[]{:S(2)}, u32[]{:S(2)}) collective-permute-start(bf16[2,128,512]{2,1,0:T(8,128)(2,1)S(1)} %pad_maximum_fusion), channel_id=1, source_target_pairs={{8,0},{16,8},{24,16},{0,24},{9,1},{17,9},{25,17},{1,25},{10,2},{18... | collective-permute-start | bytes 786440 | tf_op jit(solution)/shard_map/ppermute | solution.py:21
  31.2 8.8 %collective-permute-start.3 = (bf16[1,128,512]{2,1,0:T(8,128)(2,1)S(1)}, bf16[1,128,512]{2,1,0:T(8,128)(2,1)S(1)}, u32[]{:S(2)}, u32[]{:S(2)}) collective-permute-start(bf16[1,128,512]{2,1,0:T(8,128)(2,1)S(1)} %fusion.6.refs_1_), channel_id=1, source_target_pairs={{16,0},{24,8},{0,16},{8,24},{17,1},{25,9},{1,17},{9,25},{18,2},{26... | collective-permute-start | bytes 393224 | tf_op jit(solution)/shard_map/ppermute | solution.py:21
  34.6 8.2 %collective-permute-start.4 = (bf16[1,128,512]{2,1,0:T(8,128)(2,1)S(1)}, bf16[1,128,512]{2,1,0:T(8,128)(2,1)S(1)}, u32[]{:S(2)}, u32[]{:S(2)}) collective-permute-start(bf16[1,128,512]{2,1,0:T(8,128)(2,1)S(1)} %collective-permute-done.refs_2_), channel_id=1, source_target_pairs={{16,0},{24,8},{0,16},{8,24},{17,1},{25,9},{1,17},{9,25},{18,2},{26... | collective-permute-start | bytes 393224 | tf_op jit(solution)/shard_map/ppermute | solution.py:21
  39.3 3.6 %copy-start.9 = (s32[64,64]{1,0:T(8,128)}, s32[64,64]{1,0:T(8,128)S(1)}, u32[]{:S(2)}) copy-start(s32[64,64]{1,0:T(8,128)S(1)} %reshape_squeeze.7.refs_10_) | copy-start | bytes 49156
  40.0 3.0 %copy-start.13 = (bf16[1,128,512]{2,1,0:T(8,128)(2,1)}, bf16[1,128,512]{2,1,0:T(8,128)(2,1)S(1)}, u32[]{:S(2)}) copy-start(bf16[1,128,512]{2,1,0:T(8,128)(2,1)S(1)} %collective-permute-done.3.refs_5_) | copy-start | bytes 393220
  42.9 0.7 copy-start.14
  42.9 0.8 copy-start.10
  42.9 0.9 copy-start.11
  42.9 1.2 copy-start.1
  55.3 12.2 %collective-permute-start.5 = (bf16[4,2,64,512]{3,2,1,0:T(8,128)(2,1)}, bf16[4,2,64,512]{3,2,1,0:T(8,128)(2,1)S(1)}, u32[]{:S(2)}, u32[]{:S(2)}) collective-permute-start(bf16[4,2,64,512]{3,2,1,0:T(8,128)(2,1)} %get-tuple-element.11), channel_id=1, source_target_pairs={{0,1},{1,0},{2,3},{3,2},{4,5},{5,4},{6,7},{7,6},{8,9},{9,8},{10,11... | collective-permute-start | bytes 1572872 | tf_op jit(solution)/shard_map/ppermute | solution.py:27
  57.6 9.9 %copy-start.8 = (bf16[4,2,64,512]{3,2,1,0:T(8,128)(2,1)S(1)}, bf16[4,2,64,512]{3,2,1,0:T(8,128)(2,1)}, u32[]{:S(2)}) copy-start(bf16[4,2,64,512]{3,2,1,0:T(8,128)(2,1)} %get-tuple-element.10) | copy-start | bytes 1572868
  57.6 25.1 %all-to-all-start.1 = ((bf16[8,520,128]{2,1,0:T(8,128)(2,1)}), bf16[8,520,128]{2,1,0:T(8,128)(2,1)S(1)}, u32[]{:S(2)}, u32[]{:S(2)}) async-start(bf16[8,520,128]{2,1,0:T(8,128)(2,1)} %get-tuple-element.12), calls=%async_computation.1 | async-start | bytes 2129920 | tf_op jit(solution)/shard_map/all_to_all | solution.py:247
  67.7 29.4 %collective-permute-start.6 = (bf16[2,2,64,512]{3,2,1,0:T(8,128)(2,1)S(1)}, bf16[2,2,64,512]{3,2,1,0:T(8,128)(2,1)S(1)}, u32[]{:S(2)}, u32[]{:S(2)}) collective-permute-start(bf16[2,2,64,512]{3,2,1,0:T(8,128)(2,1)S(1)} %slice.33), channel_id=1, source_target_pairs={{0,7},{1,2},{2,1},{3,4},{4,3},{5,6},{6,5},{7,0},{8,15},{9,10},{10,... | collective-permute-start | bytes 786440 | tf_op jit(solution)/shard_map/ppermute | solution.py:27
  82.7 1.0 copy-start
  85.7 23.9 %all-to-all-start.2 = ((bf16[16,40,128]{2,1,0:T(8,128)(2,1)}), bf16[16,40,128]{2,1,0:T(8,128)(2,1)S(1)}, u32[]{:S(2)}, u32[]{:S(2)}) async-start(bf16[16,40,128]{2,1,0:T(8,128)(2,1)} %first_sum.1), calls=%async_computation.2 | async-start | bytes 327680 | tf_op jit(solution)/shard_map/all_to_all | solution.py:255
  97.2 19.1 %collective-permute-start.7 = (bf16[1,2,64,512]{3,2,1,0:T(8,128)(2,1)S(1)}, bf16[1,2,64,512]{3,2,1,0:T(8,128)(2,1)S(1)}, u32[]{:S(2)}, u32[]{:S(2)}) collective-permute-start(bf16[1,2,64,512]{3,2,1,0:T(8,128)(2,1)S(1)} %slice.34), channel_id=1, source_target_pairs={{0,3},{1,6},{2,5},{3,0},{4,7},{5,2},{6,1},{7,4},{8,11},{9,14},{10,... | collective-permute-start | bytes 393224 | tf_op jit(solution)/shard_map/ppermute | solution.py:27
  109.6 0.7 copy-start.3
  111.9 10.5 %all-to-all-start.3 = ((f32[8,40,128]{2,1,0:T(8,128)}), f32[8,40,128]{2,1,0:T(8,128)S(1)}, u32[]{:S(2)}, u32[]{:S(2)}) async-start(f32[8,40,128]{2,1,0:T(8,128)} %second_sum.1), calls=%async_computation.3 | async-start | bytes 327680 | tf_op jit(solution)/shard_map/all_to_all | solution.py:263
  122.4 0.7 copy-start.4

commit v4 on v3

--- a/solution.py
+++ b/solution.py
@@ -13,12 +13,17 @@
 temper = 0.2
 epsilon = 1e-06
 LANES = 128
+VMEM_LIMIT = 24 * 2**20
 RETURN_ORDER = (0, 3, 7, 4, 1, 6, 2, 5)
 
 
 def shifted(value, axis, by):
     count = lax.axis_size(axis)
     return lax.ppermute(value, axis, [((i + by) % count, i) for i in range(count)])
+
+
+def in_vmem(value):
+    return pltpu.with_memory_space_constraint(value, pltpu.VMEM)
 
 
 def swapped(value, axis, step_by):
@@ -153,6 +158,11 @@
             weights_out[piece, tiles * rows_x :, :] = row.astype(jnp.bfloat16)
 
 
+def spread(own_ref, out_ref):
+    for i in range(out_ref.shape[0]):
+        out_ref[i] = own_ref[...]
+
+
 def first_sum(got_ref, out_ref, *, tiles, per_block, receivers):
     total = got_ref[0].astype(jnp.float32)
     for i in range(1, got_ref.shape[0]):
@@ -171,22 +181,24 @@
     total = got_ref[0].astype(jnp.float32)
     for i in range(1, got_ref.shape[0]):
         total = total + got_ref[i].astype(jnp.float32)
+    total = total.astype(jnp.bfloat16)
     for i in range(out_ref.shape[0]):
         out_ref[i] = total
 
 
 def third_sum(got_ref, one_ref, two_ref, bias_ref, *, tiles, per_block, nz, scale):
     for c, ref in enumerate((one_ref, two_ref)):
-        total = got_ref[c]
+        total = got_ref[c].astype(jnp.float32)
         for i in range(2 + c, got_ref.shape[0], 2):
-            total = total + got_ref[i]
+            total = total + got_ref[i].astype(jnp.float32)
         total = total * scale
         for t in range(tiles):
             ref[:, t * LANES : (t + 1) * LANES] = total[t * per_block : (t + 1) * per_block]
         if c == 0:
             start = (lax.axis_index("yh") * nz + lax.axis_index("z")) * per_block
             last = jnp.broadcast_to(total[tiles * per_block : tiles * per_block + 1], (8, LANES))
-            bias_ref[...] = pltpu.roll(last, lax.rem(LANES - start, LANES), 1)[:1]
+            last = pltpu.roll(last, lax.rem(LANES - start, LANES), 1)
+            bias_ref[...] = last[0, :per_block]
 
 
 def step(feats, pos, w_one, b_one, w_two):
@@ -197,7 +209,15 @@
     blocks = nz * nx * ny
     negatives = 2.0 * half * blocks - 2.0
     own = feats[0]
-    rows = lax.all_to_all(jnp.broadcast_to(own[None], (nz, *own.shape)), "z", 0, 0, tiled=True)
+    vmem = pl.BlockSpec(memory_space=pltpu.VMEM)
+    copies = pl.pallas_call(
+        spread,
+        in_specs=[vmem],
+        out_specs=vmem,
+        out_shape=jax.ShapeDtypeStruct((nz, *own.shape), own.dtype),
+        name="spread",
+    )(own)
+    rows = lax.all_to_all(copies, "z", 0, 0, tiled=True)
 
     flat = own.reshape(2 * half, width)
     pre_act = dot_nn(flat, w_one) + b_one
@@ -216,7 +236,6 @@
     order = [(0, 0), (1, 0), (0, 1), (1, 1), (0, 3), (1, 3), (0, 2), (1, 2)]
     pos_square = pos[0].reshape(blocks, half)
 
-    vmem = pl.BlockSpec(memory_space=pltpu.VMEM)
     piece_rows = width // nx // 2 * 2 * (width // LANES) + 8
     kept, sent_back, weights = pl.pallas_call(
         lambda *refs: tile_kernel(
@@ -237,8 +256,9 @@
             pltpu.VMEM((2 * nz * half, width), jnp.bfloat16),
             pltpu.VMEM((1, len(order) * half), jnp.int32),
         ],
+        compiler_params=pltpu.CompilerParams(vmem_limit_bytes=VMEM_LIMIT),
         name="tile",
-    )(rows, *cols, w_one, w_two, b_one[None], pos_square, pos_square.T)
+    )(*map(in_vmem, (rows, *cols, w_one, w_two, b_one[None], pos_square, pos_square.T)))
 
     tiles = width // LANES
     per_block = width // blocks
@@ -251,15 +271,15 @@
         out_specs=vmem,
         out_shape=jax.ShapeDtypeStruct((receivers, short, LANES), jnp.bfloat16),
         name="first_sum",
-    )(got)
+    )(in_vmem(got))
     got = lax.all_to_all(got, ("yh", "z"), 0, 0, tiled=True)
     got = pl.pallas_call(
         second_sum,
         in_specs=[vmem],
         out_specs=vmem,
-        out_shape=jax.ShapeDtypeStruct((subs, short, LANES), jnp.float32),
+        out_shape=jax.ShapeDtypeStruct((subs, short, LANES), jnp.bfloat16),
         name="second_sum",
-    )(got)
+    )(in_vmem(got))
     got = lax.all_to_all(got, SUB, 0, 0, tiled=True)
     share_one, share_two, share_bias = pl.pallas_call(
         functools.partial(
@@ -274,11 +294,10 @@
         out_shape=[
             jax.ShapeDtypeStruct((per_block, width), jnp.float32),
             jax.ShapeDtypeStruct((per_block, width), jnp.float32),
-            jax.ShapeDtypeStruct((1, LANES), jnp.float32),
+            jax.ShapeDtypeStruct((per_block,), jnp.float32),
         ],
         name="third_sum",
-    )(got)
-    share_bias = share_bias[0, :per_block]
+    )(in_vmem(got))
 
     grad = kept
     moved = sent_back

time: 127 us -> 118 us (0.929)
  local copies, waits for them, and re-layouts: 7.97 us -> 3.85 us
  Pallas kernels: 16.5 us -> 13.6 us
    broadcast_in_dim x1 -> x0, local copies, waits for them, and re-layouts: 1.99 us -> none  [step(): jnp.broadcast_to(own[None], (nz, *own.shape))]
    pallas_call x0 -> x1, Pallas kernels: none -> 1.97 us  [step(): pl.pallas_call(spread, in_specs=[vmem], out_specs=vmem, out_shape=jax.Sha...]
    pallas_call x1, Pallas kernels: 11.3 us -> 9.5 us  [step(): pl.pallas_call(lambda *refs: tile_kernel(*refs, nz=nz, nx=nx, ny=ny, half...]
    unnamed x35 -> x19, local copies, waits for them, and re-layouts: 4 us -> 3.65 us
  transfers between devices with their start and end apart: 12 -> 12, of which waited for: 5 -> 5; matrix products, arithmetic and copies ran while one was open for 3% -> 3% of each run, Pallas kernels for 3% -> 1%
where the time goes in v4:
time: 118 us
  starting transfers between devices  68.9 us (58%)
  waiting for transfers between devices  28.2 us (24%)
  Pallas kernels  13.6 us (12%)
  local copies, waits for them, and re-layouts  3.85 us (3%)
  other arithmetic  1.71 us (1%)
    ppermute x5, starting transfers between devices, shifted(): lax.ppermute(value, axis, [((i + by) % count, i) for i in range(count)])  20.7 us
    ppermute x3, starting transfers between devices, swapped(): return lax.ppermute(value, axis, pairs)  11.6 us
    all_to_all x1, starting transfers between devices, step(): got = lax.all_to_all(got, ('yh', 'z'), 0, 0, tiled=True)  11.4 us
    all_to_all x1, starting transfers between devices, step(): rows = lax.all_to_all(copies, 'z', 0, 0, tiled=True)  11 us
    all_to_all x1, waiting for transfers between devices, step(): got = lax.all_to_all(weights, ('co', 'x'), 0, 0, tiled=True)  10.7 us
    all_to_all x1, starting transfers between devices, step(): got = lax.all_to_all(weights, ('co', 'x'), 0, 0, tiled=True)  9.76 us
    pallas_call x1, Pallas kernels, step(): pl.pallas_call(lambda *refs: tile_kernel(*refs, nz=nz, nx=nx, ny=ny, half...  9.5 us
    all_to_all x1, waiting for transfers between devices, step(): got = lax.all_to_all(got, ('yh', 'z'), 0, 0, tiled=True)  7.34 us
  transfers between devices with their start and end apart: 12, of which 5 were waited for; matrix products, arithmetic and copies ran while one was open for 3% of the time, Pallas kernels for 1%

profile of v4, /device:TPU:1, one launch (start us, length us, event | category | flops | bytes accessed | tf_op | source)
XLA Modules:
  0.0 117.6 jit_solution(16895522450820576400)
XLA Ops:
  0.6 2.0 %spread.1 = bf16[8,2,64,512]{3,2,1,0:T(8,128)(2,1)} custom-call(bf16[2,64,512]{2,1,0:T(8,128)(2,1)} %bitcast.11), custom_call_target="tpu_custom_call" | custom-call | tf_op jit(solution)/shard_map/spread/pallas_call | solution.py:213
  2.6 11.0 %all-to-all-start = ((bf16[8,2,64,512]{3,2,1,0:T(8,128)(2,1)}), bf16[8,2,64,512]{3,2,1,0:T(8,128)(2,1)S(1)}, u32[]{:S(2)}, u32[]{:S(2)}) async-start(bf16[8,2,64,512]{3,2,1,0:T(8,128)(2,1)} %spread.1), calls=%async_computation | async-start | bytes 2097152 | tf_op jit(solution)/shard_map/all_to_all | solution.py:220
  13.7 0.6 multiply_reduce_fusion
  14.2 0.1 fusion.6.refs_1_
  14.3 7.5 %collective-permute-start = (bf16[1,128,512]{2,1,0:T(8,128)(2,1)S(1)}, bf16[1,128,512]{2,1,0:T(8,128)(2,1)S(1)}, u32[]{:S(2)}, u32[]{:S(2)}) collective-permute-start(bf16[1,128,512]{2,1,0:T(8,128)(2,1)S(1)} %fusion.6.refs_1_), channel_id=1, source_target_pairs={{32,0},{0,32},{33,1},{1,33},{34,2},{2,34},{35,3},{3,35},{36,4},{4,... | collective-permute-start | bytes 393224 | tf_op jit(solution)/shard_map/ppermute | solution.py:22
  21.8 2.8 %collective-permute-done.refs_2_ = bf16[1,128,512]{2,1,0:T(8,128)(2,1)S(1)} collective-permute-done((bf16[1,128,512]{2,1,0:T(8,128)(2,1)S(1)}, bf16[1,128,512]{2,1,0:T(8,128)(2,1)S(1)}, u32[]{:S(2)}, u32[]{:S(2)}) %collective-permute-start) | collective-permute-done | bytes 131104 | tf_op jit(solution)/shard_map/ppermute | solution.py:22
  24.7 3.1 %collective-permute-start.2 = (bf16[2,128,512]{2,1,0:T(8,128)(2,1)S(1)}, bf16[2,128,512]{2,1,0:T(8,128)(2,1)S(1)}, u32[]{:S(2)}, u32[]{:S(2)}) collective-permute-start(bf16[2,128,512]{2,1,0:T(8,128)(2,1)S(1)} %pad_maximum_fusion), channel_id=1, source_target_pairs={{24,0},{0,8},{8,16},{16,24},{25,1},{1,9},{9,17},{17,25},{26,2},{2,... | collective-permute-start | bytes 786440 | tf_op jit(solution)/shard_map/ppermute | solution.py:22
  27.8 3.4 %collective-permute-start.1 = (bf16[2,128,512]{2,1,0:T(8,128)(2,1)S(1)}, bf16[2,128,512]{2,1,0:T(8,128)(2,1)S(1)}, u32[]{:S(2)}, u32[]{:S(2)}) collective-permute-start(bf16[2,128,512]{2,1,0:T(8,128)(2,1)S(1)} %pad_maximum_fusion), channel_id=1, source_target_pairs={{8,0},{16,8},{24,16},{0,24},{9,1},{17,9},{25,17},{1,25},{10,2},{18... | collective-permute-start | bytes 786440 | tf_op jit(solution)/shard_map/ppermute | solution.py:22
  31.2 3.4 %collective-permute-start.3 = (bf16[1,128,512]{2,1,0:T(8,128)(2,1)S(1)}, bf16[1,128,512]{2,1,0:T(8,128)(2,1)S(1)}, u32[]{:S(2)}, u32[]{:S(2)}) collective-permute-start(bf16[1,128,512]{2,1,0:T(8,128)(2,1)S(1)} %fusion.6.refs_1_), channel_id=1, source_target_pairs={{16,0},{24,8},{0,16},{8,24},{17,1},{25,9},{1,17},{9,25},{18,2},{26... | collective-permute-start | bytes 393224 | tf_op jit(solution)/shard_map/ppermute | solution.py:22
  34.6 3.3 %collective-permute-start.4 = (bf16[1,128,512]{2,1,0:T(8,128)(2,1)S(1)}, bf16[1,128,512]{2,1,0:T(8,128)(2,1)S(1)}, u32[]{:S(2)}, u32[]{:S(2)}) collective-permute-start(bf16[1,128,512]{2,1,0:T(8,128)(2,1)S(1)} %collective-permute-done.refs_2_), channel_id=1, source_target_pairs={{16,0},{24,8},{0,16},{8,24},{17,1},{25,9},{1,17},{9,25},{18,2},{26... | collective-permute-start | bytes 393224 | tf_op jit(solution)/shard_map/ppermute | solution.py:22
  38.0 0.5 broadcast.11
  38.5 0.7 reduce.3
  39.3 0.6 copy-done.2
  40.0 2.8 %collective-permute-done.4.refs_6_ = bf16[1,128,512]{2,1,0:T(8,128)(2,1)S(1)} collective-permute-done((bf16[1,128,512]{2,1,0:T(8,128)(2,1)S(1)}, bf16[1,128,512]{2,1,0:T(8,128)(2,1)S(1)}, u32[]{:S(2)}, u32[]{:S(2)}) %collective-permute-start.4) | collective-permute-done | bytes 131104 | tf_op jit(solution)/shard_map/ppermute | solution.py:22
  42.8 0.7 copy-done.4
  43.5 0.9 copy-done.3
  44.4 0.9 copy-done.5
  45.3 9.5 %tile.1 = (bf16[4,2,64,512]{3,2,1,0:T(8,128)(2,1)S(1)}, bf16[4,2,64,512]{3,2,1,0:T(8,128)(2,1)}, bf16[8,520,128]{2,1,0:T(8,128)(2,1)}) custom-call(bf16[8,2,64,512]{3,2,1,0:T(8,128)(2,1)S(1)} %all-to-all-done.refs_0_, bf16[1,128,512]{2,1,0:T(8,128)(2,1)S(1)} %fusion.6.refs_1_, bf16[1,128,512]{2,1,0:T(8,128)(2,1)S(1)} %collective-permute-done.refs_2_, ...), custom_call_target="tpu_custom_call" | custom-call | tf_op jit(solution)/shard_map/tile/pallas_call | solution.py:240
  54.8 2.3 %collective-permute-start.5 = (bf16[4,2,64,512]{3,2,1,0:T(8,128)(2,1)}, bf16[4,2,64,512]{3,2,1,0:T(8,128)(2,1)S(1)}, u32[]{:S(2)}, u32[]{:S(2)}) collective-permute-start(bf16[4,2,64,512]{3,2,1,0:T(8,128)(2,1)} %get-tuple-element.11), channel_id=1, source_target_pairs={{0,1},{1,0},{2,3},{3,2},{4,5},{5,4},{6,7},{7,6},{8,9},{9,8},{10,11... | collective-permute-start | bytes 1572872 | tf_op jit(solution)/shard_map/ppermute | solution.py:32
  57.1 9.8 %all-to-all-start.1 = ((bf16[8,520,128]{2,1,0:T(8,128)(2,1)}), bf16[8,520,128]{2,1,0:T(8,128)(2,1)S(1)}, u32[]{:S(2)}, u32[]{:S(2)}) async-start(bf16[8,520,128]{2,1,0:T(8,128)(2,1)} %get-tuple-element.12), calls=%async_computation.1 | async-start | bytes 2129920 | tf_op jit(solution)/shard_map/all_to_all | solution.py:267
  66.8 0.1 convert_add_fusion
  67.0 4.3 %collective-permute-start.6 = (bf16[2,2,64,512]{3,2,1,0:T(8,128)(2,1)S(1)}, bf16[2,2,64,512]{3,2,1,0:T(8,128)(2,1)S(1)}, u32[]{:S(2)}, u32[]{:S(2)}) collective-permute-start(bf16[2,2,64,512]{3,2,1,0:T(8,128)(2,1)S(1)} %slice.28), channel_id=1, source_target_pairs={{0,7},{1,2},{2,1},{3,4},{4,3},{5,6},{6,5},{7,0},{8,15},{9,10},{10,... | collective-permute-start | bytes 786440 | tf_op jit(solution)/shard_map/ppermute | solution.py:32
  71.3 10.7 %all-to-all-done.1.got_ref = bf16[8,520,128]{2,1,0:T(8,128)(2,1)S(1)} async-done(((bf16[8,520,128]{2,1,0:T(8,128)(2,1)}), bf16[8,520,128]{2,1,0:T(8,128)(2,1)S(1)}, u32[]{:S(2)}, u32[]{:S(2)}) %all-to-all-start.1) | async-done | bytes 1064992 | tf_op jit(solution)/shard_map/all_to_all | solution.py:267
  82.0 0.8 first_sum.1
  82.8 11.4 %all-to-all-start.2 = ((bf16[16,40,128]{2,1,0:T(8,128)(2,1)}), bf16[16,40,128]{2,1,0:T(8,128)(2,1)S(1)}, u32[]{:S(2)}, u32[]{:S(2)}) async-start(bf16[16,40,128]{2,1,0:T(8,128)(2,1)} %first_sum.1), calls=%async_computation.2 | async-start | bytes 327680 | tf_op jit(solution)/shard_map/all_to_all | solution.py:275
  94.3 5.1 %collective-permute-start.7 = (bf16[1,2,64,512]{3,2,1,0:T(8,128)(2,1)S(1)}, bf16[1,2,64,512]{3,2,1,0:T(8,128)(2,1)S(1)}, u32[]{:S(2)}, u32[]{:S(2)}) collective-permute-start(bf16[1,2,64,512]{3,2,1,0:T(8,128)(2,1)S(1)} %slice.29), channel_id=1, source_target_pairs={{0,3},{1,6},{2,5},{3,0},{4,7},{5,2},{6,1},{7,4},{8,11},{9,14},{10,... | collective-permute-start | bytes 393224 | tf_op jit(solution)/shard_map/ppermute | solution.py:32
  99.4 7.3 %all-to-all-done.2.got_ref = bf16[16,40,128]{2,1,0:T(8,128)(2,1)S(1)} async-done(((bf16[16,40,128]{2,1,0:T(8,128)(2,1)}), bf16[16,40,128]{2,1,0:T(8,128)(2,1)S(1)}, u32[]{:S(2)}, u32[]{:S(2)}) %all-to-all-start.2) | async-done | bytes 163872 | tf_op jit(solution)/shard_map/all_to_all | solution.py:275
  106.7 0.7 second_sum.1
  107.4 4.4 %all-to-all-start.3 = ((bf16[8,40,128]{2,1,0:T(8,128)(2,1)}), bf16[8,40,128]{2,1,0:T(8,128)(2,1)S(1)}, u32[]{:S(2)}, u32[]{:S(2)}) async-start(bf16[8,40,128]{2,1,0:T(8,128)(2,1)} %second_sum.1), calls=%async_computation.3 | async-start | bytes 163840 | tf_op jit(solution)/shard_map/all_to_all | solution.py:283
  111.7 0.7 fusion.3
  112.4 4.5 %all-to-all-done.3.got_ref = bf16[8,40,128]{2,1,0:T(8,128)(2,1)S(1)} async-done(((bf16[8,40,128]{2,1,0:T(8,128)(2,1)}), bf16[8,40,128]{2,1,0:T(8,128)(2,1)S(1)}, u32[]{:S(2)}, u32[]{:S(2)}) %all-to-all-start.3) | async-done | bytes 81952 | tf_op jit(solution)/shard_map/all_to_all | solution.py:283
  117.0 0.6 third_sum.1
  (28 shorter events, 0.4 us)
Async XLA Ops:
  2.6 11.0 %copy-start = (bf16[512,512]{1,0:T(8,128)(2,1)S(1)}, bf16[512,512]{1,0:T(8,128)(2,1)}, u32[]{:S(2)}) copy-start(bf16[512,512]{1,0:T(8,128)(2,1)} %refs_8_.1) | copy-start | bytes 1572868
  2.6 11.0 %copy-start.1 = (bf16[512,512]{1,0:T(8,128)(2,1)S(1)}, bf16[512,512]{1,0:T(8,128)(2,1)}, u32[]{:S(2)}) copy-start(bf16[512,512]{1,0:T(8,128)(2,1)} %refs_7_.1) | copy-start | bytes 1572868
  2.6 11.0 %copy-start.6 = (f32[512]{0:T(512)S(1)}, f32[512]{0:T(512)}, u32[]{:S(2)}) copy-start(f32[512]{0:T(512)} %param.8) | copy-start | bytes 6148
  2.6 11.0 %copy-start.7 = (bf16[1,2,64,512]{3,2,1,0:T(8,128)(2,1)S(1)}, bf16[1,2,64,512]{3,2,1,0:T(8,128)(2,1)}, u32[]{:S(2)}) copy-start(bf16[1,2,64,512]{3,2,1,0:T(8,128)(2,1)} %param.5) | copy-start | bytes 393220
  2.6 40.9 %all-to-all-start = ((bf16[8,2,64,512]{3,2,1,0:T(8,128)(2,1)}), bf16[8,2,64,512]{3,2,1,0:T(8,128)(2,1)S(1)}, u32[]{:S(2)}, u32[]{:S(2)}) async-start(bf16[8,2,64,512]{3,2,1,0:T(8,128)(2,1)} %spread.1), calls=%async_computation | async-start | bytes 2097152 | tf_op jit(solution)/shard_map/all_to_all | solution.py:220
  13.6 24.8 %copy-start.8 = (s32[1,4096]{1,0:T(1,128)S(1)}, s32[1,4096]{1,0:T(1,128)}, u32[]{:S(2)}) copy-start(s32[1,4096]{1,0:T(1,128)} %param.6) | copy-start | bytes 49156
  14.3 10.3 %collective-permute-start = (bf16[1,128,512]{2,1,0:T(8,128)(2,1)S(1)}, bf16[1,128,512]{2,1,0:T(8,128)(2,1)S(1)}, u32[]{:S(2)}, u32[]{:S(2)}) collective-permute-start(bf16[1,128,512]{2,1,0:T(8,128)(2,1)S(1)} %fusion.6.refs_1_), channel_id=1, source_target_pairs={{32,0},{0,32},{33,1},{1,33},{34,2},{2,34},{35,3},{3,35},{36,4},{4,... | collective-permute-start | bytes 393224 | tf_op jit(solution)/shard_map/ppermute | solution.py:22
  24.7 18.8 %collective-permute-start.2 = (bf16[2,128,512]{2,1,0:T(8,128)(2,1)S(1)}, bf16[2,128,512]{2,1,0:T(8,128)(2,1)S(1)}, u32[]{:S(2)}, u32[]{:S(2)}) collective-permute-start(bf16[2,128,512]{2,1,0:T(8,128)(2,1)S(1)} %pad_maximum_fusion), channel_id=1, source_target_pairs={{24,0},{0,8},{8,16},{16,24},{25,1},{1,9},{9,17},{17,25},{26,2},{2,... | collective-permute-start | bytes 786440 | tf_op jit(solution)/shard_map/ppermute | solution.py:22
  27.8 15.7 %collective-permute-start.1 = (bf16[2,128,512]{2,1,0:T(8,128)(2,1)S(1)}, bf16[2,128,512]{2,1,0:T(8,128)(2,1)S(1)}, u32[]{:S(2)}, u32[]{:S(2)}) collective-permute-start(bf16[2,128,512]{2,1,0:T(8,128)(2,1)S(1)} %pad_maximum_fusion), channel_id=1, source_target_pairs={{8,0},{16,8},{24,16},{0,24},{9,1},{17,9},{25,17},{1,25},{10,2},{18... | collective-permute-start | bytes 786440 | tf_op jit(solution)/shard_map/ppermute | solution.py:22
  31.2 8.2 %collective-permute-start.3 = (bf16[1,128,512]{2,1,0:T(8,128)(2,1)S(1)}, bf16[1,128,512]{2,1,0:T(8,128)(2,1)S(1)}, u32[]{:S(2)}, u32[]{:S(2)}) collective-permute-start(bf16[1,128,512]{2,1,0:T(8,128)(2,1)S(1)} %fusion.6.refs_1_), channel_id=1, source_target_pairs={{16,0},{24,8},{0,16},{8,24},{17,1},{25,9},{1,17},{9,25},{18,2},{26... | collective-permute-start | bytes 393224 | tf_op jit(solution)/shard_map/ppermute | solution.py:22
  34.6 8.2 %collective-permute-start.4 = (bf16[1,128,512]{2,1,0:T(8,128)(2,1)S(1)}, bf16[1,128,512]{2,1,0:T(8,128)(2,1)S(1)}, u32[]{:S(2)}, u32[]{:S(2)}) collective-permute-start(bf16[1,128,512]{2,1,0:T(8,128)(2,1)S(1)} %collective-permute-done.refs_2_), channel_id=1, source_target_pairs={{16,0},{24,8},{0,16},{8,24},{17,1},{25,9},{1,17},{9,25},{18,2},{26... | collective-permute-start | bytes 393224 | tf_op jit(solution)/shard_map/ppermute | solution.py:22
  39.3 0.7 copy-start.2
  42.8 0.7 copy-start.4
  43.5 0.9 copy-start.3
  44.4 0.9 copy-start.5
  54.8 12.0 %collective-permute-start.5 = (bf16[4,2,64,512]{3,2,1,0:T(8,128)(2,1)}, bf16[4,2,64,512]{3,2,1,0:T(8,128)(2,1)S(1)}, u32[]{:S(2)}, u32[]{:S(2)}) collective-permute-start(bf16[4,2,64,512]{3,2,1,0:T(8,128)(2,1)} %get-tuple-element.11), channel_id=1, source_target_pairs={{0,1},{1,0},{2,3},{3,2},{4,5},{5,4},{6,7},{7,6},{8,9},{9,8},{10,11... | collective-permute-start | bytes 1572872 | tf_op jit(solution)/shard_map/ppermute | solution.py:32
  57.1 24.9 %all-to-all-start.1 = ((bf16[8,520,128]{2,1,0:T(8,128)(2,1)}), bf16[8,520,128]{2,1,0:T(8,128)(2,1)S(1)}, u32[]{:S(2)}, u32[]{:S(2)}) async-start(bf16[8,520,128]{2,1,0:T(8,128)(2,1)} %get-tuple-element.12), calls=%async_computation.1 | async-start | bytes 2129920 | tf_op jit(solution)/shard_map/all_to_all | solution.py:267
  67.0 27.1 %collective-permute-start.6 = (bf16[2,2,64,512]{3,2,1,0:T(8,128)(2,1)S(1)}, bf16[2,2,64,512]{3,2,1,0:T(8,128)(2,1)S(1)}, u32[]{:S(2)}, u32[]{:S(2)}) collective-permute-start(bf16[2,2,64,512]{3,2,1,0:T(8,128)(2,1)S(1)} %slice.28), channel_id=1, source_target_pairs={{0,7},{1,2},{2,1},{3,4},{4,3},{5,6},{6,5},{7,0},{8,15},{9,10},{10,... | collective-permute-start | bytes 786440 | tf_op jit(solution)/shard_map/ppermute | solution.py:32
  82.8 23.9 %all-to-all-start.2 = ((bf16[16,40,128]{2,1,0:T(8,128)(2,1)}), bf16[16,40,128]{2,1,0:T(8,128)(2,1)S(1)}, u32[]{:S(2)}, u32[]{:S(2)}) async-start(bf16[16,40,128]{2,1,0:T(8,128)(2,1)} %first_sum.1), calls=%async_computation.2 | async-start | bytes 327680 | tf_op jit(solution)/shard_map/all_to_all | solution.py:275
  94.3 17.5 %collective-permute-start.7 = (bf16[1,2,64,512]{3,2,1,0:T(8,128)(2,1)S(1)}, bf16[1,2,64,512]{3,2,1,0:T(8,128)(2,1)S(1)}, u32[]{:S(2)}, u32[]{:S(2)}) collective-permute-start(bf16[1,2,64,512]{3,2,1,0:T(8,128)(2,1)S(1)} %slice.29), channel_id=1, source_target_pairs={{0,3},{1,6},{2,5},{3,0},{4,7},{5,2},{6,1},{7,4},{8,11},{9,14},{10,... | collective-permute-start | bytes 393224 | tf_op jit(solution)/shard_map/ppermute | solution.py:32
  107.4 9.6 %all-to-all-start.3 = ((bf16[8,40,128]{2,1,0:T(8,128)(2,1)}), bf16[8,40,128]{2,1,0:T(8,128)(2,1)S(1)}, u32[]{:S(2)}, u32[]{:S(2)}) async-start(bf16[8,40,128]{2,1,0:T(8,128)(2,1)} %second_sum.1), calls=%async_computation.3 | async-start | bytes 163840 | tf_op jit(solution)/shard_map/all_to_all | solution.py:283

commit v5 on v4

--- a/solution.py
+++ b/solution.py
@@ -26,6 +26,10 @@
     return pltpu.with_memory_space_constraint(value, pltpu.VMEM)
 
 
+def in_hbm(value):
+    return pltpu.with_memory_space_constraint(value, pltpu.HBM)
+
+
 def swapped(value, axis, step_by):
     count = lax.axis_size(axis)
     pairs = [(i, (i + step_by * (1 - 2 * (i % 2))) % count) for i in range(count)]
@@ -44,12 +48,30 @@
     return lax.dot_general(a, b, (((0,), (0,)), ((), ())), preferred_element_type=jnp.float32)
 
 
+def pos_of(pos_ref, block):
+    start = pl.multiple_of(block // 2 * LANES, LANES)
+    pair = jnp.broadcast_to(pos_ref[:, pl.ds(start, LANES)], (8, LANES))
+    return jnp.where(lax.rem(block, 2) == 1, pltpu.roll(pair, LANES // 2, 1), pair)
+
+
+def rows_kernel(pre_ref, w_one_ref, kept_out, sent_out, *, nz, half):
+    w_one = w_one_ref[...]
+    per = nz // 2
+    chunk = per * half
+    for k, out in ((1, sent_out), (0, kept_out)):
+        for v in range(2):
+            start = (v * 2 + k) * chunk
+            rows = dot_nt(pre_ref[start : start + chunk, :], w_one).astype(jnp.bfloat16)
+            for j in range(per):
+                out[j, v] = rows[j * half : (j + 1) * half]
+
+
 def tile_kernel(*refs, nz, nx, ny, half, width, negatives, order):
     groups = 6
     rows_ref = refs[0]
     col_refs = refs[1 : 1 + groups]
-    w_one_ref, w_two_ref, b_one_ref, pos_ref, pos_t_ref = refs[1 + groups : 6 + groups]
-    kept_out, sent_out, weights_out, x_s, cols_s, hid_s, gp_s, pre_s, cpos_s = refs[6 + groups :]
+    w_one_ref, w_two_ref, b_one_ref, pos_ref = refs[1 + groups : 5 + groups]
+    pre_s, weights_out, cols_s, x_s, hid_s, gp_s, cpos_s = refs[5 + groups :]
     my_z, my_x, my_y = lax.axis_index("z"), lax.axis_index("x"), lax.axis_index("yh")
     my_yx = my_y * nx + my_x
     count = len(order)
@@ -64,14 +86,16 @@
     for j, (dy, dx) in enumerate(order):
         block = (lax.rem(my_y + dy, ny) * nx + lax.rem(my_x + dx, nx)) * nz + my_z
         cid = cid + jnp.where(lane // half == j, block * half, 0)
-        cpos_s[:, j * half : (j + 1) * half] = pos_ref[pl.ds(block, 1), :]
+        cpos_s[:, j * half : (j + 1) * half] = pos_of(pos_ref, block)[:1, :half]
     cpos = cpos_s[...]
     w_one = w_one_ref[...]
     w_two = w_two_ref[...]
     per = 256 // half
     chunk = per * half
     bias = jnp.zeros((1, width), jnp.float32)
-    block_lane = lax.broadcasted_iota(jnp.int32, pos_t_ref.shape, 1)
+    diagonal = lax.broadcasted_iota(jnp.int32, (half, LANES), 0) == lax.broadcasted_iota(
+        jnp.int32, (half, LANES), 1
+    )
     turn = 1 - 2 * lax.rem(my_z, 2)
     held = [lax.rem(my_z + turn * d + nz, nz) for d in RETURN_ORDER]
     half_iota = lax.broadcasted_iota(jnp.int32, (half, 1), 0)
@@ -94,7 +118,7 @@
                 rpos = jnp.concatenate(
                     [
                         jnp.sum(
-                            jnp.where(block_lane == my_yx * nz + b, pos_t_ref[...], 0),
+                            jnp.where(diagonal, pos_of(pos_ref, my_yx * nz + b)[:1], 0),
                             axis=1,
                             keepdims=True,
                         )
@@ -120,15 +144,11 @@
             inner = jnp.sum(unit * grad_unit, axis=1, keepdims=True)
             grad_proj = ((grad_unit - unit * inner) / radius).astype(jnp.bfloat16)
             grad_pre = (dot_nt(grad_proj, w_two) * slope).astype(jnp.bfloat16)
-            grad_rows = dot_nt(grad_pre, w_one).astype(jnp.bfloat16)
             bias = bias + jnp.sum(grad_pre.astype(jnp.float32), axis=0, keepdims=True)
             x_s[stack_at, :] = x
             hid_s[stack_at, :] = hidden
             gp_s[stack_at, :] = grad_proj
             pre_s[stack_at, :] = grad_pre
-            for j in range(per):
-                place = (kept_out, sent_out)[(k * per + j) * 2 // nz]
-                place[(k * per + j) % (nz // 2), v] = grad_rows[j * half : (j + 1) * half]
     parts = (
         dot_tn(x_s[...], pre_s[...]).astype(jnp.bfloat16),
         dot_tn(hid_s[...], gp_s[...]).astype(jnp.bfloat16),
@@ -234,22 +254,18 @@
     across_far = shifted(across, "x", 2)
     cols = [sent, across, both_next, both_last, own_far, across_far]
     order = [(0, 0), (1, 0), (0, 1), (1, 1), (0, 3), (1, 3), (0, 2), (1, 2)]
-    pos_square = pos[0].reshape(blocks, half)
-
     piece_rows = width // nx // 2 * 2 * (width // LANES) + 8
-    kept, sent_back, weights = pl.pallas_call(
+    pre, weights = pl.pallas_call(
         lambda *refs: tile_kernel(
             *refs, nz=nz, nx=nx, ny=ny, half=half, width=width, negatives=negatives, order=order
         ),
-        in_specs=[vmem] * (len(cols) + 6),
-        out_specs=[vmem, vmem, vmem],
+        in_specs=[vmem] * (len(cols) + 5),
+        out_specs=[vmem, vmem],
         out_shape=[
-            jax.ShapeDtypeStruct((nz // 2, 2, half, width), jnp.bfloat16),
-            jax.ShapeDtypeStruct((nz // 2, 2, half, width), jnp.bfloat16),
+            jax.ShapeDtypeStruct((2 * nz * half, width), jnp.bfloat16),
             jax.ShapeDtypeStruct((2 * nx, piece_rows, LANES), jnp.bfloat16),
         ],
         scratch_shapes=[
-            pltpu.VMEM((2 * nz * half, width), jnp.bfloat16),
             pltpu.VMEM((2, len(order) * half, width), jnp.bfloat16),
             pltpu.VMEM((2 * nz * half, width), jnp.bfloat16),
             pltpu.VMEM((2 * nz * half, width), jnp.bfloat16),
@@ -258,7 +274,7 @@
         ],
         compiler_params=pltpu.CompilerParams(vmem_limit_bytes=VMEM_LIMIT),
         name="tile",
-    )(*map(in_vmem, (rows, *cols, w_one, w_two, b_one[None], pos_square, pos_square.T)))
+    )(in_vmem(rows), in_vmem(cols[0]), in_vmem(cols[1]), in_hbm(cols[2]), in_hbm(cols[3]), in_vmem(cols[4]), in_hbm(cols[5]), *map(in_vmem, (w_one, w_two, b_one[None], pos)))
 
     tiles = width // LANES
     per_block = width // blocks
@@ -299,8 +315,14 @@
         name="third_sum",
     )(in_vmem(got))
 
-    grad = kept
-    moved = sent_back
+    grad, moved = pl.pallas_call(
+        functools.partial(rows_kernel, nz=nz, half=half),
+        in_specs=[vmem, vmem],
+        out_specs=[vmem, vmem],
+        out_shape=[jax.ShapeDtypeStruct((nz // 2, 2, half, width), jnp.bfloat16)] * 2,
+        compiler_params=pltpu.CompilerParams(vmem_limit_bytes=VMEM_LIMIT),
+        name="rows",
+    )(in_vmem(pre), w_one)
     for i, step_by in enumerate((1, -1, 3)):
         moved = swapped(moved, "z", step_by)
         grad = grad.astype(jnp.float32) + moved.astype(jnp.float32)

time: 118 us -> 118 us (level)
  local copies, waits for them, and re-layouts: 3.85 us -> 0.88 us
  waiting for transfers between devices: 28.2 us -> 30.2 us
    unnamed x19 -> x16, local copies, waits for them, and re-layouts: 3.65 us -> 0.83 us
    ppermute x5, waiting for transfers between devices: 5.65 us -> 7.67 us  [shifted(): lax.ppermute(value, axis, [((i + by) % count, i) for i in range(count)])]
  transfers between devices with their start and end apart: 12 -> 12, of which waited for: 5 -> 6; matrix products, arithmetic and copies ran while one was open for 3% -> 1% of each run, Pallas kernels for 1% -> 1%
where the time goes in v5:
time: 118 us; the launch traced here: 117 us
  starting transfers between devices  68.9 us (58%)
  waiting for transfers between devices  30.2 us (26%)
  Pallas kernels  14.6 us (12%)
    ppermute x5, starting transfers between devices, shifted(): lax.ppermute(value, axis, [((i + by) % count, i) for i in range(count)])  20.7 us
    ppermute x3, starting transfers between devices, swapped(): return lax.ppermute(value, axis, pairs)  11.6 us
    all_to_all x1, starting transfers between devices, step(): got = lax.all_to_all(got, ('yh', 'z'), 0, 0, tiled=True)  11.4 us
    all_to_all x1, starting transfers between devices, step(): rows = lax.all_to_all(copies, 'z', 0, 0, tiled=True)  11 us
    all_to_all x1, waiting for transfers between devices, step(): got = lax.all_to_all(weights, ('co', 'x'), 0, 0, tiled=True)  10.7 us
    pallas_call x1, Pallas kernels, step(): pl.pallas_call(lambda *refs: tile_kernel(*refs, nz=nz, nx=nx, ny=ny, half...  9.81 us
    all_to_all x1, starting transfers between devices, step(): got = lax.all_to_all(weights, ('co', 'x'), 0, 0, tiled=True)  9.76 us
    ppermute x5, waiting for transfers between devices, shifted(): lax.ppermute(value, axis, [((i + by) % count, i) for i in range(count)])  7.67 us
  transfers between devices with their start and end apart: 12, of which 6 were waited for; matrix products, arithmetic and copies ran while one was open for 1% of the time, Pallas kernels for 1%

profile of v5, /device:TPU:1, one launch (start us, length us, event | category | flops | bytes accessed | tf_op | source)
XLA Modules:
  0.0 117.0 jit_solution(17380725313860245234)
XLA Ops:
  0.6 2.0 %spread.1 = bf16[8,2,64,512]{3,2,1,0:T(8,128)(2,1)} custom-call(bf16[2,64,512]{2,1,0:T(8,128)(2,1)} %bitcast.9), custom_call_target="tpu_custom_call" | custom-call | tf_op jit(solution)/shard_map/spread/pallas_call | solution.py:233
  2.6 11.0 %all-to-all-start = ((bf16[8,2,64,512]{3,2,1,0:T(8,128)(2,1)}), bf16[8,2,64,512]{3,2,1,0:T(8,128)(2,1)S(1)}, u32[]{:S(2)}, u32[]{:S(2)}) async-start(bf16[8,2,64,512]{3,2,1,0:T(8,128)(2,1)} %spread.1), calls=%async_computation | async-start | bytes 2097152 | tf_op jit(solution)/shard_map/all_to_all | solution.py:240
  13.7 0.6 multiply_reduce_fusion
  14.2 0.1 fusion.6.refs_1_
  14.4 7.5 %collective-permute-start = (bf16[1,128,512]{2,1,0:T(8,128)(2,1)S(1)}, bf16[1,128,512]{2,1,0:T(8,128)(2,1)S(1)}, u32[]{:S(2)}, u32[]{:S(2)}) collective-permute-start(bf16[1,128,512]{2,1,0:T(8,128)(2,1)S(1)} %fusion.6.refs_1_), channel_id=1, source_target_pairs={{32,0},{0,32},{33,1},{1,33},{34,2},{2,34},{35,3},{3,35},{36,4},{4,... | collective-permute-start | bytes 393224 | tf_op jit(solution)/shard_map/ppermute | solution.py:22
  21.8 2.8 %collective-permute-done.refs_2_ = bf16[1,128,512]{2,1,0:T(8,128)(2,1)S(1)} collective-permute-done((bf16[1,128,512]{2,1,0:T(8,128)(2,1)S(1)}, bf16[1,128,512]{2,1,0:T(8,128)(2,1)S(1)}, u32[]{:S(2)}, u32[]{:S(2)}) %collective-permute-start) | collective-permute-done | bytes 131104 | tf_op jit(solution)/shard_map/ppermute | solution.py:22
  24.7 3.1 %collective-permute-start.2 = (bf16[2,128,512]{2,1,0:T(8,128)(2,1)S(1)}, bf16[2,128,512]{2,1,0:T(8,128)(2,1)S(1)}, u32[]{:S(2)}, u32[]{:S(2)}) collective-permute-start(bf16[2,128,512]{2,1,0:T(8,128)(2,1)S(1)} %pad_maximum_fusion), channel_id=1, source_target_pairs={{24,0},{0,8},{8,16},{16,24},{25,1},{1,9},{9,17},{17,25},{26,2},{2,... | collective-permute-start | bytes 786440 | tf_op jit(solution)/shard_map/ppermute | solution.py:22
  27.8 3.4 %collective-permute-start.1 = (bf16[2,128,512]{2,1,0:T(8,128)(2,1)S(1)}, bf16[2,128,512]{2,1,0:T(8,128)(2,1)S(1)}, u32[]{:S(2)}, u32[]{:S(2)}) collective-permute-start(bf16[2,128,512]{2,1,0:T(8,128)(2,1)S(1)} %pad_maximum_fusion), channel_id=1, source_target_pairs={{8,0},{16,8},{24,16},{0,24},{9,1},{17,9},{25,17},{1,25},{10,2},{18... | collective-permute-start | bytes 786440 | tf_op jit(solution)/shard_map/ppermute | solution.py:22
  31.2 3.4 %collective-permute-start.3 = (bf16[1,128,512]{2,1,0:T(8,128)(2,1)S(1)}, bf16[1,128,512]{2,1,0:T(8,128)(2,1)S(1)}, u32[]{:S(2)}, u32[]{:S(2)}) collective-permute-start(bf16[1,128,512]{2,1,0:T(8,128)(2,1)S(1)} %fusion.6.refs_1_), channel_id=1, source_target_pairs={{16,0},{24,8},{0,16},{8,24},{17,1},{25,9},{1,17},{9,25},{18,2},{26... | collective-permute-start | bytes 393224 | tf_op jit(solution)/shard_map/ppermute | solution.py:22
  34.6 3.3 %collective-permute-start.4 = (bf16[1,128,512]{2,1,0:T(8,128)(2,1)S(1)}, bf16[1,128,512]{2,1,0:T(8,128)(2,1)S(1)}, u32[]{:S(2)}, u32[]{:S(2)}) collective-permute-start(bf16[1,128,512]{2,1,0:T(8,128)(2,1)S(1)} %collective-permute-done.refs_2_), channel_id=1, source_target_pairs={{16,0},{24,8},{0,16},{8,24},{17,1},{25,9},{1,17},{9,25},{18,2},{26... | collective-permute-start | bytes 393224 | tf_op jit(solution)/shard_map/ppermute | solution.py:22
  38.0 0.7 collective-permute-done.3.refs_5_
  38.7 4.2 %collective-permute-done.4.refs_6_ = bf16[1,128,512]{2,1,0:T(8,128)(2,1)S(1)} collective-permute-done((bf16[1,128,512]{2,1,0:T(8,128)(2,1)S(1)}, bf16[1,128,512]{2,1,0:T(8,128)(2,1)S(1)}, u32[]{:S(2)}, u32[]{:S(2)}) %collective-permute-start.4) | collective-permute-done | bytes 131104 | tf_op jit(solution)/shard_map/ppermute | solution.py:22
  42.9 0.6 copy-done.7
  43.5 0.1 copy-done.4
  43.6 0.1 copy-done.5
  43.7 9.8 %tile.1 = (bf16[1024,512]{1,0:T(8,128)(2,1)S(1)}, bf16[8,520,128]{2,1,0:T(8,128)(2,1)}) custom-call(bf16[8,2,64,512]{3,2,1,0:T(8,128)(2,1)S(1)} %all-to-all-done.refs_0_, bf16[1,128,512]{2,1,0:T(8,128)(2,1)S(1)} %fusion.6.refs_1_, bf16[1,128,512]{2,1,0:T(8,128)(2,1)S(1)} %collective-permute-done.refs_2_, bf16[2,128,512]{2,1,0:T(8,128)(2,1)} %copy-done.5, ...), custom_call_target="tpu_custom_call" | custom-call | tf_op jit(solution)/shard_map/tile/pallas_call | solution.py:258
  53.5 0.7 rows.1
  54.2 2.3 %collective-permute-start.5 = (bf16[4,2,64,512]{3,2,1,0:T(8,128)(2,1)S(1)}, bf16[4,2,64,512]{3,2,1,0:T(8,128)(2,1)S(1)}, u32[]{:S(2)}, u32[]{:S(2)}) collective-permute-start(bf16[4,2,64,512]{3,2,1,0:T(8,128)(2,1)S(1)} %get-tuple-element.13), channel_id=1, source_target_pairs={{0,1},{1,0},{2,3},{3,2},{4,5},{5,4},{6,7},{7,6},{8,9},{9,8},{10,11... | collective-permute-start | bytes 1572872 | tf_op jit(solution)/shard_map/ppermute | solution.py:36
  56.5 9.8 %all-to-all-start.1 = ((bf16[8,520,128]{2,1,0:T(8,128)(2,1)}), bf16[8,520,128]{2,1,0:T(8,128)(2,1)S(1)}, u32[]{:S(2)}, u32[]{:S(2)}) async-start(bf16[8,520,128]{2,1,0:T(8,128)(2,1)} %get-tuple-element.14), calls=%async_computation.1 | async-start | bytes 2129920 | tf_op jit(solution)/shard_map/all_to_all | solution.py:283
  66.3 0.1 convert_add_fusion
  66.5 4.3 %collective-permute-start.6 = (bf16[2,2,64,512]{3,2,1,0:T(8,128)(2,1)S(1)}, bf16[2,2,64,512]{3,2,1,0:T(8,128)(2,1)S(1)}, u32[]{:S(2)}, u32[]{:S(2)}) collective-permute-start(bf16[2,2,64,512]{3,2,1,0:T(8,128)(2,1)S(1)} %slice.28), channel_id=1, source_target_pairs={{0,7},{1,2},{2,1},{3,4},{4,3},{5,6},{6,5},{7,0},{8,15},{9,10},{10,... | collective-permute-start | bytes 786440 | tf_op jit(solution)/shard_map/ppermute | solution.py:36
  70.8 10.7 %all-to-all-done.1.got_ref = bf16[8,520,128]{2,1,0:T(8,128)(2,1)S(1)} async-done(((bf16[8,520,128]{2,1,0:T(8,128)(2,1)}), bf16[8,520,128]{2,1,0:T(8,128)(2,1)S(1)}, u32[]{:S(2)}, u32[]{:S(2)}) %all-to-all-start.1) | async-done | bytes 1064992 | tf_op jit(solution)/shard_map/all_to_all | solution.py:283
  81.4 0.8 first_sum.1
  82.2 11.4 %all-to-all-start.2 = ((bf16[16,40,128]{2,1,0:T(8,128)(2,1)}), bf16[16,40,128]{2,1,0:T(8,128)(2,1)S(1)}, u32[]{:S(2)}, u32[]{:S(2)}) async-start(bf16[16,40,128]{2,1,0:T(8,128)(2,1)} %first_sum.1), calls=%async_computation.2 | async-start | bytes 327680 | tf_op jit(solution)/shard_map/all_to_all | solution.py:291
  93.6 0.1 slice_add_fusion
  93.7 5.1 %collective-permute-start.7 = (bf16[1,2,64,512]{3,2,1,0:T(8,128)(2,1)S(1)}, bf16[1,2,64,512]{3,2,1,0:T(8,128)(2,1)S(1)}, u32[]{:S(2)}, u32[]{:S(2)}) collective-permute-start(bf16[1,2,64,512]{3,2,1,0:T(8,128)(2,1)S(1)} %slice.29), channel_id=1, source_target_pairs={{0,3},{1,6},{2,5},{3,0},{4,7},{5,2},{6,1},{7,4},{8,11},{9,14},{10,... | collective-permute-start | bytes 393224 | tf_op jit(solution)/shard_map/ppermute | solution.py:36
  98.8 7.3 %all-to-all-done.2.got_ref = bf16[16,40,128]{2,1,0:T(8,128)(2,1)S(1)} async-done(((bf16[16,40,128]{2,1,0:T(8,128)(2,1)}), bf16[16,40,128]{2,1,0:T(8,128)(2,1)S(1)}, u32[]{:S(2)}, u32[]{:S(2)}) %all-to-all-start.2) | async-done | bytes 163872 | tf_op jit(solution)/shard_map/all_to_all | solution.py:291
  106.1 0.7 second_sum.1
  106.8 4.4 %all-to-all-start.3 = ((bf16[8,40,128]{2,1,0:T(8,128)(2,1)}), bf16[8,40,128]{2,1,0:T(8,128)(2,1)S(1)}, u32[]{:S(2)}, u32[]{:S(2)}) async-start(bf16[8,40,128]{2,1,0:T(8,128)(2,1)} %second_sum.1), calls=%async_computation.3 | async-start | bytes 163840 | tf_op jit(solution)/shard_map/all_to_all | solution.py:299
  111.2 0.7 fusion.3
  111.9 4.5 %all-to-all-done.3.got_ref = bf16[8,40,128]{2,1,0:T(8,128)(2,1)S(1)} async-done(((bf16[8,40,128]{2,1,0:T(8,128)(2,1)}), bf16[8,40,128]{2,1,0:T(8,128)(2,1)S(1)}, u32[]{:S(2)}, u32[]{:S(2)}) %all-to-all-start.3) | async-done | bytes 81952 | tf_op jit(solution)/shard_map/all_to_all | solution.py:299
  116.4 0.6 third_sum.1
  (23 shorter events, 0.1 us)
Async XLA Ops:
  2.6 11.0 %copy-start = (bf16[512,512]{1,0:T(8,128)(2,1)S(1)}, bf16[512,512]{1,0:T(8,128)(2,1)}, u32[]{:S(2)}) copy-start(bf16[512,512]{1,0:T(8,128)(2,1)} %w_one_ref.1) | copy-start | bytes 1572868
  2.6 11.0 %copy-start.1 = (bf16[512,512]{1,0:T(8,128)(2,1)S(1)}, bf16[512,512]{1,0:T(8,128)(2,1)}, u32[]{:S(2)}) copy-start(bf16[512,512]{1,0:T(8,128)(2,1)} %refs_8_.1) | copy-start | bytes 1572868
  2.6 11.0 %copy-start.3 = (f32[512]{0:T(512)S(1)}, f32[512]{0:T(512)}, u32[]{:S(2)}) copy-start(f32[512]{0:T(512)} %param.8) | copy-start | bytes 6148
  2.6 11.0 %copy-start.6 = (bf16[1,2,64,512]{3,2,1,0:T(8,128)(2,1)S(1)}, bf16[1,2,64,512]{3,2,1,0:T(8,128)(2,1)}, u32[]{:S(2)}) copy-start(bf16[1,2,64,512]{3,2,1,0:T(8,128)(2,1)} %param.5) | copy-start | bytes 393220
  2.6 40.2 %all-to-all-start = ((bf16[8,2,64,512]{3,2,1,0:T(8,128)(2,1)}), bf16[8,2,64,512]{3,2,1,0:T(8,128)(2,1)S(1)}, u32[]{:S(2)}, u32[]{:S(2)}) async-start(bf16[8,2,64,512]{3,2,1,0:T(8,128)(2,1)} %spread.1), calls=%async_computation | async-start | bytes 2097152 | tf_op jit(solution)/shard_map/all_to_all | solution.py:240
  13.7 30.0 %copy-start.2 = (s32[1,4096]{1,0:T(1,128)S(1)}, s32[1,4096]{1,0:T(1,128)}, u32[]{:S(2)}) copy-start(s32[1,4096]{1,0:T(1,128)} %refs_10_.1) | copy-start | bytes 49156
  14.4 10.3 %collective-permute-start = (bf16[1,128,512]{2,1,0:T(8,128)(2,1)S(1)}, bf16[1,128,512]{2,1,0:T(8,128)(2,1)S(1)}, u32[]{:S(2)}, u32[]{:S(2)}) collective-permute-start(bf16[1,128,512]{2,1,0:T(8,128)(2,1)S(1)} %fusion.6.refs_1_), channel_id=1, source_target_pairs={{32,0},{0,32},{33,1},{1,33},{34,2},{2,34},{35,3},{3,35},{36,4},{4,... | collective-permute-start | bytes 393224 | tf_op jit(solution)/shard_map/ppermute | solution.py:22
  24.7 18.2 %collective-permute-start.2 = (bf16[2,128,512]{2,1,0:T(8,128)(2,1)S(1)}, bf16[2,128,512]{2,1,0:T(8,128)(2,1)S(1)}, u32[]{:S(2)}, u32[]{:S(2)}) collective-permute-start(bf16[2,128,512]{2,1,0:T(8,128)(2,1)S(1)} %pad_maximum_fusion), channel_id=1, source_target_pairs={{24,0},{0,8},{8,16},{16,24},{25,1},{1,9},{9,17},{17,25},{26,2},{2,... | collective-permute-start | bytes 786440 | tf_op jit(solution)/shard_map/ppermute | solution.py:22
  27.8 15.1 %collective-permute-start.1 = (bf16[2,128,512]{2,1,0:T(8,128)(2,1)S(1)}, bf16[2,128,512]{2,1,0:T(8,128)(2,1)S(1)}, u32[]{:S(2)}, u32[]{:S(2)}) collective-permute-start(bf16[2,128,512]{2,1,0:T(8,128)(2,1)S(1)} %pad_maximum_fusion), channel_id=1, source_target_pairs={{8,0},{16,8},{24,16},{0,24},{9,1},{17,9},{25,17},{1,25},{10,2},{18... | collective-permute-start | bytes 786440 | tf_op jit(solution)/shard_map/ppermute | solution.py:22
  31.2 7.5 %collective-permute-start.3 = (bf16[1,128,512]{2,1,0:T(8,128)(2,1)S(1)}, bf16[1,128,512]{2,1,0:T(8,128)(2,1)S(1)}, u32[]{:S(2)}, u32[]{:S(2)}) collective-permute-start(bf16[1,128,512]{2,1,0:T(8,128)(2,1)S(1)} %fusion.6.refs_1_), channel_id=1, source_target_pairs={{16,0},{24,8},{0,16},{8,24},{17,1},{25,9},{1,17},{9,25},{18,2},{26... | collective-permute-start | bytes 393224 | tf_op jit(solution)/shard_map/ppermute | solution.py:22
  34.6 8.2 %collective-permute-start.4 = (bf16[1,128,512]{2,1,0:T(8,128)(2,1)S(1)}, bf16[1,128,512]{2,1,0:T(8,128)(2,1)S(1)}, u32[]{:S(2)}, u32[]{:S(2)}) collective-permute-start(bf16[1,128,512]{2,1,0:T(8,128)(2,1)S(1)} %collective-permute-done.refs_2_), channel_id=1, source_target_pairs={{16,0},{24,8},{0,16},{8,24},{17,1},{25,9},{1,17},{9,25},{18,2},{26... | collective-permute-start | bytes 393224 | tf_op jit(solution)/shard_map/ppermute | solution.py:22
  42.8 0.7 copy-start.7
  42.8 0.7 copy-start.4
  42.8 0.8 copy-start.5
  54.2 12.0 %collective-permute-start.5 = (bf16[4,2,64,512]{3,2,1,0:T(8,128)(2,1)S(1)}, bf16[4,2,64,512]{3,2,1,0:T(8,128)(2,1)S(1)}, u32[]{:S(2)}, u32[]{:S(2)}) collective-permute-start(bf16[4,2,64,512]{3,2,1,0:T(8,128)(2,1)S(1)} %get-tuple-element.13), channel_id=1, source_target_pairs={{0,1},{1,0},{2,3},{3,2},{4,5},{5,4},{6,7},{7,6},{8,9},{9,8},{10,11... | collective-permute-start | bytes 1572872 | tf_op jit(solution)/shard_map/ppermute | solution.py:36
  56.5 24.9 %all-to-all-start.1 = ((bf16[8,520,128]{2,1,0:T(8,128)(2,1)}), bf16[8,520,128]{2,1,0:T(8,128)(2,1)S(1)}, u32[]{:S(2)}, u32[]{:S(2)}) async-start(bf16[8,520,128]{2,1,0:T(8,128)(2,1)} %get-tuple-element.14), calls=%async_computation.1 | async-start | bytes 2129920 | tf_op jit(solution)/shard_map/all_to_all | solution.py:283
  66.5 27.1 %collective-permute-start.6 = (bf16[2,2,64,512]{3,2,1,0:T(8,128)(2,1)S(1)}, bf16[2,2,64,512]{3,2,1,0:T(8,128)(2,1)S(1)}, u32[]{:S(2)}, u32[]{:S(2)}) collective-permute-start(bf16[2,2,64,512]{3,2,1,0:T(8,128)(2,1)S(1)} %slice.28), channel_id=1, source_target_pairs={{0,7},{1,2},{2,1},{3,4},{4,3},{5,6},{6,5},{7,0},{8,15},{9,10},{10,... | collective-permute-start | bytes 786440 | tf_op jit(solution)/shard_map/ppermute | solution.py:36
  82.2 23.9 %all-to-all-start.2 = ((bf16[16,40,128]{2,1,0:T(8,128)(2,1)}), bf16[16,40,128]{2,1,0:T(8,128)(2,1)S(1)}, u32[]{:S(2)}, u32[]{:S(2)}) async-start(bf16[16,40,128]{2,1,0:T(8,128)(2,1)} %first_sum.1), calls=%async_computation.2 | async-start | bytes 327680 | tf_op jit(solution)/shard_map/all_to_all | solution.py:291
  93.7 17.5 %collective-permute-start.7 = (bf16[1,2,64,512]{3,2,1,0:T(8,128)(2,1)S(1)}, bf16[1,2,64,512]{3,2,1,0:T(8,128)(2,1)S(1)}, u32[]{:S(2)}, u32[]{:S(2)}) collective-permute-start(bf16[1,2,64,512]{3,2,1,0:T(8,128)(2,1)S(1)} %slice.29), channel_id=1, source_target_pairs={{0,3},{1,6},{2,5},{3,0},{4,7},{5,2},{6,1},{7,4},{8,11},{9,14},{10,... | collective-permute-start | bytes 393224 | tf_op jit(solution)/shard_map/ppermute | solution.py:36
  106.8 9.6 %all-to-all-start.3 = ((bf16[8,40,128]{2,1,0:T(8,128)(2,1)}), bf16[8,40,128]{2,1,0:T(8,128)(2,1)S(1)}, u32[]{:S(2)}, u32[]{:S(2)}) async-start(bf16[8,40,128]{2,1,0:T(8,128)(2,1)} %second_sum.1), calls=%async_computation.3 | async-start | bytes 163840 | tf_op jit(solution)/shard_map/all_to_all | solution.py:299

commit v6 on v4

--- a/solution.py
+++ b/solution.py
@@ -14,6 +14,7 @@
 epsilon = 1e-06
 LANES = 128
 VMEM_LIMIT = 24 * 2**20
+HELD = (0, 1)
 RETURN_ORDER = (0, 3, 7, 4, 1, 6, 2, 5)
 
 
@@ -24,6 +25,10 @@
 
 def in_vmem(value):
     return pltpu.with_memory_space_constraint(value, pltpu.VMEM)
+
+
+def in_hbm(value):
+    return pltpu.with_memory_space_constraint(value, pltpu.HBM)
 
 
 def swapped(value, axis, step_by):
@@ -44,12 +49,18 @@
     return lax.dot_general(a, b, (((0,), (0,)), ((), ())), preferred_element_type=jnp.float32)
 
 
+def pos_of(pos_ref, block):
+    start = pl.multiple_of(block // 2 * LANES, LANES)
+    pair = jnp.broadcast_to(pos_ref[:, pl.ds(start, LANES)], (8, LANES))
+    return jnp.where(lax.rem(block, 2) == 1, pltpu.roll(pair, LANES // 2, 1), pair)
+
+
 def tile_kernel(*refs, nz, nx, ny, half, width, negatives, order):
     groups = 6
     rows_ref = refs[0]
     col_refs = refs[1 : 1 + groups]
-    w_one_ref, w_two_ref, b_one_ref, pos_ref, pos_t_ref = refs[1 + groups : 6 + groups]
-    kept_out, sent_out, weights_out, x_s, cols_s, hid_s, gp_s, pre_s, cpos_s = refs[6 + groups :]
+    w_one_ref, w_two_ref, b_one_ref, pos_ref = refs[1 + groups : 5 + groups]
+    kept_out, sent_out, weights_out, x_s, cols_s, hid_s, gp_s, pre_s, cpos_s = refs[5 + groups :]
     my_z, my_x, my_y = lax.axis_index("z"), lax.axis_index("x"), lax.axis_index("yh")
     my_yx = my_y * nx + my_x
     count = len(order)
@@ -64,14 +75,16 @@
     for j, (dy, dx) in enumerate(order):
         block = (lax.rem(my_y + dy, ny) * nx + lax.rem(my_x + dx, nx)) * nz + my_z
         cid = cid + jnp.where(lane // half == j, block * half, 0)
-        cpos_s[:, j * half : (j + 1) * half] = pos_ref[pl.ds(block, 1), :]
+        cpos_s[:, j * half : (j + 1) * half] = pos_of(pos_ref, block)[:1, :half]
     cpos = cpos_s[...]
     w_one = w_one_ref[...]
     w_two = w_two_ref[...]
     per = 256 // half
     chunk = per * half
     bias = jnp.zeros((1, width), jnp.float32)
-    block_lane = lax.broadcasted_iota(jnp.int32, pos_t_ref.shape, 1)
+    diagonal = lax.broadcasted_iota(jnp.int32, (half, LANES), 0) == lax.broadcasted_iota(
+        jnp.int32, (half, LANES), 1
+    )
     turn = 1 - 2 * lax.rem(my_z, 2)
     held = [lax.rem(my_z + turn * d + nz, nz) for d in RETURN_ORDER]
     half_iota = lax.broadcasted_iota(jnp.int32, (half, 1), 0)
@@ -94,7 +107,7 @@
                 rpos = jnp.concatenate(
                     [
                         jnp.sum(
-                            jnp.where(block_lane == my_yx * nz + b, pos_t_ref[...], 0),
+                            jnp.where(diagonal, pos_of(pos_ref, my_yx * nz + b)[:1], 0),
                             axis=1,
                             keepdims=True,
                         )
@@ -168,13 +181,14 @@
     for i in range(1, got_ref.shape[0]):
         total = total + got_ref[i].astype(jnp.float32)
     rows_x = receivers * per_block
+    nz = out_ref.shape[0]
     for r in range(receivers):
         picked = [
             total[t * rows_x + r * per_block : t * rows_x + (r + 1) * per_block]
             for t in range(tiles)
         ]
         picked.append(total[tiles * rows_x :])
-        out_ref[r] = jnp.concatenate(picked, axis=0).astype(jnp.bfloat16)
+        out_ref[r % nz, r // nz] = jnp.concatenate(picked, axis=0).astype(jnp.bfloat16)
 
 
 def second_sum(got_ref, out_ref):
@@ -186,11 +200,13 @@
         out_ref[i] = total
 
 
-def third_sum(got_ref, one_ref, two_ref, bias_ref, *, tiles, per_block, nz, scale):
+def third_sum(got_ref, one_ref, two_ref, bias_ref, *, tiles, per_block, nz, ny, scale):
     for c, ref in enumerate((one_ref, two_ref)):
-        total = got_ref[c].astype(jnp.float32)
-        for i in range(2 + c, got_ref.shape[0], 2):
-            total = total + got_ref[i].astype(jnp.float32)
+        total = None
+        for i in range(got_ref.shape[0]):
+            if i // ny % 2 == c:
+                part = got_ref[i].astype(jnp.float32)
+                total = part if total is None else total + part
         total = total * scale
         for t in range(tiles):
             ref[:, t * LANES : (t + 1) * LANES] = total[t * per_block : (t + 1) * per_block]
@@ -234,14 +250,13 @@
     across_far = shifted(across, "x", 2)
     cols = [sent, across, both_next, both_last, own_far, across_far]
     order = [(0, 0), (1, 0), (0, 1), (1, 1), (0, 3), (1, 3), (0, 2), (1, 2)]
-    pos_square = pos[0].reshape(blocks, half)
-
     piece_rows = width // nx // 2 * 2 * (width // LANES) + 8
+    placed = [in_hbm(c) if i in HELD else in_vmem(c) for i, c in enumerate(cols)]
     kept, sent_back, weights = pl.pallas_call(
         lambda *refs: tile_kernel(
             *refs, nz=nz, nx=nx, ny=ny, half=half, width=width, negatives=negatives, order=order
         ),
-        in_specs=[vmem] * (len(cols) + 6),
+        in_specs=[vmem] * (len(cols) + 5),
         out_specs=[vmem, vmem, vmem],
         out_shape=[
             jax.ShapeDtypeStruct((nz // 2, 2, half, width), jnp.bfloat16),
@@ -258,7 +273,7 @@
         ],
         compiler_params=pltpu.CompilerParams(vmem_limit_bytes=VMEM_LIMIT),
         name="tile",
-    )(*map(in_vmem, (rows, *cols, w_one, w_two, b_one[None], pos_square, pos_square.T)))
+    )(in_vmem(rows), *placed, in_vmem(w_one), in_vmem(w_two), b_one[None], pos)
 
     tiles = width // LANES
     per_block = width // blocks
@@ -269,24 +284,26 @@
         functools.partial(first_sum, tiles=tiles, per_block=per_block, receivers=receivers),
         in_specs=[vmem],
         out_specs=vmem,
-        out_shape=jax.ShapeDtypeStruct((receivers, short, LANES), jnp.bfloat16),
+        out_shape=jax.ShapeDtypeStruct((nz, ny, short, LANES), jnp.bfloat16),
         name="first_sum",
     )(in_vmem(got))
-    got = lax.all_to_all(got, ("yh", "z"), 0, 0, tiled=True)
+    got = lax.all_to_all(got, "z", 0, 0, tiled=True)
     got = pl.pallas_call(
         second_sum,
         in_specs=[vmem],
         out_specs=vmem,
-        out_shape=jax.ShapeDtypeStruct((subs, short, LANES), jnp.bfloat16),
+        out_shape=jax.ShapeDtypeStruct((subs, ny, short, LANES), jnp.bfloat16),
         name="second_sum",
     )(in_vmem(got))
-    got = lax.all_to_all(got, SUB, 0, 0, tiled=True)
+    got = got.reshape(subs * ny, short, LANES)
+    got = lax.all_to_all(got, ("yl", "co", "yh"), 0, 0, tiled=True)
     share_one, share_two, share_bias = pl.pallas_call(
         functools.partial(
             third_sum,
             tiles=tiles,
             per_block=per_block,
             nz=nz,
+            ny=ny,
             scale=1.0 / (2.0 * half * blocks * subs),
         ),
         in_specs=[vmem],

time: 118 us -> 117 us (level)
  local copies, waits for them, and re-layouts: 3.85 us -> 0.08 us
  waiting for transfers between devices: 28.2 us -> 30.7 us
    unnamed x19 -> x14, local copies, waits for them, and re-layouts: 3.65 us -> 0.03 us
    ppermute x5, waiting for transfers between devices: 5.65 us -> 7.67 us  [shifted(): lax.ppermute(value, axis, [((i + by) % count, i) for i in range(count)])]
  transfers between devices with their start and end apart: 12 -> 12, of which waited for: 5 -> 6; matrix products, arithmetic and copies ran while one was open for 3% -> 1% of each run, Pallas kernels for 1% -> 1%
where the time goes in v6:
time: 117 us
  starting transfers between devices  68.9 us (59%)
  waiting for transfers between devices  30.7 us (26%)
  Pallas kernels  14.5 us (12%)
    ppermute x5, starting transfers between devices, shifted(): lax.ppermute(value, axis, [((i + by) % count, i) for i in range(count)])  20.7 us
    ppermute x3, starting transfers between devices, swapped(): return lax.ppermute(value, axis, pairs)  11.7 us
    all_to_all x1, starting transfers between devices, step(): rows = lax.all_to_all(copies, 'z', 0, 0, tiled=True)  11 us
    all_to_all x1, waiting for transfers between devices, step(): got = lax.all_to_all(weights, ('co', 'x'), 0, 0, tiled=True)  10.7 us
    pallas_call x1, Pallas kernels, step(): pl.pallas_call(lambda *refs: tile_kernel(*refs, nz=nz, nx=nx, ny=ny, half...  10.4 us
    all_to_all x1, starting transfers between devices, step(): got = lax.all_to_all(got, ('yl', 'co', 'yh'), 0, 0, tiled=True)  10.2 us
    all_to_all x1, starting transfers between devices, step(): got = lax.all_to_all(weights, ('co', 'x'), 0, 0, tiled=True)  9.78 us
    all_to_all x1, waiting for transfers between devices, step(): got = lax.all_to_all(got, ('yl', 'co', 'yh'), 0, 0, tiled=True)  8.9 us
  transfers between devices with their start and end apart: 12, of which 6 were waited for; matrix products, arithmetic and copies ran while one was open for 1% of the time, Pallas kernels for 1%

profile of v6, /device:TPU:1, one launch (start us, length us, event | category | flops | bytes accessed | tf_op | source)
XLA Modules:
  0.0 116.6 jit_solution(8520270013429142556)
XLA Ops:
  0.6 2.0 %spread.1 = bf16[8,2,64,512]{3,2,1,0:T(8,128)(2,1)} custom-call(bf16[2,64,512]{2,1,0:T(8,128)(2,1)} %bitcast.11), custom_call_target="tpu_custom_call" | custom-call | tf_op jit(solution)/shard_map/spread/pallas_call | solution.py:229
  2.6 11.0 %all-to-all-start = ((bf16[8,2,64,512]{3,2,1,0:T(8,128)(2,1)}), bf16[8,2,64,512]{3,2,1,0:T(8,128)(2,1)S(1)}, u32[]{:S(2)}, u32[]{:S(2)}) async-start(bf16[8,2,64,512]{3,2,1,0:T(8,128)(2,1)} %spread.1), calls=%async_computation | async-start | bytes 2097152 | tf_op jit(solution)/shard_map/all_to_all | solution.py:236
  13.6 0.0 copy-start.2
  13.7 0.6 multiply_reduce_fusion
  14.2 0.1 fusion.6.refs_1_
  14.4 0.0 copy-start.4
  14.4 7.5 %collective-permute-start = (bf16[1,128,512]{2,1,0:T(8,128)(2,1)S(1)}, bf16[1,128,512]{2,1,0:T(8,128)(2,1)S(1)}, u32[]{:S(2)}, u32[]{:S(2)}) collective-permute-start(bf16[1,128,512]{2,1,0:T(8,128)(2,1)S(1)} %fusion.6.refs_1_), channel_id=1, source_target_pairs={{32,0},{0,32},{33,1},{1,33},{34,2},{2,34},{35,3},{3,35},{36,4},{4,... | collective-permute-start | bytes 393224 | tf_op jit(solution)/shard_map/ppermute | solution.py:23
  21.8 2.8 %collective-permute-done.refs_2_ = bf16[1,128,512]{2,1,0:T(8,128)(2,1)S(1)} collective-permute-done((bf16[1,128,512]{2,1,0:T(8,128)(2,1)S(1)}, bf16[1,128,512]{2,1,0:T(8,128)(2,1)S(1)}, u32[]{:S(2)}, u32[]{:S(2)}) %collective-permute-start) | collective-permute-done | bytes 131104 | tf_op jit(solution)/shard_map/ppermute | solution.py:23
  24.7 3.1 %collective-permute-start.2 = (bf16[2,128,512]{2,1,0:T(8,128)(2,1)S(1)}, bf16[2,128,512]{2,1,0:T(8,128)(2,1)S(1)}, u32[]{:S(2)}, u32[]{:S(2)}) collective-permute-start(bf16[2,128,512]{2,1,0:T(8,128)(2,1)S(1)} %pad_maximum_fusion), channel_id=1, source_target_pairs={{24,0},{0,8},{8,16},{16,24},{25,1},{1,9},{9,17},{17,25},{26,2},{2,... | collective-permute-start | bytes 786440 | tf_op jit(solution)/shard_map/ppermute | solution.py:23
  27.8 3.4 %collective-permute-start.1 = (bf16[2,128,512]{2,1,0:T(8,128)(2,1)S(1)}, bf16[2,128,512]{2,1,0:T(8,128)(2,1)S(1)}, u32[]{:S(2)}, u32[]{:S(2)}) collective-permute-start(bf16[2,128,512]{2,1,0:T(8,128)(2,1)S(1)} %pad_maximum_fusion), channel_id=1, source_target_pairs={{8,0},{16,8},{24,16},{0,24},{9,1},{17,9},{25,17},{1,25},{10,2},{18... | collective-permute-start | bytes 786440 | tf_op jit(solution)/shard_map/ppermute | solution.py:23
  31.2 3.4 %collective-permute-start.3 = (bf16[1,128,512]{2,1,0:T(8,128)(2,1)S(1)}, bf16[1,128,512]{2,1,0:T(8,128)(2,1)S(1)}, u32[]{:S(2)}, u32[]{:S(2)}) collective-permute-start(bf16[1,128,512]{2,1,0:T(8,128)(2,1)S(1)} %fusion.6.refs_1_), channel_id=1, source_target_pairs={{16,0},{24,8},{0,16},{8,24},{17,1},{25,9},{1,17},{9,25},{18,2},{26... | collective-permute-start | bytes 393224 | tf_op jit(solution)/shard_map/ppermute | solution.py:23
  34.6 3.3 %collective-permute-start.4 = (bf16[1,128,512]{2,1,0:T(8,128)(2,1)S(1)}, bf16[1,128,512]{2,1,0:T(8,128)(2,1)S(1)}, u32[]{:S(2)}, u32[]{:S(2)}) collective-permute-start(bf16[1,128,512]{2,1,0:T(8,128)(2,1)S(1)} %collective-permute-done.refs_2_), channel_id=1, source_target_pairs={{16,0},{24,8},{0,16},{8,24},{17,1},{25,9},{1,17},{9,25},{18,2},{26... | collective-permute-start | bytes 393224 | tf_op jit(solution)/shard_map/ppermute | solution.py:23
  38.0 0.7 collective-permute-done.3.refs_5_
  38.7 4.2 %collective-permute-done.4.refs_6_ = bf16[1,128,512]{2,1,0:T(8,128)(2,1)S(1)} collective-permute-done((bf16[1,128,512]{2,1,0:T(8,128)(2,1)S(1)}, bf16[1,128,512]{2,1,0:T(8,128)(2,1)S(1)}, u32[]{:S(2)}, u32[]{:S(2)}) %collective-permute-start.4) | collective-permute-done | bytes 131104 | tf_op jit(solution)/shard_map/ppermute | solution.py:23
  42.8 0.0 collective-permute-done.2.refs_4_
  42.8 0.0 collective-permute-done.1.refs_3_
  42.9 10.4 %tile.1 = (bf16[4,2,64,512]{3,2,1,0:T(8,128)(2,1)S(1)}, bf16[4,2,64,512]{3,2,1,0:T(8,128)(2,1)}, bf16[8,520,128]{2,1,0:T(8,128)(2,1)}) custom-call(bf16[8,2,64,512]{3,2,1,0:T(8,128)(2,1)S(1)} %all-to-all-done.refs_0_, bf16[1,128,512]{2,1,0:T(8,128)(2,1)} %copy-done.4, bf16[1,128,512]{2,1,0:T(8,128)(2,1)} %copy-done.5, ...), custom_call_target="tpu_custom_call" | custom-call | tf_op jit(solution)/shard_map/tile/pallas_call | solution.py:255
  53.3 2.2 %collective-permute-start.5 = (bf16[4,2,64,512]{3,2,1,0:T(8,128)(2,1)}, bf16[4,2,64,512]{3,2,1,0:T(8,128)(2,1)S(1)}, u32[]{:S(2)}, u32[]{:S(2)}) collective-permute-start(bf16[4,2,64,512]{3,2,1,0:T(8,128)(2,1)} %get-tuple-element.11), channel_id=1, source_target_pairs={{0,1},{1,0},{2,3},{3,2},{4,5},{5,4},{6,7},{7,6},{8,9},{9,8},{10,11... | collective-permute-start | bytes 1572872 | tf_op jit(solution)/shard_map/ppermute | solution.py:37
  55.6 9.8 %all-to-all-start.1 = ((bf16[8,520,128]{2,1,0:T(8,128)(2,1)}), bf16[8,520,128]{2,1,0:T(8,128)(2,1)S(1)}, u32[]{:S(2)}, u32[]{:S(2)}) async-start(bf16[8,520,128]{2,1,0:T(8,128)(2,1)} %get-tuple-element.12), calls=%async_computation.1 | async-start | bytes 2129920 | tf_op jit(solution)/shard_map/all_to_all | solution.py:282
  65.3 0.1 convert_add_fusion
  65.5 4.3 %collective-permute-start.6 = (bf16[2,2,64,512]{3,2,1,0:T(8,128)(2,1)S(1)}, bf16[2,2,64,512]{3,2,1,0:T(8,128)(2,1)S(1)}, u32[]{:S(2)}, u32[]{:S(2)}) collective-permute-start(bf16[2,2,64,512]{3,2,1,0:T(8,128)(2,1)S(1)} %slice.28), channel_id=1, source_target_pairs={{0,7},{1,2},{2,1},{3,4},{4,3},{5,6},{6,5},{7,0},{8,15},{9,10},{10,... | collective-permute-start | bytes 786440 | tf_op jit(solution)/shard_map/ppermute | solution.py:37
  69.8 10.7 %all-to-all-done.1.got_ref = bf16[8,520,128]{2,1,0:T(8,128)(2,1)S(1)} async-done(((bf16[8,520,128]{2,1,0:T(8,128)(2,1)}), bf16[8,520,128]{2,1,0:T(8,128)(2,1)S(1)}, u32[]{:S(2)}, u32[]{:S(2)}) %all-to-all-start.1) | async-done | bytes 1064992 | tf_op jit(solution)/shard_map/all_to_all | solution.py:282
  80.5 0.8 first_sum.1
  81.3 5.5 %all-to-all-start.2 = ((bf16[8,2,40,128]{3,2,1,0:T(8,128)(2,1)}), bf16[8,2,40,128]{3,2,1,0:T(8,128)(2,1)S(1)}, u32[]{:S(2)}, u32[]{:S(2)}) async-start(bf16[8,2,40,128]{3,2,1,0:T(8,128)(2,1)} %first_sum.1), calls=%async_computation.2 | async-start | bytes 327680 | tf_op jit(solution)/shard_map/all_to_all | solution.py:290
  86.8 0.1 slice_add_fusion
  86.9 5.2 %collective-permute-start.7 = (bf16[1,2,64,512]{3,2,1,0:T(8,128)(2,1)S(1)}, bf16[1,2,64,512]{3,2,1,0:T(8,128)(2,1)S(1)}, u32[]{:S(2)}, u32[]{:S(2)}) collective-permute-start(bf16[1,2,64,512]{3,2,1,0:T(8,128)(2,1)S(1)} %slice.29), channel_id=1, source_target_pairs={{0,3},{1,6},{2,5},{3,0},{4,7},{5,2},{6,1},{7,4},{8,11},{9,14},{10,... | collective-permute-start | bytes 393224 | tf_op jit(solution)/shard_map/ppermute | solution.py:37
  92.0 3.5 %all-to-all-done.2.got_ref = bf16[8,2,40,128]{3,2,1,0:T(8,128)(2,1)S(1)} async-done(((bf16[8,2,40,128]{3,2,1,0:T(8,128)(2,1)}), bf16[8,2,40,128]{3,2,1,0:T(8,128)(2,1)S(1)}, u32[]{:S(2)}, u32[]{:S(2)}) %all-to-all-start.2) | async-done | bytes 163872 | tf_op jit(solution)/shard_map/all_to_all | solution.py:290
  95.5 0.7 second_sum.1
  96.2 10.2 %all-to-all-start.3 = ((bf16[16,40,128]{2,1,0:T(8,128)(2,1)}), bf16[16,40,128]{2,1,0:T(8,128)(2,1)S(1)}, u32[]{:S(2)}, u32[]{:S(2)}) async-start(bf16[16,40,128]{2,1,0:T(8,128)(2,1)} %bitcast.10), calls=%async_computation.3 | async-start | bytes 327680 | tf_op jit(solution)/shard_map/all_to_all | solution.py:299
  106.4 0.7 fusion.3
  107.1 8.9 %all-to-all-done.3.got_ref = bf16[16,40,128]{2,1,0:T(8,128)(2,1)S(1)} async-done(((bf16[16,40,128]{2,1,0:T(8,128)(2,1)}), bf16[16,40,128]{2,1,0:T(8,128)(2,1)S(1)}, u32[]{:S(2)}, u32[]{:S(2)}) %all-to-all-start.3) | async-done | bytes 163872 | tf_op jit(solution)/shard_map/all_to_all | solution.py:299
  116.0 0.6 third_sum.1
  (20 shorter events, 0.1 us)
Async XLA Ops:
  2.6 11.0 %copy-start = (bf16[512,512]{1,0:T(8,128)(2,1)S(1)}, bf16[512,512]{1,0:T(8,128)(2,1)}, u32[]{:S(2)}) copy-start(bf16[512,512]{1,0:T(8,128)(2,1)} %refs_8_.1) | copy-start | bytes 1572868
  2.6 11.0 %copy-start.1 = (bf16[512,512]{1,0:T(8,128)(2,1)S(1)}, bf16[512,512]{1,0:T(8,128)(2,1)}, u32[]{:S(2)}) copy-start(bf16[512,512]{1,0:T(8,128)(2,1)} %refs_7_.1) | copy-start | bytes 1572868
  2.6 11.0 %copy-start.3 = (f32[512]{0:T(512)S(1)}, f32[512]{0:T(512)}, u32[]{:S(2)}) copy-start(f32[512]{0:T(512)} %param.8) | copy-start | bytes 6148
  2.6 11.0 %copy-start.6 = (bf16[1,2,64,512]{3,2,1,0:T(8,128)(2,1)S(1)}, bf16[1,2,64,512]{3,2,1,0:T(8,128)(2,1)}, u32[]{:S(2)}) copy-start(bf16[1,2,64,512]{3,2,1,0:T(8,128)(2,1)} %param.5) | copy-start | bytes 393220
  2.6 40.2 %all-to-all-start = ((bf16[8,2,64,512]{3,2,1,0:T(8,128)(2,1)}), bf16[8,2,64,512]{3,2,1,0:T(8,128)(2,1)S(1)}, u32[]{:S(2)}, u32[]{:S(2)}) async-start(bf16[8,2,64,512]{3,2,1,0:T(8,128)(2,1)} %spread.1), calls=%async_computation | async-start | bytes 2097152 | tf_op jit(solution)/shard_map/all_to_all | solution.py:236
  13.6 29.2 %copy-start.2 = (s32[1,4096]{1,0:T(1,128)S(1)}, s32[1,4096]{1,0:T(1,128)}, u32[]{:S(2)}) copy-start(s32[1,4096]{1,0:T(1,128)} %refs_10_.1) | copy-start | bytes 49156
  14.4 28.5 %copy-start.4 = (bf16[1,128,512]{2,1,0:T(8,128)(2,1)}, bf16[1,128,512]{2,1,0:T(8,128)(2,1)S(1)}, u32[]{:S(2)}) copy-start(bf16[1,128,512]{2,1,0:T(8,128)(2,1)S(1)} %fusion.6.refs_1_) | copy-start | bytes 393220
  14.4 10.3 %collective-permute-start = (bf16[1,128,512]{2,1,0:T(8,128)(2,1)S(1)}, bf16[1,128,512]{2,1,0:T(8,128)(2,1)S(1)}, u32[]{:S(2)}, u32[]{:S(2)}) collective-permute-start(bf16[1,128,512]{2,1,0:T(8,128)(2,1)S(1)} %fusion.6.refs_1_), channel_id=1, source_target_pairs={{32,0},{0,32},{33,1},{1,33},{34,2},{2,34},{35,3},{3,35},{36,4},{4,... | collective-permute-start | bytes 393224 | tf_op jit(solution)/shard_map/ppermute | solution.py:23
  24.6 18.2 %copy-start.5 = (bf16[1,128,512]{2,1,0:T(8,128)(2,1)}, bf16[1,128,512]{2,1,0:T(8,128)(2,1)S(1)}, u32[]{:S(2)}) copy-start(bf16[1,128,512]{2,1,0:T(8,128)(2,1)S(1)} %collective-permute-done.refs_2_) | copy-start | bytes 393220
  24.7 18.2 %collective-permute-start.2 = (bf16[2,128,512]{2,1,0:T(8,128)(2,1)S(1)}, bf16[2,128,512]{2,1,0:T(8,128)(2,1)S(1)}, u32[]{:S(2)}, u32[]{:S(2)}) collective-permute-start(bf16[2,128,512]{2,1,0:T(8,128)(2,1)S(1)} %pad_maximum_fusion), channel_id=1, source_target_pairs={{24,0},{0,8},{8,16},{16,24},{25,1},{1,9},{9,17},{17,25},{26,2},{2,... | collective-permute-start | bytes 786440 | tf_op jit(solution)/shard_map/ppermute | solution.py:23
  27.8 15.1 %collective-permute-start.1 = (bf16[2,128,512]{2,1,0:T(8,128)(2,1)S(1)}, bf16[2,128,512]{2,1,0:T(8,128)(2,1)S(1)}, u32[]{:S(2)}, u32[]{:S(2)}) collective-permute-start(bf16[2,128,512]{2,1,0:T(8,128)(2,1)S(1)} %pad_maximum_fusion), channel_id=1, source_target_pairs={{8,0},{16,8},{24,16},{0,24},{9,1},{17,9},{25,17},{1,25},{10,2},{18... | collective-permute-start | bytes 786440 | tf_op jit(solution)/shard_map/ppermute | solution.py:23
  31.2 7.5 %collective-permute-start.3 = (bf16[1,128,512]{2,1,0:T(8,128)(2,1)S(1)}, bf16[1,128,512]{2,1,0:T(8,128)(2,1)S(1)}, u32[]{:S(2)}, u32[]{:S(2)}) collective-permute-start(bf16[1,128,512]{2,1,0:T(8,128)(2,1)S(1)} %fusion.6.refs_1_), channel_id=1, source_target_pairs={{16,0},{24,8},{0,16},{8,24},{17,1},{25,9},{1,17},{9,25},{18,2},{26... | collective-permute-start | bytes 393224 | tf_op jit(solution)/shard_map/ppermute | solution.py:23
  34.6 8.2 %collective-permute-start.4 = (bf16[1,128,512]{2,1,0:T(8,128)(2,1)S(1)}, bf16[1,128,512]{2,1,0:T(8,128)(2,1)S(1)}, u32[]{:S(2)}, u32[]{:S(2)}) collective-permute-start(bf16[1,128,512]{2,1,0:T(8,128)(2,1)S(1)} %collective-permute-done.refs_2_), channel_id=1, source_target_pairs={{16,0},{24,8},{0,16},{8,24},{17,1},{25,9},{1,17},{9,25},{18,2},{26... | collective-permute-start | bytes 393224 | tf_op jit(solution)/shard_map/ppermute | solution.py:23
  53.3 12.0 %collective-permute-start.5 = (bf16[4,2,64,512]{3,2,1,0:T(8,128)(2,1)}, bf16[4,2,64,512]{3,2,1,0:T(8,128)(2,1)S(1)}, u32[]{:S(2)}, u32[]{:S(2)}) collective-permute-start(bf16[4,2,64,512]{3,2,1,0:T(8,128)(2,1)} %get-tuple-element.11), channel_id=1, source_target_pairs={{0,1},{1,0},{2,3},{3,2},{4,5},{5,4},{6,7},{7,6},{8,9},{9,8},{10,11... | collective-permute-start | bytes 1572872 | tf_op jit(solution)/shard_map/ppermute | solution.py:37
  55.6 24.9 %all-to-all-start.1 = ((bf16[8,520,128]{2,1,0:T(8,128)(2,1)}), bf16[8,520,128]{2,1,0:T(8,128)(2,1)S(1)}, u32[]{:S(2)}, u32[]{:S(2)}) async-start(bf16[8,520,128]{2,1,0:T(8,128)(2,1)} %get-tuple-element.12), calls=%async_computation.1 | async-start | bytes 2129920 | tf_op jit(solution)/shard_map/all_to_all | solution.py:282
  65.5 21.2 %collective-permute-start.6 = (bf16[2,2,64,512]{3,2,1,0:T(8,128)(2,1)S(1)}, bf16[2,2,64,512]{3,2,1,0:T(8,128)(2,1)S(1)}, u32[]{:S(2)}, u32[]{:S(2)}) collective-permute-start(bf16[2,2,64,512]{3,2,1,0:T(8,128)(2,1)S(1)} %slice.28), channel_id=1, source_target_pairs={{0,7},{1,2},{2,1},{3,4},{4,3},{5,6},{6,5},{7,0},{8,15},{9,10},{10,... | collective-permute-start | bytes 786440 | tf_op jit(solution)/shard_map/ppermute | solution.py:37
  81.3 14.3 %all-to-all-start.2 = ((bf16[8,2,40,128]{3,2,1,0:T(8,128)(2,1)}), bf16[8,2,40,128]{3,2,1,0:T(8,128)(2,1)S(1)}, u32[]{:S(2)}, u32[]{:S(2)}) async-start(bf16[8,2,40,128]{3,2,1,0:T(8,128)(2,1)} %first_sum.1), calls=%async_computation.2 | async-start | bytes 327680 | tf_op jit(solution)/shard_map/all_to_all | solution.py:290
  86.9 19.5 %collective-permute-start.7 = (bf16[1,2,64,512]{3,2,1,0:T(8,128)(2,1)S(1)}, bf16[1,2,64,512]{3,2,1,0:T(8,128)(2,1)S(1)}, u32[]{:S(2)}, u32[]{:S(2)}) collective-permute-start(bf16[1,2,64,512]{3,2,1,0:T(8,128)(2,1)S(1)} %slice.29), channel_id=1, source_target_pairs={{0,3},{1,6},{2,5},{3,0},{4,7},{5,2},{6,1},{7,4},{8,11},{9,14},{10,... | collective-permute-start | bytes 393224 | tf_op jit(solution)/shard_map/ppermute | solution.py:37
  96.2 19.8 %all-to-all-start.3 = ((bf16[16,40,128]{2,1,0:T(8,128)(2,1)}), bf16[16,40,128]{2,1,0:T(8,128)(2,1)S(1)}, u32[]{:S(2)}, u32[]{:S(2)}) async-start(bf16[16,40,128]{2,1,0:T(8,128)(2,1)} %bitcast.10), calls=%async_computation.3 | async-start | bytes 327680 | tf_op jit(solution)/shard_map/all_to_all | solution.py:299

commit v7 on v6

--- a/solution.py
+++ b/solution.py
@@ -60,12 +60,23 @@
     rows_ref = refs[0]
     col_refs = refs[1 : 1 + groups]
     w_one_ref, w_two_ref, b_one_ref, pos_ref = refs[1 + groups : 5 + groups]
-    kept_out, sent_out, weights_out, x_s, cols_s, hid_s, gp_s, pre_s, cpos_s = refs[5 + groups :]
+    kept_out, sent_out, weights_out, x_s, cols_s, hid_s, gp_s, pre_s, cpos_s, col_sem = refs[5 + groups :]
     my_z, my_x, my_y = lax.axis_index("z"), lax.axis_index("x"), lax.axis_index("yh")
     my_yx = my_y * nx + my_x
     count = len(order)
-    at = 0
-    for ref in col_refs:
+    early = [
+        pltpu.make_async_copy(
+            col_refs[i].at[0, pl.ds(v * half, half)],
+            cols_s.at[v, pl.ds(i * half, half)],
+            col_sem.at[2 * i + v],
+        )
+        for i in range(2)
+        for v in range(2)
+    ]
+    for copy in early:
+        copy.start()
+    at = 2
+    for ref in col_refs[2:]:
         for i in range(ref.shape[0]):
             for v in range(2):
                 cols_s[v, at * half : (at + 1) * half, :] = ref[i, v * half : (v + 1) * half, :]
@@ -115,6 +126,9 @@
                     ],
                     axis=0,
                 )
+            if v == 0 and k == 0:
+                for copy in early:
+                    copy.wait()
             total = None
             for cv in range(2):
                 col = cols_s[cv]
@@ -181,14 +195,13 @@
     for i in range(1, got_ref.shape[0]):
         total = total + got_ref[i].astype(jnp.float32)
     rows_x = receivers * per_block
-    nz = out_ref.shape[0]
     for r in range(receivers):
         picked = [
             total[t * rows_x + r * per_block : t * rows_x + (r + 1) * per_block]
             for t in range(tiles)
         ]
         picked.append(total[tiles * rows_x :])
-        out_ref[r % nz, r // nz] = jnp.concatenate(picked, axis=0).astype(jnp.bfloat16)
+        out_ref[r] = jnp.concatenate(picked, axis=0).astype(jnp.bfloat16)
 
 
 def second_sum(got_ref, out_ref):
@@ -200,11 +213,11 @@
         out_ref[i] = total
 
 
-def third_sum(got_ref, one_ref, two_ref, bias_ref, *, tiles, per_block, nz, ny, scale):
+def third_sum(got_ref, one_ref, two_ref, bias_ref, *, tiles, per_block, nz, scale):
     for c, ref in enumerate((one_ref, two_ref)):
         total = None
         for i in range(got_ref.shape[0]):
-            if i // ny % 2 == c:
+            if i % 2 == c:
                 part = got_ref[i].astype(jnp.float32)
                 total = part if total is None else total + part
         total = total * scale
@@ -256,7 +269,7 @@
         lambda *refs: tile_kernel(
             *refs, nz=nz, nx=nx, ny=ny, half=half, width=width, negatives=negatives, order=order
         ),
-        in_specs=[vmem] * (len(cols) + 5),
+        in_specs=[vmem] + [pl.BlockSpec(memory_space=pltpu.HBM)] * 2 + [vmem] * (len(cols) + 2),
         out_specs=[vmem, vmem, vmem],
         out_shape=[
             jax.ShapeDtypeStruct((nz // 2, 2, half, width), jnp.bfloat16),
@@ -270,6 +283,7 @@
             pltpu.VMEM((2 * nz * half, width), jnp.bfloat16),
             pltpu.VMEM((2 * nz * half, width), jnp.bfloat16),
             pltpu.VMEM((1, len(order) * half), jnp.int32),
+            pltpu.SemaphoreType.DMA((4,)),
         ],
         compiler_params=pltpu.CompilerParams(vmem_limit_bytes=VMEM_LIMIT),
         name="tile",
@@ -284,26 +298,24 @@
         functools.partial(first_sum, tiles=tiles, per_block=per_block, receivers=receivers),
         in_specs=[vmem],
         out_specs=vmem,
-        out_shape=jax.ShapeDtypeStruct((nz, ny, short, LANES), jnp.bfloat16),
+        out_shape=jax.ShapeDtypeStruct((receivers, short, LANES), jnp.bfloat16),
         name="first_sum",
     )(in_vmem(got))
-    got = lax.all_to_all(got, "z", 0, 0, tiled=True)
+    got = lax.all_to_all(got, ("yh", "z"), 0, 0, tiled=True)
     got = pl.pallas_call(
         second_sum,
         in_specs=[vmem],
         out_specs=vmem,
-        out_shape=jax.ShapeDtypeStruct((subs, ny, short, LANES), jnp.bfloat16),
+        out_shape=jax.ShapeDtypeStruct((subs, short, LANES), jnp.bfloat16),
         name="second_sum",
     )(in_vmem(got))
-    got = got.reshape(subs * ny, short, LANES)
-    got = lax.all_to_all(got, ("yl", "co", "yh"), 0, 0, tiled=True)
+    got = lax.all_to_all(got, SUB, 0, 0, tiled=True)
     share_one, share_two, share_bias = pl.pallas_call(
         functools.partial(
             third_sum,
             tiles=tiles,
             per_block=per_block,
             nz=nz,
-            ny=ny,
             scale=1.0 / (2.0 * half * blocks * subs),
         ),
         in_specs=[vmem],

time: 117 us -> 117 us (level)
  no operation moved by 1% of the time
where the time goes in v7:
time: 117 us; the launch traced here: 116 us
  starting transfers between devices  68.9 us (59%)
  waiting for transfers between devices  30.2 us (26%)
  Pallas kernels  14.3 us (12%)
    ppermute x5, starting transfers between devices, shifted(): lax.ppermute(value, axis, [((i + by) % count, i) for i in range(count)])  20.7 us
    ppermute x3, starting transfers between devices, swapped(): return lax.ppermute(value, axis, pairs)  11.6 us
    all_to_all x1, starting transfers between devices, step(): got = lax.all_to_all(got, ('yh', 'z'), 0, 0, tiled=True)  11.4 us
    all_to_all x1, starting transfers between devices, step(): rows = lax.all_to_all(copies, 'z', 0, 0, tiled=True)  11 us
    all_to_all x1, waiting for transfers between devices, step(): got = lax.all_to_all(weights, ('co', 'x'), 0, 0, tiled=True)  10.6 us
    pallas_call x1, Pallas kernels, step(): pl.pallas_call(lambda *refs: tile_kernel(*refs, nz=nz, nx=nx, ny=ny, half...  10.3 us
    all_to_all x1, starting transfers between devices, step(): got = lax.all_to_all(weights, ('co', 'x'), 0, 0, tiled=True)  9.78 us
    ppermute x5, waiting for transfers between devices, shifted(): lax.ppermute(value, axis, [((i + by) % count, i) for i in range(count)])  7.67 us
  transfers between devices with their start and end apart: 12, of which 6 were waited for; matrix products, arithmetic and copies ran while one was open for 1% of the time, Pallas kernels for 1%

profile of v7, /device:TPU:1, one launch (start us, length us, event | category | flops | bytes accessed | tf_op | source)
XLA Modules:
  0.0 116.0 jit_solution(8270628036235899823)
XLA Ops:
  0.6 2.0 %spread.1 = bf16[8,2,64,512]{3,2,1,0:T(8,128)(2,1)} custom-call(bf16[2,64,512]{2,1,0:T(8,128)(2,1)} %bitcast.9), custom_call_target="tpu_custom_call" | custom-call | tf_op jit(solution)/shard_map/spread/pallas_call | solution.py:242
  2.6 11.0 %all-to-all-start = ((bf16[8,2,64,512]{3,2,1,0:T(8,128)(2,1)}), bf16[8,2,64,512]{3,2,1,0:T(8,128)(2,1)S(1)}, u32[]{:S(2)}, u32[]{:S(2)}) async-start(bf16[8,2,64,512]{3,2,1,0:T(8,128)(2,1)} %spread.1), calls=%async_computation | async-start | bytes 2097152 | tf_op jit(solution)/shard_map/all_to_all | solution.py:249
  13.6 0.0 copy-start.2
  13.7 0.6 multiply_reduce_fusion
  14.2 0.1 fusion.6.refs_1_
  14.4 0.0 copy-start.4
  14.4 7.5 %collective-permute-start = (bf16[1,128,512]{2,1,0:T(8,128)(2,1)S(1)}, bf16[1,128,512]{2,1,0:T(8,128)(2,1)S(1)}, u32[]{:S(2)}, u32[]{:S(2)}) collective-permute-start(bf16[1,128,512]{2,1,0:T(8,128)(2,1)S(1)} %fusion.6.refs_1_), channel_id=1, source_target_pairs={{32,0},{0,32},{33,1},{1,33},{34,2},{2,34},{35,3},{3,35},{36,4},{4,... | collective-permute-start | bytes 393224 | tf_op jit(solution)/shard_map/ppermute | solution.py:23
  21.8 2.8 %collective-permute-done.refs_2_ = bf16[1,128,512]{2,1,0:T(8,128)(2,1)S(1)} collective-permute-done((bf16[1,128,512]{2,1,0:T(8,128)(2,1)S(1)}, bf16[1,128,512]{2,1,0:T(8,128)(2,1)S(1)}, u32[]{:S(2)}, u32[]{:S(2)}) %collective-permute-start) | collective-permute-done | bytes 131104 | tf_op jit(solution)/shard_map/ppermute | solution.py:23
  24.7 3.1 %collective-permute-start.2 = (bf16[2,128,512]{2,1,0:T(8,128)(2,1)S(1)}, bf16[2,128,512]{2,1,0:T(8,128)(2,1)S(1)}, u32[]{:S(2)}, u32[]{:S(2)}) collective-permute-start(bf16[2,128,512]{2,1,0:T(8,128)(2,1)S(1)} %pad_maximum_fusion), channel_id=1, source_target_pairs={{24,0},{0,8},{8,16},{16,24},{25,1},{1,9},{9,17},{17,25},{26,2},{2,... | collective-permute-start | bytes 786440 | tf_op jit(solution)/shard_map/ppermute | solution.py:23
  27.8 3.4 %collective-permute-start.1 = (bf16[2,128,512]{2,1,0:T(8,128)(2,1)S(1)}, bf16[2,128,512]{2,1,0:T(8,128)(2,1)S(1)}, u32[]{:S(2)}, u32[]{:S(2)}) collective-permute-start(bf16[2,128,512]{2,1,0:T(8,128)(2,1)S(1)} %pad_maximum_fusion), channel_id=1, source_target_pairs={{8,0},{16,8},{24,16},{0,24},{9,1},{17,9},{25,17},{1,25},{10,2},{18... | collective-permute-start | bytes 786440 | tf_op jit(solution)/shard_map/ppermute | solution.py:23
  31.2 3.4 %collective-permute-start.3 = (bf16[1,128,512]{2,1,0:T(8,128)(2,1)S(1)}, bf16[1,128,512]{2,1,0:T(8,128)(2,1)S(1)}, u32[]{:S(2)}, u32[]{:S(2)}) collective-permute-start(bf16[1,128,512]{2,1,0:T(8,128)(2,1)S(1)} %fusion.6.refs_1_), channel_id=1, source_target_pairs={{16,0},{24,8},{0,16},{8,24},{17,1},{25,9},{1,17},{9,25},{18,2},{26... | collective-permute-start | bytes 393224 | tf_op jit(solution)/shard_map/ppermute | solution.py:23
  34.6 3.3 %collective-permute-start.4 = (bf16[1,128,512]{2,1,0:T(8,128)(2,1)S(1)}, bf16[1,128,512]{2,1,0:T(8,128)(2,1)S(1)}, u32[]{:S(2)}, u32[]{:S(2)}) collective-permute-start(bf16[1,128,512]{2,1,0:T(8,128)(2,1)S(1)} %collective-permute-done.refs_2_), channel_id=1, source_target_pairs={{16,0},{24,8},{0,16},{8,24},{17,1},{25,9},{1,17},{9,25},{18,2},{26... | collective-permute-start | bytes 393224 | tf_op jit(solution)/shard_map/ppermute | solution.py:23
  38.0 0.7 collective-permute-done.3.refs_5_
  38.7 4.2 %collective-permute-done.4.refs_6_ = bf16[1,128,512]{2,1,0:T(8,128)(2,1)S(1)} collective-permute-done((bf16[1,128,512]{2,1,0:T(8,128)(2,1)S(1)}, bf16[1,128,512]{2,1,0:T(8,128)(2,1)S(1)}, u32[]{:S(2)}, u32[]{:S(2)}) %collective-permute-start.4) | collective-permute-done | bytes 131104 | tf_op jit(solution)/shard_map/ppermute | solution.py:23
  42.8 0.0 collective-permute-done.2.refs_4_
  42.8 0.0 collective-permute-done.1.refs_3_
  42.9 10.3 %tile.1 = (bf16[4,2,64,512]{3,2,1,0:T(8,128)(2,1)S(1)}, bf16[4,2,64,512]{3,2,1,0:T(8,128)(2,1)}, bf16[8,520,128]{2,1,0:T(8,128)(2,1)}) custom-call(bf16[8,2,64,512]{3,2,1,0:T(8,128)(2,1)S(1)} %all-to-all-done.refs_0_, bf16[1,128,512]{2,1,0:T(8,128)(2,1)} %copy-done.4, bf16[1,128,512]{2,1,0:T(8,128)(2,1)} %copy-done.5, ...), custom_call_target="tpu_custom_call" | custom-call | tf_op jit(solution)/shard_map/tile/pallas_call | solution.py:268
  53.2 2.3 %collective-permute-start.5 = (bf16[4,2,64,512]{3,2,1,0:T(8,128)(2,1)}, bf16[4,2,64,512]{3,2,1,0:T(8,128)(2,1)S(1)}, u32[]{:S(2)}, u32[]{:S(2)}) collective-permute-start(bf16[4,2,64,512]{3,2,1,0:T(8,128)(2,1)} %get-tuple-element.11), channel_id=1, source_target_pairs={{0,1},{1,0},{2,3},{3,2},{4,5},{5,4},{6,7},{7,6},{8,9},{9,8},{10,11... | collective-permute-start | bytes 1572872 | tf_op jit(solution)/shard_map/ppermute | solution.py:37
  55.4 9.8 %all-to-all-start.1 = ((bf16[8,520,128]{2,1,0:T(8,128)(2,1)}), bf16[8,520,128]{2,1,0:T(8,128)(2,1)S(1)}, u32[]{:S(2)}, u32[]{:S(2)}) async-start(bf16[8,520,128]{2,1,0:T(8,128)(2,1)} %get-tuple-element.12), calls=%async_computation.1 | async-start | bytes 2129920 | tf_op jit(solution)/shard_map/all_to_all | solution.py:296
  65.2 0.1 convert_add_fusion
  65.4 4.3 %collective-permute-start.6 = (bf16[2,2,64,512]{3,2,1,0:T(8,128)(2,1)S(1)}, bf16[2,2,64,512]{3,2,1,0:T(8,128)(2,1)S(1)}, u32[]{:S(2)}, u32[]{:S(2)}) collective-permute-start(bf16[2,2,64,512]{3,2,1,0:T(8,128)(2,1)S(1)} %slice.28), channel_id=1, source_target_pairs={{0,7},{1,2},{2,1},{3,4},{4,3},{5,6},{6,5},{7,0},{8,15},{9,10},{10,... | collective-permute-start | bytes 786440 | tf_op jit(solution)/shard_map/ppermute | solution.py:37
  69.7 10.6 %all-to-all-done.1.got_ref = bf16[8,520,128]{2,1,0:T(8,128)(2,1)S(1)} async-done(((bf16[8,520,128]{2,1,0:T(8,128)(2,1)}), bf16[8,520,128]{2,1,0:T(8,128)(2,1)S(1)}, u32[]{:S(2)}, u32[]{:S(2)}) %all-to-all-start.1) | async-done | bytes 1064992 | tf_op jit(solution)/shard_map/all_to_all | solution.py:296
  80.4 0.8 first_sum.1
  81.2 11.4 %all-to-all-start.2 = ((bf16[16,40,128]{2,1,0:T(8,128)(2,1)}), bf16[16,40,128]{2,1,0:T(8,128)(2,1)S(1)}, u32[]{:S(2)}, u32[]{:S(2)}) async-start(bf16[16,40,128]{2,1,0:T(8,128)(2,1)} %first_sum.1), calls=%async_computation.2 | async-start | bytes 327680 | tf_op jit(solution)/shard_map/all_to_all | solution.py:304
  92.5 0.1 slice_add_fusion
  92.7 5.1 %collective-permute-start.7 = (bf16[1,2,64,512]{3,2,1,0:T(8,128)(2,1)S(1)}, bf16[1,2,64,512]{3,2,1,0:T(8,128)(2,1)S(1)}, u32[]{:S(2)}, u32[]{:S(2)}) collective-permute-start(bf16[1,2,64,512]{3,2,1,0:T(8,128)(2,1)S(1)} %slice.29), channel_id=1, source_target_pairs={{0,3},{1,6},{2,5},{3,0},{4,7},{5,2},{6,1},{7,4},{8,11},{9,14},{10,... | collective-permute-start | bytes 393224 | tf_op jit(solution)/shard_map/ppermute | solution.py:37
  97.7 7.3 %all-to-all-done.2.got_ref = bf16[16,40,128]{2,1,0:T(8,128)(2,1)S(1)} async-done(((bf16[16,40,128]{2,1,0:T(8,128)(2,1)}), bf16[16,40,128]{2,1,0:T(8,128)(2,1)S(1)}, u32[]{:S(2)}, u32[]{:S(2)}) %all-to-all-start.2) | async-done | bytes 163872 | tf_op jit(solution)/shard_map/all_to_all | solution.py:304
  105.1 0.7 second_sum.1
  105.8 4.4 %all-to-all-start.3 = ((bf16[8,40,128]{2,1,0:T(8,128)(2,1)}), bf16[8,40,128]{2,1,0:T(8,128)(2,1)S(1)}, u32[]{:S(2)}, u32[]{:S(2)}) async-start(bf16[8,40,128]{2,1,0:T(8,128)(2,1)} %second_sum.1), calls=%async_computation.3 | async-start | bytes 163840 | tf_op jit(solution)/shard_map/all_to_all | solution.py:312
  110.1 0.7 fusion.3
  110.8 4.5 %all-to-all-done.3.got_ref = bf16[8,40,128]{2,1,0:T(8,128)(2,1)S(1)} async-done(((bf16[8,40,128]{2,1,0:T(8,128)(2,1)}), bf16[8,40,128]{2,1,0:T(8,128)(2,1)S(1)}, u32[]{:S(2)}, u32[]{:S(2)}) %all-to-all-start.3) | async-done | bytes 81952 | tf_op jit(solution)/shard_map/all_to_all | solution.py:312
  115.4 0.6 third_sum.1
  (20 shorter events, 0.1 us)
Async XLA Ops:
  2.6 11.0 %copy-start = (bf16[512,512]{1,0:T(8,128)(2,1)S(1)}, bf16[512,512]{1,0:T(8,128)(2,1)}, u32[]{:S(2)}) copy-start(bf16[512,512]{1,0:T(8,128)(2,1)} %refs_8_.1) | copy-start | bytes 1572868
  2.6 11.0 %copy-start.1 = (bf16[512,512]{1,0:T(8,128)(2,1)S(1)}, bf16[512,512]{1,0:T(8,128)(2,1)}, u32[]{:S(2)}) copy-start(bf16[512,512]{1,0:T(8,128)(2,1)} %refs_7_.1) | copy-start | bytes 1572868
  2.6 11.0 %copy-start.3 = (f32[512]{0:T(512)S(1)}, f32[512]{0:T(512)}, u32[]{:S(2)}) copy-start(f32[512]{0:T(512)} %param.8) | copy-start | bytes 6148
  2.6 11.0 %copy-start.6 = (bf16[1,2,64,512]{3,2,1,0:T(8,128)(2,1)S(1)}, bf16[1,2,64,512]{3,2,1,0:T(8,128)(2,1)}, u32[]{:S(2)}) copy-start(bf16[1,2,64,512]{3,2,1,0:T(8,128)(2,1)} %param.5) | copy-start | bytes 393220
  2.6 40.2 %all-to-all-start = ((bf16[8,2,64,512]{3,2,1,0:T(8,128)(2,1)}), bf16[8,2,64,512]{3,2,1,0:T(8,128)(2,1)S(1)}, u32[]{:S(2)}, u32[]{:S(2)}) async-start(bf16[8,2,64,512]{3,2,1,0:T(8,128)(2,1)} %spread.1), calls=%async_computation | async-start | bytes 2097152 | tf_op jit(solution)/shard_map/all_to_all | solution.py:249
  13.6 29.2 %copy-start.2 = (s32[1,4096]{1,0:T(1,128)S(1)}, s32[1,4096]{1,0:T(1,128)}, u32[]{:S(2)}) copy-start(s32[1,4096]{1,0:T(1,128)} %refs_10_.1) | copy-start | bytes 49156
  14.4 28.5 %copy-start.4 = (bf16[1,128,512]{2,1,0:T(8,128)(2,1)}, bf16[1,128,512]{2,1,0:T(8,128)(2,1)S(1)}, u32[]{:S(2)}) copy-start(bf16[1,128,512]{2,1,0:T(8,128)(2,1)S(1)} %fusion.6.refs_1_) | copy-start | bytes 393220
  14.4 10.3 %collective-permute-start = (bf16[1,128,512]{2,1,0:T(8,128)(2,1)S(1)}, bf16[1,128,512]{2,1,0:T(8,128)(2,1)S(1)}, u32[]{:S(2)}, u32[]{:S(2)}) collective-permute-start(bf16[1,128,512]{2,1,0:T(8,128)(2,1)S(1)} %fusion.6.refs_1_), channel_id=1, source_target_pairs={{32,0},{0,32},{33,1},{1,33},{34,2},{2,34},{35,3},{3,35},{36,4},{4,... | collective-permute-start | bytes 393224 | tf_op jit(solution)/shard_map/ppermute | solution.py:23
  24.6 18.2 %copy-start.5 = (bf16[1,128,512]{2,1,0:T(8,128)(2,1)}, bf16[1,128,512]{2,1,0:T(8,128)(2,1)S(1)}, u32[]{:S(2)}) copy-start(bf16[1,128,512]{2,1,0:T(8,128)(2,1)S(1)} %collective-permute-done.refs_2_) | copy-start | bytes 393220
  24.7 18.2 %collective-permute-start.2 = (bf16[2,128,512]{2,1,0:T(8,128)(2,1)S(1)}, bf16[2,128,512]{2,1,0:T(8,128)(2,1)S(1)}, u32[]{:S(2)}, u32[]{:S(2)}) collective-permute-start(bf16[2,128,512]{2,1,0:T(8,128)(2,1)S(1)} %pad_maximum_fusion), channel_id=1, source_target_pairs={{24,0},{0,8},{8,16},{16,24},{25,1},{1,9},{9,17},{17,25},{26,2},{2,... | collective-permute-start | bytes 786440 | tf_op jit(solution)/shard_map/ppermute | solution.py:23
  27.8 15.1 %collective-permute-start.1 = (bf16[2,128,512]{2,1,0:T(8,128)(2,1)S(1)}, bf16[2,128,512]{2,1,0:T(8,128)(2,1)S(1)}, u32[]{:S(2)}, u32[]{:S(2)}) collective-permute-start(bf16[2,128,512]{2,1,0:T(8,128)(2,1)S(1)} %pad_maximum_fusion), channel_id=1, source_target_pairs={{8,0},{16,8},{24,16},{0,24},{9,1},{17,9},{25,17},{1,25},{10,2},{18... | collective-permute-start | bytes 786440 | tf_op jit(solution)/shard_map/ppermute | solution.py:23
  31.2 7.5 %collective-permute-start.3 = (bf16[1,128,512]{2,1,0:T(8,128)(2,1)S(1)}, bf16[1,128,512]{2,1,0:T(8,128)(2,1)S(1)}, u32[]{:S(2)}, u32[]{:S(2)}) collective-permute-start(bf16[1,128,512]{2,1,0:T(8,128)(2,1)S(1)} %fusion.6.refs_1_), channel_id=1, source_target_pairs={{16,0},{24,8},{0,16},{8,24},{17,1},{25,9},{1,17},{9,25},{18,2},{26... | collective-permute-start | bytes 393224 | tf_op jit(solution)/shard_map/ppermute | solution.py:23
  34.6 8.2 %collective-permute-start.4 = (bf16[1,128,512]{2,1,0:T(8,128)(2,1)S(1)}, bf16[1,128,512]{2,1,0:T(8,128)(2,1)S(1)}, u32[]{:S(2)}, u32[]{:S(2)}) collective-permute-start(bf16[1,128,512]{2,1,0:T(8,128)(2,1)S(1)} %collective-permute-done.refs_2_), channel_id=1, source_target_pairs={{16,0},{24,8},{0,16},{8,24},{17,1},{25,9},{1,17},{9,25},{18,2},{26... | collective-permute-start | bytes 393224 | tf_op jit(solution)/shard_map/ppermute | solution.py:23
  53.2 12.0 %collective-permute-start.5 = (bf16[4,2,64,512]{3,2,1,0:T(8,128)(2,1)}, bf16[4,2,64,512]{3,2,1,0:T(8,128)(2,1)S(1)}, u32[]{:S(2)}, u32[]{:S(2)}) collective-permute-start(bf16[4,2,64,512]{3,2,1,0:T(8,128)(2,1)} %get-tuple-element.11), channel_id=1, source_target_pairs={{0,1},{1,0},{2,3},{3,2},{4,5},{5,4},{6,7},{7,6},{8,9},{9,8},{10,11... | collective-permute-start | bytes 1572872 | tf_op jit(solution)/shard_map/ppermute | solution.py:37
  55.4 24.9 %all-to-all-start.1 = ((bf16[8,520,128]{2,1,0:T(8,128)(2,1)}), bf16[8,520,128]{2,1,0:T(8,128)(2,1)S(1)}, u32[]{:S(2)}, u32[]{:S(2)}) async-start(bf16[8,520,128]{2,1,0:T(8,128)(2,1)} %get-tuple-element.12), calls=%async_computation.1 | async-start | bytes 2129920 | tf_op jit(solution)/shard_map/all_to_all | solution.py:296
  65.4 27.1 %collective-permute-start.6 = (bf16[2,2,64,512]{3,2,1,0:T(8,128)(2,1)S(1)}, bf16[2,2,64,512]{3,2,1,0:T(8,128)(2,1)S(1)}, u32[]{:S(2)}, u32[]{:S(2)}) collective-permute-start(bf16[2,2,64,512]{3,2,1,0:T(8,128)(2,1)S(1)} %slice.28), channel_id=1, source_target_pairs={{0,7},{1,2},{2,1},{3,4},{4,3},{5,6},{6,5},{7,0},{8,15},{9,10},{10,... | collective-permute-start | bytes 786440 | tf_op jit(solution)/shard_map/ppermute | solution.py:37
  81.2 23.9 %all-to-all-start.2 = ((bf16[16,40,128]{2,1,0:T(8,128)(2,1)}), bf16[16,40,128]{2,1,0:T(8,128)(2,1)S(1)}, u32[]{:S(2)}, u32[]{:S(2)}) async-start(bf16[16,40,128]{2,1,0:T(8,128)(2,1)} %first_sum.1), calls=%async_computation.2 | async-start | bytes 327680 | tf_op jit(solution)/shard_map/all_to_all | solution.py:304
  92.7 17.5 %collective-permute-start.7 = (bf16[1,2,64,512]{3,2,1,0:T(8,128)(2,1)S(1)}, bf16[1,2,64,512]{3,2,1,0:T(8,128)(2,1)S(1)}, u32[]{:S(2)}, u32[]{:S(2)}) collective-permute-start(bf16[1,2,64,512]{3,2,1,0:T(8,128)(2,1)S(1)} %slice.29), channel_id=1, source_target_pairs={{0,3},{1,6},{2,5},{3,0},{4,7},{5,2},{6,1},{7,4},{8,11},{9,14},{10,... | collective-permute-start | bytes 393224 | tf_op jit(solution)/shard_map/ppermute | solution.py:37
  105.8 9.6 %all-to-all-start.3 = ((bf16[8,40,128]{2,1,0:T(8,128)(2,1)}), bf16[8,40,128]{2,1,0:T(8,128)(2,1)S(1)}, u32[]{:S(2)}, u32[]{:S(2)}) async-start(bf16[8,40,128]{2,1,0:T(8,128)(2,1)} %second_sum.1), calls=%async_computation.3 | async-start | bytes 163840 | tf_op jit(solution)/shard_map/all_to_all | solution.py:312

commit v8 on v6

--- a/solution.py
+++ b/solution.py
@@ -49,18 +49,12 @@
     return lax.dot_general(a, b, (((0,), (0,)), ((), ())), preferred_element_type=jnp.float32)
 
 
-def pos_of(pos_ref, block):
-    start = pl.multiple_of(block // 2 * LANES, LANES)
-    pair = jnp.broadcast_to(pos_ref[:, pl.ds(start, LANES)], (8, LANES))
-    return jnp.where(lax.rem(block, 2) == 1, pltpu.roll(pair, LANES // 2, 1), pair)
-
-
 def tile_kernel(*refs, nz, nx, ny, half, width, negatives, order):
     groups = 6
     rows_ref = refs[0]
     col_refs = refs[1 : 1 + groups]
-    w_one_ref, w_two_ref, b_one_ref, pos_ref = refs[1 + groups : 5 + groups]
-    kept_out, sent_out, weights_out, x_s, cols_s, hid_s, gp_s, pre_s, cpos_s = refs[5 + groups :]
+    w_one_ref, w_two_ref, b_one_ref, pos_ref, pos_t_ref = refs[1 + groups : 6 + groups]
+    kept_out, sent_out, weights_out, x_s, cols_s, hid_s, gp_s, pre_s, cpos_s = refs[6 + groups :]
     my_z, my_x, my_y = lax.axis_index("z"), lax.axis_index("x"), lax.axis_index("yh")
     my_yx = my_y * nx + my_x
     count = len(order)
@@ -75,16 +69,14 @@
     for j, (dy, dx) in enumerate(order):
         block = (lax.rem(my_y + dy, ny) * nx + lax.rem(my_x + dx, nx)) * nz + my_z
         cid = cid + jnp.where(lane // half == j, block * half, 0)
-        cpos_s[:, j * half : (j + 1) * half] = pos_of(pos_ref, block)[:1, :half]
+        cpos_s[:, j * half : (j + 1) * half] = pos_ref[pl.ds(block, 1), :]
     cpos = cpos_s[...]
     w_one = w_one_ref[...]
     w_two = w_two_ref[...]
     per = 256 // half
     chunk = per * half
     bias = jnp.zeros((1, width), jnp.float32)
-    diagonal = lax.broadcasted_iota(jnp.int32, (half, LANES), 0) == lax.broadcasted_iota(
-        jnp.int32, (half, LANES), 1
-    )
+    block_lane = lax.broadcasted_iota(jnp.int32, pos_t_ref.shape, 1)
     turn = 1 - 2 * lax.rem(my_z, 2)
     held = [lax.rem(my_z + turn * d + nz, nz) for d in RETURN_ORDER]
     half_iota = lax.broadcasted_iota(jnp.int32, (half, 1), 0)
@@ -107,7 +99,7 @@
                 rpos = jnp.concatenate(
                     [
                         jnp.sum(
-                            jnp.where(diagonal, pos_of(pos_ref, my_yx * nz + b)[:1], 0),
+                            jnp.where(block_lane == my_yx * nz + b, pos_t_ref[...], 0),
                             axis=1,
                             keepdims=True,
                         )
@@ -251,12 +243,13 @@
     cols = [sent, across, both_next, both_last, own_far, across_far]
     order = [(0, 0), (1, 0), (0, 1), (1, 1), (0, 3), (1, 3), (0, 2), (1, 2)]
     piece_rows = width // nx // 2 * 2 * (width // LANES) + 8
+    pos_square = pos[0].reshape(blocks, half)
     placed = [in_hbm(c) if i in HELD else in_vmem(c) for i, c in enumerate(cols)]
     kept, sent_back, weights = pl.pallas_call(
         lambda *refs: tile_kernel(
             *refs, nz=nz, nx=nx, ny=ny, half=half, width=width, negatives=negatives, order=order
         ),
-        in_specs=[vmem] * (len(cols) + 5),
+        in_specs=[vmem] * (len(cols) + 6),
         out_specs=[vmem, vmem, vmem],
         out_shape=[
             jax.ShapeDtypeStruct((nz // 2, 2, half, width), jnp.bfloat16),
@@ -273,7 +266,7 @@
         ],
         compiler_params=pltpu.CompilerParams(vmem_limit_bytes=VMEM_LIMIT),
         name="tile",
-    )(in_vmem(rows), *placed, in_vmem(w_one), in_vmem(w_two), b_one[None], pos)
+    )(in_vmem(rows), *placed, in_vmem(w_one), in_vmem(w_two), b_one[None], pos_square, pos_square.T)
 
     tiles = width // LANES
     per_block = width // blocks

time: 117 us -> 117 us (level)
  waiting for transfers between devices: 30.7 us -> 29.4 us
    ppermute x5, waiting for transfers between devices: 7.67 us -> 6.31 us  [shifted(): lax.ppermute(value, axis, [((i + by) % count, i) for i in range(count)])]
  transfers between devices with their start and end apart: 12 -> 12, of which waited for: 6 -> 5; matrix products, arithmetic and copies ran while one was open for 1% -> 3% of each run, Pallas kernels for 1% -> 1%
where the time goes in v8:
time: 117 us
  starting transfers between devices  68.8 us (59%)
  waiting for transfers between devices  29.4 us (25%)
  Pallas kernels  14.5 us (12%)
  other arithmetic  1.73 us (1%)
    ppermute x5, starting transfers between devices, shifted(): lax.ppermute(value, axis, [((i + by) % count, i) for i in range(count)])  20.7 us
    ppermute x3, starting transfers between devices, swapped(): return lax.ppermute(value, axis, pairs)  11.7 us
    all_to_all x1, starting transfers between devices, step(): rows = lax.all_to_all(copies, 'z', 0, 0, tiled=True)  11 us
    all_to_all x1, waiting for transfers between devices, step(): got = lax.all_to_all(weights, ('co', 'x'), 0, 0, tiled=True)  10.7 us
    pallas_call x1, Pallas kernels, step(): pl.pallas_call(lambda *refs: tile_kernel(*refs, nz=nz, nx=nx, ny=ny, half...  10.4 us
    all_to_all x1, starting transfers between devices, step(): got = lax.all_to_all(got, ('yl', 'co', 'yh'), 0, 0, tiled=True)  10.2 us
    all_to_all x1, starting transfers between devices, step(): got = lax.all_to_all(weights, ('co', 'x'), 0, 0, tiled=True)  9.8 us
    all_to_all x1, waiting for transfers between devices, step(): got = lax.all_to_all(got, ('yl', 'co', 'yh'), 0, 0, tiled=True)  8.9 us
  transfers between devices with their start and end apart: 12, of which 5 were waited for; matrix products, arithmetic and copies ran while one was open for 3% of the time, Pallas kernels for 1%

profile of v8, /device:TPU:1, one launch (start us, length us, event | category | flops | bytes accessed | tf_op | source)
XLA Modules:
  0.0 116.6 jit_solution(5562292525240370839)
XLA Ops:
  0.6 2.0 %spread.1 = bf16[8,2,64,512]{3,2,1,0:T(8,128)(2,1)} custom-call(bf16[2,64,512]{2,1,0:T(8,128)(2,1)} %bitcast.13), custom_call_target="tpu_custom_call" | custom-call | tf_op jit(solution)/shard_map/spread/pallas_call | solution.py:221
  2.6 11.0 %all-to-all-start = ((bf16[8,2,64,512]{3,2,1,0:T(8,128)(2,1)}), bf16[8,2,64,512]{3,2,1,0:T(8,128)(2,1)S(1)}, u32[]{:S(2)}, u32[]{:S(2)}) async-start(bf16[8,2,64,512]{3,2,1,0:T(8,128)(2,1)} %spread.1), calls=%async_computation | async-start | bytes 2097152 | tf_op jit(solution)/shard_map/all_to_all | solution.py:228
  13.6 0.0 copy-start.6
  13.7 0.6 multiply_reduce_fusion
  14.2 0.1 fusion.6.refs_1_
  14.4 7.5 %collective-permute-start = (bf16[1,128,512]{2,1,0:T(8,128)(2,1)S(1)}, bf16[1,128,512]{2,1,0:T(8,128)(2,1)S(1)}, u32[]{:S(2)}, u32[]{:S(2)}) collective-permute-start(bf16[1,128,512]{2,1,0:T(8,128)(2,1)S(1)} %fusion.6.refs_1_), channel_id=1, source_target_pairs={{32,0},{0,32},{33,1},{1,33},{34,2},{2,34},{35,3},{3,35},{36,4},{4,... | collective-permute-start | bytes 393224 | tf_op jit(solution)/shard_map/ppermute | solution.py:23
  21.8 2.8 %collective-permute-done.refs_2_ = bf16[1,128,512]{2,1,0:T(8,128)(2,1)S(1)} collective-permute-done((bf16[1,128,512]{2,1,0:T(8,128)(2,1)S(1)}, bf16[1,128,512]{2,1,0:T(8,128)(2,1)S(1)}, u32[]{:S(2)}, u32[]{:S(2)}) %collective-permute-start) | collective-permute-done | bytes 131104 | tf_op jit(solution)/shard_map/ppermute | solution.py:23
  24.7 3.1 %collective-permute-start.2 = (bf16[2,128,512]{2,1,0:T(8,128)(2,1)S(1)}, bf16[2,128,512]{2,1,0:T(8,128)(2,1)S(1)}, u32[]{:S(2)}, u32[]{:S(2)}) collective-permute-start(bf16[2,128,512]{2,1,0:T(8,128)(2,1)S(1)} %pad_maximum_fusion), channel_id=1, source_target_pairs={{24,0},{0,8},{8,16},{16,24},{25,1},{1,9},{9,17},{17,25},{26,2},{2,... | collective-permute-start | bytes 786440 | tf_op jit(solution)/shard_map/ppermute | solution.py:23
  27.8 3.4 %collective-permute-start.1 = (bf16[2,128,512]{2,1,0:T(8,128)(2,1)S(1)}, bf16[2,128,512]{2,1,0:T(8,128)(2,1)S(1)}, u32[]{:S(2)}, u32[]{:S(2)}) collective-permute-start(bf16[2,128,512]{2,1,0:T(8,128)(2,1)S(1)} %pad_maximum_fusion), channel_id=1, source_target_pairs={{8,0},{16,8},{24,16},{0,24},{9,1},{17,9},{25,17},{1,25},{10,2},{18... | collective-permute-start | bytes 786440 | tf_op jit(solution)/shard_map/ppermute | solution.py:23
  31.2 3.4 %collective-permute-start.3 = (bf16[1,128,512]{2,1,0:T(8,128)(2,1)S(1)}, bf16[1,128,512]{2,1,0:T(8,128)(2,1)S(1)}, u32[]{:S(2)}, u32[]{:S(2)}) collective-permute-start(bf16[1,128,512]{2,1,0:T(8,128)(2,1)S(1)} %fusion.6.refs_1_), channel_id=1, source_target_pairs={{16,0},{24,8},{0,16},{8,24},{17,1},{25,9},{1,17},{9,25},{18,2},{26... | collective-permute-start | bytes 393224 | tf_op jit(solution)/shard_map/ppermute | solution.py:23
  34.6 3.3 %collective-permute-start.4 = (bf16[1,128,512]{2,1,0:T(8,128)(2,1)S(1)}, bf16[1,128,512]{2,1,0:T(8,128)(2,1)S(1)}, u32[]{:S(2)}, u32[]{:S(2)}) collective-permute-start(bf16[1,128,512]{2,1,0:T(8,128)(2,1)S(1)} %collective-permute-done.refs_2_), channel_id=1, source_target_pairs={{16,0},{24,8},{0,16},{8,24},{17,1},{25,9},{1,17},{9,25},{18,2},{26... | collective-permute-start | bytes 393224 | tf_op jit(solution)/shard_map/ppermute | solution.py:23
  38.0 0.5 broadcast.11
  38.5 0.7 reduce.3
  39.2 0.1 reshape_squeeze.7.refs_10_
  39.3 0.1 copy.10
  39.3 3.5 %collective-permute-done.4.refs_6_ = bf16[1,128,512]{2,1,0:T(8,128)(2,1)S(1)} collective-permute-done((bf16[1,128,512]{2,1,0:T(8,128)(2,1)S(1)}, bf16[1,128,512]{2,1,0:T(8,128)(2,1)S(1)}, u32[]{:S(2)}, u32[]{:S(2)}) %collective-permute-start.4) | collective-permute-done | bytes 131104 | tf_op jit(solution)/shard_map/ppermute | solution.py:23
  42.9 10.4 %tile.1 = (bf16[4,2,64,512]{3,2,1,0:T(8,128)(2,1)S(1)}, bf16[4,2,64,512]{3,2,1,0:T(8,128)(2,1)}, bf16[8,520,128]{2,1,0:T(8,128)(2,1)}) custom-call(bf16[8,2,64,512]{3,2,1,0:T(8,128)(2,1)S(1)} %all-to-all-done.refs_0_, bf16[1,128,512]{2,1,0:T(8,128)(2,1)} %copy-done.3, bf16[1,128,512]{2,1,0:T(8,128)(2,1)} %copy-done.4, ...), custom_call_target="tpu_custom_call" | custom-call | tf_op jit(solution)/shard_map/tile/pallas_call | solution.py:248
  53.3 2.2 %collective-permute-start.5 = (bf16[4,2,64,512]{3,2,1,0:T(8,128)(2,1)}, bf16[4,2,64,512]{3,2,1,0:T(8,128)(2,1)S(1)}, u32[]{:S(2)}, u32[]{:S(2)}) collective-permute-start(bf16[4,2,64,512]{3,2,1,0:T(8,128)(2,1)} %get-tuple-element.11), channel_id=1, source_target_pairs={{0,1},{1,0},{2,3},{3,2},{4,5},{5,4},{6,7},{7,6},{8,9},{9,8},{10,11... | collective-permute-start | bytes 1572872 | tf_op jit(solution)/shard_map/ppermute | solution.py:37
  55.5 9.8 %all-to-all-start.1 = ((bf16[8,520,128]{2,1,0:T(8,128)(2,1)}), bf16[8,520,128]{2,1,0:T(8,128)(2,1)S(1)}, u32[]{:S(2)}, u32[]{:S(2)}) async-start(bf16[8,520,128]{2,1,0:T(8,128)(2,1)} %get-tuple-element.12), calls=%async_computation.1 | async-start | bytes 2129920 | tf_op jit(solution)/shard_map/all_to_all | solution.py:275
  65.3 0.1 convert_add_fusion
  65.5 4.3 %collective-permute-start.6 = (bf16[2,2,64,512]{3,2,1,0:T(8,128)(2,1)S(1)}, bf16[2,2,64,512]{3,2,1,0:T(8,128)(2,1)S(1)}, u32[]{:S(2)}, u32[]{:S(2)}) collective-permute-start(bf16[2,2,64,512]{3,2,1,0:T(8,128)(2,1)S(1)} %slice.28), channel_id=1, source_target_pairs={{0,7},{1,2},{2,1},{3,4},{4,3},{5,6},{6,5},{7,0},{8,15},{9,10},{10,... | collective-permute-start | bytes 786440 | tf_op jit(solution)/shard_map/ppermute | solution.py:37
  69.8 10.7 %all-to-all-done.1.got_ref = bf16[8,520,128]{2,1,0:T(8,128)(2,1)S(1)} async-done(((bf16[8,520,128]{2,1,0:T(8,128)(2,1)}), bf16[8,520,128]{2,1,0:T(8,128)(2,1)S(1)}, u32[]{:S(2)}, u32[]{:S(2)}) %all-to-all-start.1) | async-done | bytes 1064992 | tf_op jit(solution)/shard_map/all_to_all | solution.py:275
  80.5 0.8 first_sum.1
  81.3 5.5 %all-to-all-start.2 = ((bf16[8,2,40,128]{3,2,1,0:T(8,128)(2,1)}), bf16[8,2,40,128]{3,2,1,0:T(8,128)(2,1)S(1)}, u32[]{:S(2)}, u32[]{:S(2)}) async-start(bf16[8,2,40,128]{3,2,1,0:T(8,128)(2,1)} %first_sum.1), calls=%async_computation.2 | async-start | bytes 327680 | tf_op jit(solution)/shard_map/all_to_all | solution.py:283
  86.8 0.1 slice_add_fusion
  86.9 5.2 %collective-permute-start.7 = (bf16[1,2,64,512]{3,2,1,0:T(8,128)(2,1)S(1)}, bf16[1,2,64,512]{3,2,1,0:T(8,128)(2,1)S(1)}, u32[]{:S(2)}, u32[]{:S(2)}) collective-permute-start(bf16[1,2,64,512]{3,2,1,0:T(8,128)(2,1)S(1)} %slice.29), channel_id=1, source_target_pairs={{0,3},{1,6},{2,5},{3,0},{4,7},{5,2},{6,1},{7,4},{8,11},{9,14},{10,... | collective-permute-start | bytes 393224 | tf_op jit(solution)/shard_map/ppermute | solution.py:37
  92.1 3.5 %all-to-all-done.2.got_ref = bf16[8,2,40,128]{3,2,1,0:T(8,128)(2,1)S(1)} async-done(((bf16[8,2,40,128]{3,2,1,0:T(8,128)(2,1)}), bf16[8,2,40,128]{3,2,1,0:T(8,128)(2,1)S(1)}, u32[]{:S(2)}, u32[]{:S(2)}) %all-to-all-start.2) | async-done | bytes 163872 | tf_op jit(solution)/shard_map/all_to_all | solution.py:283
  95.5 0.7 second_sum.1
  96.2 10.2 %all-to-all-start.3 = ((bf16[16,40,128]{2,1,0:T(8,128)(2,1)}), bf16[16,40,128]{2,1,0:T(8,128)(2,1)S(1)}, u32[]{:S(2)}, u32[]{:S(2)}) async-start(bf16[16,40,128]{2,1,0:T(8,128)(2,1)} %bitcast.12), calls=%async_computation.3 | async-start | bytes 327680 | tf_op jit(solution)/shard_map/all_to_all | solution.py:292
  106.4 0.7 fusion.3
  107.1 8.9 %all-to-all-done.3.got_ref = bf16[16,40,128]{2,1,0:T(8,128)(2,1)S(1)} async-done(((bf16[16,40,128]{2,1,0:T(8,128)(2,1)}), bf16[16,40,128]{2,1,0:T(8,128)(2,1)S(1)}, u32[]{:S(2)}, u32[]{:S(2)}) %all-to-all-start.3) | async-done | bytes 163872 | tf_op jit(solution)/shard_map/all_to_all | solution.py:292
  116.0 0.6 third_sum.1
  (24 shorter events, 0.1 us)
Async XLA Ops:
  2.6 11.0 %copy-start = (bf16[512,512]{1,0:T(8,128)(2,1)S(1)}, bf16[512,512]{1,0:T(8,128)(2,1)}, u32[]{:S(2)}) copy-start(bf16[512,512]{1,0:T(8,128)(2,1)} %refs_8_.1) | copy-start | bytes 1572868
  2.6 11.0 %copy-start.1 = (bf16[512,512]{1,0:T(8,128)(2,1)S(1)}, bf16[512,512]{1,0:T(8,128)(2,1)}, u32[]{:S(2)}) copy-start(bf16[512,512]{1,0:T(8,128)(2,1)} %refs_7_.1) | copy-start | bytes 1572868
  2.6 11.0 %copy-start.2 = (f32[512]{0:T(512)S(1)}, f32[512]{0:T(512)}, u32[]{:S(2)}) copy-start(f32[512]{0:T(512)} %param.8) | copy-start | bytes 6148
  2.6 11.0 %copy-start.5 = (bf16[1,2,64,512]{3,2,1,0:T(8,128)(2,1)S(1)}, bf16[1,2,64,512]{3,2,1,0:T(8,128)(2,1)}, u32[]{:S(2)}) copy-start(bf16[1,2,64,512]{3,2,1,0:T(8,128)(2,1)} %param.5) | copy-start | bytes 393220
  2.6 40.2 %all-to-all-start = ((bf16[8,2,64,512]{3,2,1,0:T(8,128)(2,1)}), bf16[8,2,64,512]{3,2,1,0:T(8,128)(2,1)S(1)}, u32[]{:S(2)}, u32[]{:S(2)}) async-start(bf16[8,2,64,512]{3,2,1,0:T(8,128)(2,1)} %spread.1), calls=%async_computation | async-start | bytes 2097152 | tf_op jit(solution)/shard_map/all_to_all | solution.py:228
  13.6 24.8 %copy-start.6 = (s32[1,4096]{1,0:T(1,128)S(1)}, s32[1,4096]{1,0:T(1,128)}, u32[]{:S(2)}) copy-start(s32[1,4096]{1,0:T(1,128)} %param.6) | copy-start | bytes 49156
  14.3 28.5 %copy-start.3 = (bf16[1,128,512]{2,1,0:T(8,128)(2,1)}, bf16[1,128,512]{2,1,0:T(8,128)(2,1)S(1)}, u32[]{:S(2)}) copy-start(bf16[1,128,512]{2,1,0:T(8,128)(2,1)S(1)} %fusion.6.refs_1_) | copy-start | bytes 393220
  14.4 10.3 %collective-permute-start = (bf16[1,128,512]{2,1,0:T(8,128)(2,1)S(1)}, bf16[1,128,512]{2,1,0:T(8,128)(2,1)S(1)}, u32[]{:S(2)}, u32[]{:S(2)}) collective-permute-start(bf16[1,128,512]{2,1,0:T(8,128)(2,1)S(1)} %fusion.6.refs_1_), channel_id=1, source_target_pairs={{32,0},{0,32},{33,1},{1,33},{34,2},{2,34},{35,3},{3,35},{36,4},{4,... | collective-permute-start | bytes 393224 | tf_op jit(solution)/shard_map/ppermute | solution.py:23
  24.6 18.2 %copy-start.4 = (bf16[1,128,512]{2,1,0:T(8,128)(2,1)}, bf16[1,128,512]{2,1,0:T(8,128)(2,1)S(1)}, u32[]{:S(2)}) copy-start(bf16[1,128,512]{2,1,0:T(8,128)(2,1)S(1)} %collective-permute-done.refs_2_) | copy-start | bytes 393220
  24.7 18.2 %collective-permute-start.2 = (bf16[2,128,512]{2,1,0:T(8,128)(2,1)S(1)}, bf16[2,128,512]{2,1,0:T(8,128)(2,1)S(1)}, u32[]{:S(2)}, u32[]{:S(2)}) collective-permute-start(bf16[2,128,512]{2,1,0:T(8,128)(2,1)S(1)} %pad_maximum_fusion), channel_id=1, source_target_pairs={{24,0},{0,8},{8,16},{16,24},{25,1},{1,9},{9,17},{17,25},{26,2},{2,... | collective-permute-start | bytes 786440 | tf_op jit(solution)/shard_map/ppermute | solution.py:23
  27.8 15.1 %collective-permute-start.1 = (bf16[2,128,512]{2,1,0:T(8,128)(2,1)S(1)}, bf16[2,128,512]{2,1,0:T(8,128)(2,1)S(1)}, u32[]{:S(2)}, u32[]{:S(2)}) collective-permute-start(bf16[2,128,512]{2,1,0:T(8,128)(2,1)S(1)} %pad_maximum_fusion), channel_id=1, source_target_pairs={{8,0},{16,8},{24,16},{0,24},{9,1},{17,9},{25,17},{1,25},{10,2},{18... | collective-permute-start | bytes 786440 | tf_op jit(solution)/shard_map/ppermute | solution.py:23
  31.2 8.2 %collective-permute-start.3 = (bf16[1,128,512]{2,1,0:T(8,128)(2,1)S(1)}, bf16[1,128,512]{2,1,0:T(8,128)(2,1)S(1)}, u32[]{:S(2)}, u32[]{:S(2)}) collective-permute-start(bf16[1,128,512]{2,1,0:T(8,128)(2,1)S(1)} %fusion.6.refs_1_), channel_id=1, source_target_pairs={{16,0},{24,8},{0,16},{8,24},{17,1},{25,9},{1,17},{9,25},{18,2},{26... | collective-permute-start | bytes 393224 | tf_op jit(solution)/shard_map/ppermute | solution.py:23
  34.6 8.2 %collective-permute-start.4 = (bf16[1,128,512]{2,1,0:T(8,128)(2,1)S(1)}, bf16[1,128,512]{2,1,0:T(8,128)(2,1)S(1)}, u32[]{:S(2)}, u32[]{:S(2)}) collective-permute-start(bf16[1,128,512]{2,1,0:T(8,128)(2,1)S(1)} %collective-permute-done.refs_2_), channel_id=1, source_target_pairs={{16,0},{24,8},{0,16},{8,24},{17,1},{25,9},{1,17},{9,25},{18,2},{26... | collective-permute-start | bytes 393224 | tf_op jit(solution)/shard_map/ppermute | solution.py:23
  53.3 12.0 %collective-permute-start.5 = (bf16[4,2,64,512]{3,2,1,0:T(8,128)(2,1)}, bf16[4,2,64,512]{3,2,1,0:T(8,128)(2,1)S(1)}, u32[]{:S(2)}, u32[]{:S(2)}) collective-permute-start(bf16[4,2,64,512]{3,2,1,0:T(8,128)(2,1)} %get-tuple-element.11), channel_id=1, source_target_pairs={{0,1},{1,0},{2,3},{3,2},{4,5},{5,4},{6,7},{7,6},{8,9},{9,8},{10,11... | collective-permute-start | bytes 1572872 | tf_op jit(solution)/shard_map/ppermute | solution.py:37
  55.5 25.0 %all-to-all-start.1 = ((bf16[8,520,128]{2,1,0:T(8,128)(2,1)}), bf16[8,520,128]{2,1,0:T(8,128)(2,1)S(1)}, u32[]{:S(2)}, u32[]{:S(2)}) async-start(bf16[8,520,128]{2,1,0:T(8,128)(2,1)} %get-tuple-element.12), calls=%async_computation.1 | async-start | bytes 2129920 | tf_op jit(solution)/shard_map/all_to_all | solution.py:275
  65.5 21.2 %collective-permute-start.6 = (bf16[2,2,64,512]{3,2,1,0:T(8,128)(2,1)S(1)}, bf16[2,2,64,512]{3,2,1,0:T(8,128)(2,1)S(1)}, u32[]{:S(2)}, u32[]{:S(2)}) collective-permute-start(bf16[2,2,64,512]{3,2,1,0:T(8,128)(2,1)S(1)} %slice.28), channel_id=1, source_target_pairs={{0,7},{1,2},{2,1},{3,4},{4,3},{5,6},{6,5},{7,0},{8,15},{9,10},{10,... | collective-permute-start | bytes 786440 | tf_op jit(solution)/shard_map/ppermute | solution.py:37
  81.3 14.2 %all-to-all-start.2 = ((bf16[8,2,40,128]{3,2,1,0:T(8,128)(2,1)}), bf16[8,2,40,128]{3,2,1,0:T(8,128)(2,1)S(1)}, u32[]{:S(2)}, u32[]{:S(2)}) async-start(bf16[8,2,40,128]{3,2,1,0:T(8,128)(2,1)} %first_sum.1), calls=%async_computation.2 | async-start | bytes 327680 | tf_op jit(solution)/shard_map/all_to_all | solution.py:283
  86.9 19.5 %collective-permute-start.7 = (bf16[1,2,64,512]{3,2,1,0:T(8,128)(2,1)S(1)}, bf16[1,2,64,512]{3,2,1,0:T(8,128)(2,1)S(1)}, u32[]{:S(2)}, u32[]{:S(2)}) collective-permute-start(bf16[1,2,64,512]{3,2,1,0:T(8,128)(2,1)S(1)} %slice.29), channel_id=1, source_target_pairs={{0,3},{1,6},{2,5},{3,0},{4,7},{5,2},{6,1},{7,4},{8,11},{9,14},{10,... | collective-permute-start | bytes 393224 | tf_op jit(solution)/shard_map/ppermute | solution.py:37
  96.2 19.8 %all-to-all-start.3 = ((bf16[16,40,128]{2,1,0:T(8,128)(2,1)}), bf16[16,40,128]{2,1,0:T(8,128)(2,1)S(1)}, u32[]{:S(2)}, u32[]{:S(2)}) async-start(bf16[16,40,128]{2,1,0:T(8,128)(2,1)} %bitcast.12), calls=%async_computation.3 | async-start | bytes 327680 | tf_op jit(solution)/shard_map/all_to_all | solution.py:292
